TPU v7x, 32 devices: a whole 2x2x4 slice. The times are simulated.
32 devices in a mesh: parts: 2 (over y), blk: 16 (over z, x, core).
Axes of the slice: x: 2, y: 2, z: 4, core: 2. Of those that a mesh axis runs over, the one named last changes fastest.
Arguments:
- features: bfloat16 [8192, 128], P(('parts', 'blk')), parts along dimension 0, may hold values from -6 to 6
- w_first: bfloat16 [128, 256], replicated, may hold values from -0.5 to 0.5
- w_second: bfloat16 [256, 8192], replicated, may hold values from -0.375 to 0.375
- panel: bfloat16 [64, 64, 256], P(('parts', 'blk')), parts along dimension 0, may hold values from -6 to 6
- energies: float32 [256], replicated, may hold values from -1 to 1
- pair_dest: int32 [8192, 1], P(('parts', 'blk')), parts along dimension 0, may hold values from 0 to 15, as said below
- pair_row: int32 [8192], P(('parts', 'blk')), parts along dimension 0, may hold values from 0 to 1
- pair_col: int32 [8192], P(('parts', 'blk')), parts along dimension 0, may hold values from 0 to 1
Outputs:
- residual: float32 [64, 64, 256], P(('parts', 'blk')), parts along dimension 0
- loss: float32 [2], P('parts'), parts along dimension 0
- grad_first: float32 [256, 256], P('parts'), parts along dimension 0
- grad_second: float32 [512, 8192], P('parts', 'blk'), parts along dimension 0
There are 2 independent parts, one for each index of `parts`. A program takes and returns all parts, laid end to end along the dimension named above; an argument that names none is the same for every part. Nothing has to cross between parts.
Inputs may be any that keep to these rules, and one draw needn't show every extreme that they name: `pair_dest`: among one device's 256 pairs at most 24 have their block row on one device; every device owns the block rows of exactly 24 of its own pairs. Owners lie mostly near the listing device along the axis.
All inputs are finite; a program needn't handle non-finite values.
Results may differ from a plain program's by a relative error of at most 0.004.
Values may be sent and summed in bfloat16 or wider, within the bound.
No kernel may reach another device: no remote copies, remote signals or barrier semaphores. Data moves between devices by JAX's collectives and lax.ppermute only.
A program may use at most 128 MiB of HBM per device.

v0:
```python
import jax
import jax.numpy as jnp
from jax import lax
from jax.sharding import PartitionSpec as P


def predict(feats, w_first, w_second, orbitals):
    pre = jnp.dot(feats, w_first, preferred_element_type=jnp.float32)
    hidden = jax.nn.silu(pre).astype(jnp.bfloat16)
    blocks = (jnp.dot(hidden, w_second, preferred_element_type=jnp.float32) / orbitals).astype(
        jnp.bfloat16
    )
    return (pre, hidden, blocks)


def weight_terms(feats, pre, hidden, d_flat, w_second, orbitals):
    term_second = jnp.dot(hidden.T, d_flat, preferred_element_type=jnp.float32) / orbitals
    d_hidden = (
        lax.dot_general(
            d_flat, w_second, (((1,), (1,)), ((), ())), preferred_element_type=jnp.float32
        )
        / orbitals
    )
    sig = jax.nn.sigmoid(pre)
    d_pre = (d_hidden * sig * (1.0 + pre * (1.0 - sig))).astype(jnp.bfloat16)
    term_first = jnp.dot(feats.T, d_pre, preferred_element_type=jnp.float32)
    return (term_first, term_second)


def slot_work(slot_blocks, slot_panel, slot_rows, energies, blk_dev, total_blocks):
    slots, unused_two, orbitals, unused_o = slot_blocks.shape
    columns = slot_panel.shape[2]
    group = 32
    steps_count = slots // group
    grouped = (
        slot_blocks.reshape(steps_count, group, 2, orbitals, orbitals),
        slot_panel.reshape(steps_count, group, orbitals, columns),
        slot_rows.reshape(steps_count, group),
    )
    row_ids = jnp.arange(blk_dev, dtype=jnp.int32)

    def forward(total, item):
        blocks, coeffs, rows = item
        h_panel = jnp.einsum(
            "sab,sbp->sap", blocks[:, 0], coeffs, preferred_element_type=jnp.float32
        )
        s_panel = jnp.einsum(
            "sab,sbp->sap", blocks[:, 1], coeffs, preferred_element_type=jnp.float32
        )
        contrib = h_panel - s_panel * energies
        selector = (rows[None, :] == row_ids[:, None]).astype(jnp.float32)
        added = jnp.einsum("rs,sap->rap", selector, contrib, precision=lax.Precision.HIGHEST)
        return (total + added, None)

    residual = lax.scan(forward, jnp.zeros((blk_dev, orbitals, columns), jnp.float32), grouped)[0]
    grad_h = (residual / total_blocks).astype(jnp.bfloat16)
    grad_s = (-(residual * energies) / total_blocks).astype(jnp.bfloat16)

    def backward(carry, item):
        blocks, coeffs, rows = item
        valid = (rows >= 0)[:, None, None]
        safe_rows = jnp.maximum(rows, 0)
        gh_rows = jnp.where(valid, grad_h[safe_rows], jnp.zeros((), jnp.bfloat16))
        gs_rows = jnp.where(valid, grad_s[safe_rows], jnp.zeros((), jnp.bfloat16))
        d_h = jnp.einsum(
            "sap,sbp->sab", gh_rows, coeffs, preferred_element_type=jnp.float32
        ).astype(jnp.bfloat16)
        d_s = jnp.einsum(
            "sap,sbp->sab", gs_rows, coeffs, preferred_element_type=jnp.float32
        ).astype(jnp.bfloat16)
        return (carry, jnp.stack([d_h, d_s], axis=1))

    d_blocks = lax.scan(backward, 0, grouped)[1]
    return (residual, d_blocks.reshape(slots, 2, orbitals, orbitals))


def local(features, w_first, w_second, panel, energies, pair_dest, pair_row, pair_col):
    n_dev = lax.axis_size("blk")
    my_index = lax.axis_index("blk")
    pair_count, feat_width = features.shape
    blk_dev, orbitals, columns = panel.shape
    capacity = 3 * pair_count // (2 * n_dev)
    slots = n_dev * capacity
    total_blocks = blk_dev * n_dev
    dest = pair_dest[:, 0]
    dest_table = (dest[:, None] == jnp.arange(n_dev, dtype=jnp.int32)[None, :]).astype(jnp.int32)
    rank_in = jnp.sum(jnp.cumsum(dest_table, axis=0) * dest_table, axis=1) - 1
    slot_of = dest * capacity + rank_in
    source = (
        jnp.full((slots,), pair_count, jnp.int32)
        .at[slot_of]
        .set(jnp.arange(pair_count, dtype=jnp.int32))
    )
    empty_label = jnp.full((1,), -1, jnp.int32)
    rows_sent = jnp.concatenate([pair_row, empty_label])[source]
    cols_sent = jnp.concatenate([my_index * blk_dev + pair_col, jnp.zeros((1,), jnp.int32)])[source]
    labels = jnp.stack([rows_sent, cols_sent], axis=-1).reshape(n_dev, capacity, 2)
    whole_panel = lax.all_gather(panel, "blk", axis=0, tiled=True)
    pre, hidden, blocks = predict(features, w_first, w_second, orbitals)
    padded = jnp.concatenate([blocks, jnp.zeros((1, blocks.shape[1]), jnp.bfloat16)], axis=0)
    send_blocks = padded[source].reshape(n_dev, capacity, 2, orbitals, orbitals)
    got_blocks, got_labels = (
        lax.all_to_all(send_blocks, "blk", split_axis=0, concat_axis=0, tiled=True),
        lax.all_to_all(labels, "blk", split_axis=0, concat_axis=0, tiled=True),
    )
    got_labels = got_labels.reshape(slots, 2)
    slot_panel = whole_panel[got_labels[:, 1]]
    residual, d_blocks = slot_work(
        got_blocks.reshape(slots, 2, orbitals, orbitals),
        slot_panel,
        got_labels[:, 0],
        energies,
        blk_dev,
        total_blocks,
    )
    back = lax.all_to_all(
        d_blocks.reshape(n_dev, capacity, 2, orbitals, orbitals),
        "blk",
        split_axis=0,
        concat_axis=0,
        tiled=True,
    )
    d_flat = back.reshape(slots, 2 * orbitals * orbitals)[slot_of]
    term_first, term_second = weight_terms(features, pre, hidden, d_flat, w_second, orbitals)
    grad_second = lax.psum_scatter(term_second, "blk", scatter_dimension=1, tiled=True)
    grad_first, square_sum = lax.psum((term_first, jnp.sum(residual * residual)), "blk")
    loss = (square_sum / (total_blocks * orbitals * columns)).reshape(1)
    return (residual, loss, grad_first, grad_second)


def solution(mesh):
    in_specs = (
        P(("parts", "blk"), None),
        P(),
        P(),
        P(("parts", "blk"), None, None),
        P(),
        P(("parts", "blk"), None),
        P(("parts", "blk")),
        P(("parts", "blk")),
    )
    out_specs = (P(("parts", "blk"), None, None), P("parts"), P("parts", None), P("parts", "blk"))
    return jax.shard_map(local, mesh=mesh, in_specs=in_specs, out_specs=out_specs, check_vma=False)
```

profile of v0, /device:TPU:0, one launch (start us, length us, event | category | flops | bytes accessed | tf_op | source)
XLA Modules:
  0.0 824.7 jit_solution(7765582669645620948)
XLA Ops:
  12.3 2.8 gather_fusion.3
  15.9 2.8 gather_fusion.2
  19.4 7.4 all-to-all-start
  27.8 3.5 fusion.35
  31.3 2.5 concatenate.12
  33.7 17.6 %gather_fusion.4 = bf16[384,8192]{1,0:T(8,128)(2,1)} fusion(bf16[257,8192]{1,0:T(8,128)(2,1)} %concatenate.12, s32[1024]{0:T(1024)S(1)} %pad_clamp_fusion.3), kind=kCustom, calls=%fused_computation.4 | custom fusion | bytes 12584448 | tf_op jit(solution)/shard_map/gather | solution.py:101
  51.4 17.9 %reshape.77 = bf16[16,24,2,64,64]{4,3,2,1,0:T(8,128)(2,1)} reshape(bf16[384,8192]{1,0:T(8,128)(2,1)} %gather_fusion.4) | data formatting | bytes 12582912 | tf_op jit(solution)/shard_map/reshape | solution.py:101
  69.2 16.7 %reshape.156 = bf16[16,2,98304]{2,1,0:T(2,128)(2,1)} reshape(bf16[16,24,2,64,64]{4,3,2,1,0:T(8,128)(2,1)} %reshape.77) | data formatting | bytes 12582912
  85.9 6.0 all-to-all-start.1
  92.9 98.0 %all-gather.2.cloned.1.call-done = bf16[32,64,256]{2,1,0:T(8,128)(2,1)} async-done(((bf16[2,64,256]{2,1,0:T(8,128)(2,1)}), bf16[32,64,256]{2,1,0:T(8,128)(2,1)}) %all-gather.2.cloned.1.call-update) | async-done | bytes 1048592 | tf_op jit(solution)/shard_map/all_gather | solution.py:98
  191.0 12.4 %gather_fusion.5 = bf16[384,64,256]{2,1,0:T(8,128)(2,1)} fusion(bf16[32,64,256]{2,1,0:T(8,128)(2,1)} %all-gather.2.cloned.1.call-done, s32[1024]{0:T(1024)S(1)} %pad_clamp_fusion.2), kind=kCustom, calls=%fused_computation.5 | custom fusion | bytes 25167360 | tf_op jit(solution)/shard_map/gather | solution.py:107
  203.4 9.1 %all-to-all-done.1 = bf16[16,2,98304]{2,1,0:T(2,128)(2,1)} async-done(((bf16[16,2,98304]{2,1,0:T(2,128)(2,1)}), bf16[16,2,98304]{2,1,0:T(2,128)(2,1)}, u32[]{:S(2)}, u32[]{:S(2)}) %all-to-all-start.1) | async-done | bytes 6291488 | tf_op jit(solution)/shard_map/all_to_all | solution.py:103
  212.5 16.4 %reshape.157 = bf16[16,24,2,64,64]{4,3,2,1,0:T(8,128)(2,1)} reshape(bf16[16,2,98304]{2,1,0:T(2,128)(2,1)} %all-to-all-done.1) | data formatting | bytes 12582912
  229.0 82.3 %while.22 = (s32[]{:T(128)}, f32[2,64,256]{2,0,1:T(2,128)S(1)}, s32[12,32]{1,0:T(8,128)S(1)}, bf16[12,32,2,64,64]{4,3,2,1,0:T(8,128)(2,1)}, bf16[12,32,64,256]{3...) while((s32[]{:T(128)}, f32[2,64,256]{2,0,1:T(2,128)S(1)}, ...), condition=%wide.region_5.6_spmd.clone, body=%wide.region_4.5_spmd.clone.sunk | while | flops 147914816 | bytes 13372387 | solution.py:55
  233.6 2.2 fusion.85
  240.5 2.2 fusion.85
  267.9 2.2 fusion.85
  274.8 2.2 fusion.85
  281.7 2.2 fusion.85
  288.5 2.2 fusion.85
  312.1 72.8 %while.21 = (s32[]{:T(128)}, bf16[12,32,2,64,64]{4,3,2,1,0:T(8,128)(2,1)}, s32[12,32]{1,0:T(8,128)S(1)}, bf16[2,64,256]{2,1,0:T(8,128)(2,1)S(1)}, bf16[12,32,64,...) while((s32[]{:T(128)}, bf16[12,32,2,64,64]{4,3,2,1,0:T(8,128)(2,1)}, ...), condition=%wide.region_9.10_spmd, body=%wide.region_8.9_spmd.sunk | while | flops 135791680 | bytes 10492341 | solution.py:73
  384.8 16.6 %reshape.158 = bf16[16,2,98304]{2,1,0:T(2,128)(2,1)} reshape(bf16[16,24,2,64,64]{4,3,2,1,0:T(8,128)(2,1)} %bitcast.100) | data formatting | bytes 12582912
  401.5 28.0 %all-to-all-start.2 = ((bf16[16,2,98304]{2,1,0:T(2,128)(2,1)}), bf16[16,2,98304]{2,1,0:T(2,128)(2,1)}, u32[]{:S(2)}, u32[]{:S(2)}) async-start(bf16[16,2,98304]{2,1,0:T(2,128)(2,1)} %reshape.158), calls=%async_computation.2 | async-start | bytes 12582912 | tf_op jit(solution)/shard_map/all_to_all | solution.py:116
  429.9 113.9 %all-to-all-done.2 = bf16[16,2,98304]{2,1,0:T(2,128)(2,1)} async-done(((bf16[16,2,98304]{2,1,0:T(2,128)(2,1)}), bf16[16,2,98304]{2,1,0:T(2,128)(2,1)}, u32[]{:S(2)}, u32[]{:S(2)}) %all-to-all-start.2) | async-done | bytes 6291488 | tf_op jit(solution)/shard_map/all_to_all | solution.py:116
  543.7 16.3 %reshape.159 = bf16[16,24,2,64,64]{4,3,2,1,0:T(8,128)(2,1)} reshape(bf16[16,2,98304]{2,1,0:T(2,128)(2,1)} %all-to-all-done.2) | data formatting | bytes 12582912
  560.0 17.0 %reshape.80 = bf16[384,8192]{1,0:T(8,128)(2,1)} reshape(bf16[16,24,2,64,64]{4,3,2,1,0:T(8,128)(2,1)} %reshape.159) | data formatting | bytes 12582912 | tf_op jit(solution)/shard_map/reshape | solution.py:123
  577.0 12.6 %gather_fusion.6 = bf16[256,8192]{1,0:T(8,128)(2,1)} fusion(bf16[384,8192]{1,0:T(8,128)(2,1)} %reshape.80, s32[1024]{0:T(1024)S(1)} %pad_clamp_fusion.1), kind=kCustom, calls=%fused_computation.6 | custom fusion | bytes 8389632 | tf_op jit(solution)/shard_map/gather | solution.py:123
  589.6 5.7 convolution_bitcast_fusion
  595.3 6.7 convolution_multiply_fusion
  602.1 56.7 %psum.14 = f32[]{:T(128)} all-reduce(f32[]{:T(128)} %get-tuple-element.172), channel_id=1, replica_groups=mesh['parts'=2,'blk'=16] {'blk'}, use_global_device_ids=true, to_apply=%region_7.8 | all-reduce | flops 1 | bytes 8 | tf_op jit(solution)/shard_map/psum | solution.py:126
  660.1 45.8 %all-reduce.3.cloned.1.call-done = f32[128,256]{0,1:T(8,128)} async-done(((f32[128,256]{0,1:T(8,128)}), f32[128,256]{0,1:T(8,128)}) %all-reduce.3.cloned.1.call-update) | async-done | bytes 131088 | tf_op jit(solution)/shard_map/psum | solution.py:126
  707.6 109.5 %reduce-scatter.2.cloned.1.call-done = f32[256,512]{1,0:T(8,128)} async-done(((f32[256,8192]{1,0:T(8,128)}), f32[256,512]{1,0:T(8,128)}) %reduce-scatter.2.cloned.1.call-update) | async-done | bytes 524304 | tf_op jit(solution)/shard_map/reduce_scatter | solution.py:125
  (193 shorter events, 153.0 us)
Async XLA Ops:
  7.2 19.6 %copy-start = (bf16[256,128]{1,0:T(8,128)(2,1)S(1)}, bf16[256,128]{1,0:T(8,128)(2,1)}, u32[]{:S(2)}) copy-start(bf16[256,128]{1,0:T(8,128)(2,1)} %param.12) | copy-start | bytes 196612
  19.4 66.5 %all-to-all-start = ((s32[16,24,2]{1,2,0:T(2,128)}), s32[16,24,2]{1,2,0:T(2,128)S(1)}, u32[]{:S(2)}, u32[]{:S(2)}) async-start(s32[16,24,2]{1,2,0:T(2,128)} %pad_add_fusion), calls=%async_computation | async-start | bytes 32768 | tf_op jit(solution)/shard_map/all_to_all | solution.py:104
  85.9 126.6 %all-to-all-start.1 = ((bf16[16,2,98304]{2,1,0:T(2,128)(2,1)}), bf16[16,2,98304]{2,1,0:T(2,128)(2,1)}, u32[]{:S(2)}, u32[]{:S(2)}) async-start(bf16[16,2,98304]{2,1,0:T(2,128)(2,1)} %reshape.156), calls=%async_computation.1 | async-start | bytes 12582912 | tf_op jit(solution)/shard_map/all_to_all | solution.py:103
  92.0 99.0 %all-gather.2.cloned.1.call-start = ((), (), s32[]{:S(2)}) async-start(), calls=%async_computation.4 | async-start | bytes 1114112 | tf_op jit(solution)/shard_map/all_gather | solution.py:98
  203.4 25.6 %copy-start.1 = (f32[256]{0:T(256)S(1)}, f32[256]{0:T(256)}, u32[]{:S(2)}) copy-start(f32[256]{0:T(256)} %param.16) | copy-start | bytes 3076
  401.5 142.2 %all-to-all-start.2 = ((bf16[16,2,98304]{2,1,0:T(2,128)(2,1)}), bf16[16,2,98304]{2,1,0:T(2,128)(2,1)}, u32[]{:S(2)}, u32[]{:S(2)}) async-start(bf16[16,2,98304]{2,1,0:T(2,128)(2,1)} %reshape.158), calls=%async_computation.2 | async-start | bytes 12582912 | tf_op jit(solution)/shard_map/all_to_all | solution.py:116
  429.5 276.4 %all-reduce.3.cloned.1.call-start = ((), (), s32[]{:S(2)}) async-start(), calls=%async_computation.5 | async-start | bytes 262144 | tf_op jit(solution)/shard_map/psum | solution.py:126
  595.3 221.8 %reduce-scatter.2.cloned.1.call-start = ((), (), s32[]{:S(2)}) async-start(), calls=%async_computation.6 | async-start | bytes 8912896 | tf_op jit(solution)/shard_map/reduce_scatter | solution.py:125
Sparse Core Ops, SparseCore 0:
  95.0 95.9 all-gather.1
  595.4 110.4 all-reduce.2
  710.5 106.4 reduce-scatter.1
where the time goes:
time: 830 us; the launch traced here: 825 us
  waiting for transfers between devices  377 us (45%)
  local copies, waits for them, and re-layouts  186 us (22%)
  matrix products  124 us (15%)
  blocking collectives  56.7 us (7%)
  starting transfers between devices  42.1 us (5%)
  other arithmetic  21.9 us (3%)
  between operations  15.7 us (2%)
    all_to_all x1, waiting for transfers between devices, local(): lax.all_to_all(d_blocks.reshape(n_dev, capacity, 2, orbitals, orbitals),...  114 us
    reduce_scatter x1, waiting for transfers between devices, local(): lax.psum_scatter(term_second, 'blk', scatter_dimension=1, tiled=True)  109 us
    all_gather x1, waiting for transfers between devices, local(): whole_panel = lax.all_gather(panel, 'blk', axis=0, tiled=True)  98 us
    unnamed x10, local copies, waits for them, and re-layouts  68.4 us
    psum x1, blocking collectives, local(): lax.psum((term_first, jnp.sum(residual * residual)), 'blk')  56.7 us
    psum x1, waiting for transfers between devices, local(): lax.psum((term_first, jnp.sum(residual * residual)), 'blk')  45.8 us
    all_to_all x1, starting transfers between devices, local(): lax.all_to_all(d_blocks.reshape(n_dev, capacity, 2, orbitals, orbitals),...  28 us
    dot_general x12, matrix products, forward(): jnp.einsum('rs,sap->rap', selector, contrib, precision=lax.Precision.HIGH...  26.3 us
  transfers between devices with their start and end apart: 6, of which 5 were waited for; matrix products, arithmetic and copies ran while one was open for 10% of the time, Pallas kernels for 0%

commit v1 on v0

--- a/solution.py
+++ b/solution.py
@@ -1,7 +1,294 @@
+import functools
+
 import jax
 import jax.numpy as jnp
 from jax import lax
+from jax.experimental import pallas as pl
+from jax.experimental.pallas import tpu as pltpu
 from jax.sharding import PartitionSpec as P
+
+BF16 = jnp.bfloat16
+F32 = jnp.float32
+VMEM_LIMIT = 56 << 20
+
+
+def dot(a, b, dims):
+    return lax.dot_general(a, b, ((dims[:1], dims[1:]), ((), ())), preferred_element_type=F32)
+
+
+def group_kernel(gid_ref, feats_ref, w_first_ref, out_ref, *, orbitals):
+    pre = dot(feats_ref[...], w_first_ref[...], (1, 0))
+    hidden = (pre / (1.0 + jnp.exp(-pre))).astype(BF16)
+    groups, pairs = out_ref.shape[0], feats_ref.shape[0]
+    rows = lax.broadcasted_iota(jnp.int32, (groups, pairs), 0)
+    pick = (rows == gid_ref[...]).astype(F32).astype(BF16)
+    out_ref[...] = (dot(pick, hidden, (1, 0)) * (1.0 / orbitals)).astype(BF16)
+
+
+def swap_kernel(w_ref, out_ref):
+    for k in range(w_ref.shape[1] // 128):
+        cols = slice(k * 128, (k + 1) * 128)
+        out_ref[:, cols] = pltpu.roll(w_ref[:, cols].astype(F32), 64, 1).astype(BF16)
+
+
+def main_kernel(*refs, chips, z_count, rows_split, half_cols):
+    (me_ref, *piece_refs) = refs[: 1 + chips]
+    (
+        partner_ref,
+        feats_ref,
+        gid_ref,
+        w_first_ref,
+        w_ref,
+        w_swap_ref,
+        energies_ref,
+        res_ref,
+        keep_ref,
+        send_ref,
+        first_ref,
+        h_ref,
+        c_ref,
+        x_ref,
+        r_ref,
+        g_ref,
+        l_ref,
+        dh_ref,
+    ) = refs[1 + chips :]
+    me = me_ref[0]
+    core = me % 2
+    chip = me // 2
+    x_count = chips // z_count
+    my_z, my_x = chip // x_count, chip % x_count
+    listers = 2 * chips
+    rs = rows_split
+    hid = w_ref.shape[0]
+    half = w_ref.shape[1] // 2
+    columns = energies_ref.shape[1]
+    ah_count = half // 128
+    total_blocks = 2 * rs
+    lane = lax.broadcasted_iota(jnp.int32, (rs, 128), 1)
+    low = lane < 64
+
+    def place(lister, block):
+        at = pl.multiple_of(lister * 128, 128)
+        c_ref[0, pl.ds(at, 128), :] = block
+        c_ref[1, pl.ds(at, 64), :] = block[64:, :]
+        c_ref[1, pl.ds(at + 64, 64), :] = block[:64, :]
+
+    for m in range(chips):
+        dz, dx = m // x_count, m % x_count
+        src = ((my_z - dz) % z_count) * x_count + (my_x - dx) % x_count
+        same, other = 2 * src + core, 2 * src + 1 - core
+        piece = piece_refs[m]
+        place(same, piece[4 * rs : 4 * rs + 128, :])
+        place(other, partner_ref[m * 128 : (m + 1) * 128, :])
+        for which, lister in ((0, same), (1, other)):
+            at = pl.multiple_of(lister * rs, rs)
+            for pc in range(2):
+                lo = which * 2 * rs + pc * rs
+                h_ref[pc, pl.ds(at, rs), :] = piece[lo : lo + rs, :]
+
+    h0, h1 = h_ref[0], h_ref[1]
+    step_cols = 512
+    steps = half // step_cols
+    per = step_cols // 128
+
+    def forward(i, carry):
+        hs, nb = i // steps, i % steps
+        at = pl.multiple_of(i * step_cols, step_cols)
+        y0 = dot(h0, w_ref[:, pl.ds(at, step_cols)], (1, 0))
+        y1 = dot(h1, w_swap_ref[:, pl.ds(at, step_cols)], (1, 0))
+        for k in range(per):
+            row = pl.multiple_of((hs * ah_count + nb * per + k) * rs, rs)
+            for j in range(listers):
+                v0 = y0[j * rs : (j + 1) * rs, k * 128 : (k + 1) * 128]
+                v1 = y1[j * rs : (j + 1) * rs, k * 128 : (k + 1) * 128]
+                cols = slice(j * 128, (j + 1) * 128)
+                x_ref[0, pl.ds(row, rs), cols] = jnp.where(low, v0, v1).astype(BF16)
+                x_ref[1, pl.ds(row, rs), cols] = jnp.where(low, v1, v0).astype(BF16)
+        return carry
+
+    lax.fori_loop(0, 2 * steps, forward, 0)
+
+    energies = energies_ref[...]
+    n_rows = ah_count * rs
+    mb = 256
+    f_width = w_first_ref.shape[0]
+    first_ref[...] = jnp.zeros_like(first_ref)
+
+    def product(i, carry):
+        par, b = i // (n_rows // mb), i % (n_rows // mb)
+        at = pl.multiple_of(b * mb, mb)
+        r_h = dot(x_ref[par, pl.ds(at, mb), :], c_ref[par], (1, 0))
+        r_s = dot(x_ref[par, pl.ds(n_rows + at, mb), :], c_ref[par], (1, 0))
+        res = r_h - r_s * energies
+        r_ref[par, pl.ds(at, mb), :] = res
+        g_ref[0, par, pl.ds(at, mb), :] = (res / total_blocks).astype(BF16)
+        g_ref[1, par, pl.ds(at, mb), :] = (-(res * energies) / total_blocks).astype(BF16)
+        first_ref[f_width:, :] += jnp.sum((res * res).reshape(mb // 8, 8, columns), axis=0)
+        return carry
+
+    lax.fori_loop(0, 2 * (n_rows // mb), product, 0)
+
+    blk_dev = res_ref.shape[0]
+    for i in range(blk_dev):
+        for par in range(2):
+            for ah in range(ah_count):
+                res_ref[i, 2 * ah + par : 2 * ah + par + 1, :] = r_ref[
+                    par, pl.ds(ah * rs + chip * blk_dev + i, 1), :
+                ]
+
+    jb_count = 2
+    jb_width = jb_count * 128
+
+    def backward(i, carry):
+        hs, jb = i // (listers // jb_count), i % (listers // jb_count)
+        at = pl.multiple_of(jb * jb_width, jb_width)
+        d_e = dot(g_ref[hs, 0], c_ref[0, pl.ds(at, jb_width), :], (1, 1))
+        d_o = dot(g_ref[hs, 1], c_ref[1, pl.ds(at, jb_width), :], (1, 1))
+        for j in range(jb_count):
+            row = pl.multiple_of((jb * jb_count + j) * rs, rs)
+            for ah in range(ah_count):
+                v0 = d_e[ah * rs : (ah + 1) * rs, j * 128 : (j + 1) * 128]
+                v1 = d_o[ah * rs : (ah + 1) * rs, j * 128 : (j + 1) * 128]
+                cols = pl.ds(pl.multiple_of(hs * half + ah * 128, 128), 128)
+                l_ref[0, pl.ds(row, rs), cols] = jnp.where(low, v0, v1).astype(BF16)
+                l_ref[1, pl.ds(row, rs), cols] = jnp.where(low, v1, v0).astype(BF16)
+        return carry
+
+    lax.fori_loop(0, 2 * (listers // jb_count), backward, 0)
+
+    orbitals = 64
+    for pc, weights in ((0, w_ref), (1, w_swap_ref)):
+        dh_ref[pc] = dot(l_ref[pc], weights[...], (1, 1)) / orbitals
+
+    width = 2 * half_cols
+    at = pl.multiple_of(chip * width, width)
+    g0 = dot(h0, l_ref[0, :, pl.ds(at, width)], (0, 0))
+    g1 = dot(h1, l_ref[1, :, pl.ds(at, width)], (0, 0))
+    even = core == 0
+    for k in range(half_cols // 128):
+        a, b = slice(k * 128, (k + 1) * 128), slice(half_cols + k * 128, half_cols + (k + 1) * 128)
+        va = g0[:, a] + pltpu.roll(g1[:, a], 64, 1)
+        vb = g0[:, b] + pltpu.roll(g1[:, b], 64, 1)
+        keep_ref[:, a] = jnp.where(even, va, vb)
+        send_ref[:, a] = jnp.where(even, vb, va)
+
+    pairs = gid_ref.shape[1]
+    group_row = lax.broadcasted_iota(jnp.int32, (2 * rs, pairs), 0) + core * (2 * rs)
+
+    def first(j, carry):
+        feats = feats_ref[pl.ds(pl.multiple_of(j * pairs, pairs), pairs), :]
+        pre = dot(feats, w_first_ref[...], (1, 0))
+        sig = 1.0 / (1.0 + jnp.exp(-pre))
+        at = pl.multiple_of(j * rs, rs)
+        d_group = jnp.concatenate([dh_ref[0, pl.ds(at, rs), :], dh_ref[1, pl.ds(at, rs), :]], axis=0)
+        head = d_group.astype(BF16)
+        tail = (d_group - head.astype(F32)).astype(BF16)
+        pick = (group_row == gid_ref[pl.ds(j, 1), :]).astype(F32).astype(BF16)
+        both = jnp.concatenate([head, tail], axis=0)
+        d_hidden = dot(jnp.concatenate([pick, pick], axis=0), both, (0, 0))
+        d_pre = (d_hidden * sig * (1.0 + pre * (1.0 - sig))).astype(BF16)
+        first_ref[:f_width, :] += dot(feats, d_pre, (0, 0))
+        return carry
+
+    lax.fori_loop(0, listers, first, 0)
+
+
+def near(features, w_first, w_second, panel, energies, pair_dest, pair_row, pair_col, z_count):
+    n_dev = lax.axis_size("blk")
+    me = lax.axis_index("blk")
+    pairs, f_width = features.shape
+    blk_dev, orbitals, columns = panel.shape
+    hid, flat = w_second.shape
+    chips, rs = n_dev // 2, n_dev * blk_dev // 2
+    x_count = chips // z_count
+    half_cols = flat // n_dev
+    dest = pair_dest[:, 0]
+    gid = (dest % 2) * (2 * rs) + pair_col * rs + (dest // 2) * blk_dev + pair_row
+
+    grouped = pl.pallas_call(
+        functools.partial(group_kernel, orbitals=orbitals),
+        out_shape=jax.ShapeDtypeStruct((4 * rs, hid), BF16),
+        name="group",
+    )(gid.reshape(1, pairs), features, w_first)
+    w_swap = pl.pallas_call(
+        swap_kernel,
+        out_shape=jax.ShapeDtypeStruct(w_second.shape, BF16),
+        compiler_params=pltpu.CompilerParams(vmem_limit_bytes=VMEM_LIMIT),
+        name="swap",
+    )(w_second)
+
+    def to_core(v):
+        return lax.ppermute(v, "blk", [(i, i ^ 1) for i in range(n_dev)])
+
+    def shift(m):
+        dz, dx = m // x_count, m % x_count
+        moves = []
+        for i in range(n_dev):
+            chip, core = i // 2, i % 2
+            z, x = chip // x_count, chip % x_count
+            to = ((z + dz) % z_count) * x_count + (x + dx) % x_count
+            moves.append((i, 2 * to + core))
+        return moves
+
+    core = me % 2
+    mine = lax.dynamic_slice_in_dim(grouped, core * 2 * rs, 2 * rs, 0)
+    theirs = lax.dynamic_slice_in_dim(grouped, (1 - core) * 2 * rs, 2 * rs, 0)
+    from_core = to_core(theirs)
+    piece = jnp.concatenate([mine, from_core, panel.reshape(blk_dev * orbitals, columns)], axis=0)
+    pieces = [piece] + [lax.ppermute(piece, "blk", shift(m)) for m in range(1, chips)]
+    partner = to_core(jnp.concatenate([v[4 * rs :] for v in pieces], axis=0))
+
+    pack = jnp.concatenate([features, gid.astype(BF16).reshape(pairs // f_width, f_width)], axis=0)
+    packs = jnp.stack([pack] + [lax.ppermute(pack, "blk", shift(m)) for m in range(1, chips)])
+    packs = jnp.stack([packs, to_core(packs)], axis=1)
+    zz, xx = jnp.meshgrid(jnp.arange(z_count), jnp.arange(x_count), indexing="ij")
+    chip = me // 2
+    source = ((chip // x_count - zz) % z_count * x_count + (chip % x_count - xx) % x_count).reshape(-1)
+    order = jnp.stack([source, source], axis=1) * 2 + jnp.stack([core, 1 - core])[None, :]
+    back = jnp.zeros((n_dev,), jnp.int32).at[order.reshape(-1)].set(jnp.arange(n_dev))
+    packs = packs.reshape(n_dev, -1, f_width)[back]
+    all_feats = packs[:, :pairs].reshape(n_dev * pairs, f_width)
+    all_gid = packs[:, pairs:].reshape(n_dev, pairs).astype(jnp.int32)
+
+    listers = n_dev
+    k_width = listers * 128
+    n_rows = rs * orbitals // 2
+    res, keep, send, first = pl.pallas_call(
+        functools.partial(main_kernel, chips=chips, z_count=z_count, rows_split=rs, half_cols=half_cols),
+        out_shape=(
+            jax.ShapeDtypeStruct((blk_dev, orbitals, columns), F32),
+            jax.ShapeDtypeStruct((hid, half_cols), F32),
+            jax.ShapeDtypeStruct((hid, half_cols), F32),
+            jax.ShapeDtypeStruct((f_width + 8, hid), F32),
+        ),
+        in_specs=[pl.BlockSpec(memory_space=pltpu.SMEM)] + [pl.BlockSpec(memory_space=pltpu.VMEM)] * (chips + 7),
+        scratch_shapes=[
+            pltpu.VMEM((2, listers * rs, hid), BF16),
+            pltpu.VMEM((2, k_width, columns), BF16),
+            pltpu.VMEM((2, 2 * n_rows, k_width), BF16),
+            pltpu.VMEM((2, n_rows, columns), F32),
+            pltpu.VMEM((2, 2, n_rows, columns), BF16),
+            pltpu.VMEM((2, listers * rs, flat), BF16),
+            pltpu.VMEM((2, listers * rs, hid), F32),
+        ],
+        compiler_params=pltpu.CompilerParams(vmem_limit_bytes=VMEM_LIMIT),
+        name="step",
+    )(
+        me.reshape(1).astype(jnp.int32),
+        *pieces,
+        partner,
+        all_feats,
+        all_gid,
+        w_first,
+        w_second,
+        w_swap,
+        energies.reshape(1, columns),
+    )
+    grad_second = keep + to_core(send)
+    first = first + to_core(first)
+    loss = (jnp.sum(first[f_width:]) / (n_dev * blk_dev * orbitals * columns)).reshape(1)
+    return (res, loss, first[:f_width], grad_second)
 
 
 def predict(feats, w_first, w_second, orbitals):
@@ -140,4 +427,6 @@
         P(("parts", "blk")),
     )
     out_specs = (P(("parts", "blk"), None, None), P("parts"), P("parts", None), P("parts", "blk"))
-    return jax.shard_map(local, mesh=mesh, in_specs=in_specs, out_specs=out_specs, check_vma=False)
+    n_dev = mesh.shape["blk"]
+    step = functools.partial(near, z_count=4) if n_dev == 16 else local
+    return jax.shard_map(step, mesh=mesh, in_specs=in_specs, out_specs=out_specs, check_vma=False)

time: 830 us -> 105 us (0.13)
  waiting for transfers between devices: 377 us -> 24.7 us
  local copies, waits for them, and re-layouts: 186 us -> 12.1 us
  matrix products: 124 us -> 0 us
  blocking collectives: 56.7 us -> 0 us
  Pallas kernels: 0 us -> 36.3 us
  starting transfers between devices: 42.1 us -> 21.5 us
  other arithmetic: 21.9 us -> 7.56 us
  between operations: 15.7 us -> 2.68 us
    dot_general x64 -> x0, matrix products: 124 us -> none  [the longest x12 26.3 us: forward(): jnp.einsum('rs,sap->rap', selector, contrib, precision=lax.Precision.HIGH...]
    all_to_all x3 -> x0, waiting for transfers between devices: 123 us -> none  [the longest x1 114 us: local(): lax.all_to_all(d_blocks.reshape(n_dev, capacity, 2, orbitals, orbitals),...]
    reduce_scatter x1 -> x0, waiting for transfers between devices: 109 us -> none  [local(): lax.psum_scatter(term_second, 'blk', scatter_dimension=1, tiled=True)]
    all_gather x1 -> x0, waiting for transfers between devices: 98 us -> none  [local(): whole_panel = lax.all_gather(panel, 'blk', axis=0, tiled=True)]
    gather x29 -> x1, local copies, waits for them, and re-layouts: 62.9 us -> 0.76 us  [near(): packs = packs.reshape(n_dev, -1, f_width)[back]]
    unnamed x10 -> x32, local copies, waits for them, and re-layouts: 68.4 us -> 6.88 us
    psum x1 -> x0, blocking collectives: 56.7 us -> none  [local(): lax.psum((term_first, jnp.sum(residual * residual)), 'blk')]
    psum x1 -> x0, waiting for transfers between devices: 45.8 us -> none  [local(): lax.psum((term_first, jnp.sum(residual * residual)), 'blk')]
  transfers between devices with their start and end apart: 6 -> 19, of which waited for: 5 -> 6; matrix products, arithmetic and copies ran while one was open for 10% -> 14% of each run, Pallas kernels for 0% -> 7%
where the time goes in v1:
time: 105 us
  Pallas kernels  36.3 us (35%)
  waiting for transfers between devices  24.7 us (24%)
  starting transfers between devices  21.5 us (20%)
  local copies, waits for them, and re-layouts  12.1 us (12%)
  other arithmetic  7.56 us (7%)
  between operations  2.68 us (3%)
    pallas_call x1, Pallas kernels, near(): pl.pallas_call(functools.partial(main_kernel, chips=chips, z_count=z_coun...  29.2 us
    ppermute x7, waiting for transfers between devices, near(): lax.ppermute(piece, 'blk', shift(m))  14.2 us
    ppermute x7, starting transfers between devices, near(): lax.ppermute(pack, 'blk', shift(m))  13 us
    ppermute x7, waiting for transfers between devices, near(): lax.ppermute(pack, 'blk', shift(m))  8.68 us
    ppermute x7, starting transfers between devices, near(): lax.ppermute(piece, 'blk', shift(m))  7.47 us
    unnamed x32, local copies, waits for them, and re-layouts  6.88 us
    pallas_call x1, Pallas kernels, near(): pl.pallas_call(swap_kernel, out_shape=jax.ShapeDtypeStruct(w_second.shape...  5.27 us
  transfers between devices with their start and end apart: 19, of which 6 were waited for; matrix products, arithmetic and copies ran while one was open for 14% of the time, Pallas kernels for 7%

profile of v1, /device:TPU:0, one launch (start us, length us, event | category | flops | bytes accessed | tf_op | source)
XLA Modules:
  0.0 104.8 jit_solution(11196124601537097996)
XLA Ops:
  0.6 1.3 %convert_bitcast_fusion = (bf16[2,128]{1,0:T(2,128)(2,1)S(1)}, s32[256]{0:T(256)}) fusion(s32[256]{0:T(256)} %param.14, s32[256]{0:T(256)} %bitcast.49, s32[256]{0:T(256)} %param.15), kind=kLoop, calls=%fused_computation.53 | loop fusion | flops 6656 | bytes 4608 | tf_op jit(solution)/shard_map/reshape | solution.py:242
  1.9 0.8 pad_maximum_fusion.2
  2.8 5.0 %collective-permute-start.14 = (bf16[258,128]{1,0:T(8,128)(2,1)S(1)}, bf16[258,128]{1,0:T(8,128)(2,1)S(1)}, u32[]{:S(2)}, u32[]{:S(2)}) collective-permute-start(bf16[258,128]{1,0:T(8,128)(2,1)S(1)} %pad_maximum_fusion.2), channel_id=1, source_target_pairs={{0,12},{1,13},{2,14},{3,15},{4,0},{5,1},{6,2},{7,3},{8,4},{9,5},{1... | collective-permute-start | bytes 198152 | tf_op jit(solution)/shard_map/ppermute | solution.py:243
  8.2 3.5 %collective-permute-start.12 = (bf16[258,128]{1,0:T(8,128)(2,1)S(1)}, bf16[258,128]{1,0:T(8,128)(2,1)S(1)}, u32[]{:S(2)}, u32[]{:S(2)}) collective-permute-start(bf16[258,128]{1,0:T(8,128)(2,1)S(1)} %pad_maximum_fusion.2), channel_id=1, source_target_pairs={{0,8},{1,9},{2,10},{3,11},{4,12},{5,13},{6,14},{7,15},{8,0},{9,1},... | collective-permute-start | bytes 198152 | tf_op jit(solution)/shard_map/ppermute | solution.py:243
  11.7 1.9 %group.1 = bf16[64,256]{1,0:T(8,128)(2,1)} custom-call(s32[1,256]{1,0:T(1,128)} %bitcast.47, bf16[256,128]{1,0:T(8,128)(2,1)} %feats_ref.1, bf16[128,256]{1,0:T(8,128)(2,1)} %refs_12_.1), custom_call_target="tpu_custom_call" | custom-call | tf_op jit(solution)/shard_map/group/pallas_call | solution.py:209
  13.5 0.7 constant_dynamic-slice_fusion.1
  14.3 0.8 bitcast_dynamic-update-slice_fusion.7
  15.7 1.5 %constant_dynamic-update-slice_fusion = bf16[1024,256]{1,0:T(8,128)(2,1)} fusion(bf16[128,256]{1,0:T(8,128)(2,1)} %bitcast.43), kind=kLoop, calls=%fused_computation.21 | loop fusion | bytes 131072
  18.4 0.8 pad_maximum_fusion.1.refs_1_
  19.3 3.2 %collective-permute-done.9 = bf16[258,128]{1,0:T(8,128)(2,1)S(1)} collective-permute-done((bf16[258,128]{1,0:T(8,128)(2,1)S(1)}, bf16[258,128]{1,0:T(8,128)(2,1)S(1)}, u32[]{:S(2)}, u32[]{:S(2)}) %collective-permute-start.9) | collective-permute-done | bytes 66080 | tf_op jit(solution)/shard_map/ppermute | solution.py:243
  23.0 5.5 %collective-permute-done.10 = bf16[258,128]{1,0:T(8,128)(2,1)S(1)} collective-permute-done((bf16[258,128]{1,0:T(8,128)(2,1)S(1)}, bf16[258,128]{1,0:T(8,128)(2,1)S(1)}, u32[]{:S(2)}, u32[]{:S(2)}) %collective-permute-start.10) | collective-permute-done | bytes 66080 | tf_op jit(solution)/shard_map/ppermute | solution.py:243
  28.5 2.9 %collective-permute-start.15 = (bf16[258,128]{1,0:T(8,128)(2,1)S(1)}, bf16[258,128]{1,0:T(8,128)(2,1)S(1)}, u32[]{:S(2)}, u32[]{:S(2)}) collective-permute-start(bf16[258,128]{1,0:T(8,128)(2,1)S(1)} %pad_maximum_fusion.2), channel_id=1, source_target_pairs={{0,14},{1,15},{2,12},{3,13},{4,2},{5,3},{6,0},{7,1},{8,6},{9,7},{1... | collective-permute-start | bytes 198152 | tf_op jit(solution)/shard_map/ppermute | solution.py:243
  31.7 4.4 %collective-permute-start.5 = (bf16[192,256]{1,0:T(8,128)(2,1)S(1)}, bf16[192,256]{1,0:T(8,128)(2,1)S(1)}, u32[]{:S(2)}, u32[]{:S(2)}) collective-permute-start(bf16[192,256]{1,0:T(8,128)(2,1)S(1)} %pad_maximum_fusion.1.refs_1_), channel_id=1, source_target_pairs={{0,10},{1,11},{2,8},{3,9},{4,14},{5,15},{6,12},{7,13},{8,2},{9,3},... | collective-permute-start | bytes 294920 | tf_op jit(solution)/shard_map/ppermute | solution.py:239
  36.9 4.0 %collective-permute-done.1.refs_2_ = bf16[192,256]{1,0:T(8,128)(2,1)S(1)} collective-permute-done((bf16[192,256]{1,0:T(8,128)(2,1)S(1)}, bf16[192,256]{1,0:T(8,128)(2,1)S(1)}, u32[]{:S(2)}, u32[]{:S(2)}) %collective-permute-start.1) | collective-permute-done | bytes 98336 | tf_op jit(solution)/shard_map/ppermute | solution.py:239
  40.9 1.8 %collective-permute-start.2 = (bf16[192,256]{1,0:T(8,128)(2,1)S(1)}, bf16[192,256]{1,0:T(8,128)(2,1)S(1)}, u32[]{:S(2)}, u32[]{:S(2)}) collective-permute-start(bf16[192,256]{1,0:T(8,128)(2,1)S(1)} %pad_maximum_fusion.1.refs_1_), channel_id=1, source_target_pairs={{0,4},{1,5},{2,6},{3,7},{4,8},{5,9},{6,10},{7,11},{8,12},{9,13},{1... | collective-permute-start | bytes 294920 | tf_op jit(solution)/shard_map/ppermute | solution.py:239
  42.7 0.6 slice_dynamic-update-slice_fusion.6
  43.3 4.0 %collective-permute-done.2.refs_3_ = bf16[192,256]{1,0:T(8,128)(2,1)S(1)} collective-permute-done((bf16[192,256]{1,0:T(8,128)(2,1)S(1)}, bf16[192,256]{1,0:T(8,128)(2,1)S(1)}, u32[]{:S(2)}, u32[]{:S(2)}) %collective-permute-start.2) | collective-permute-done | bytes 98336 | tf_op jit(solution)/shard_map/ppermute | solution.py:239
  48.5 6.2 %collective-permute-done.3.refs_4_ = bf16[192,256]{1,0:T(8,128)(2,1)S(1)} collective-permute-done((bf16[192,256]{1,0:T(8,128)(2,1)S(1)}, bf16[192,256]{1,0:T(8,128)(2,1)S(1)}, u32[]{:S(2)}, u32[]{:S(2)}) %collective-permute-start.3) | collective-permute-done | bytes 98336 | tf_op jit(solution)/shard_map/ppermute | solution.py:239
  54.7 0.7 slice_dynamic-update-slice_fusion.4
  55.3 0.7 slice_dynamic-update-slice_fusion.3
  56.0 0.7 slice_dynamic-update-slice_fusion.2
  56.7 0.7 slice_dynamic-update-slice_fusion.1
  57.3 0.7 slice_dynamic-update-slice_fusion
  58.5 5.3 %swap.1.refs_14_ = bf16[256,8192]{1,0:T(8,128)(2,1)} custom-call(bf16[256,8192]{1,0:T(8,128)(2,1)} %refs_13_.1), custom_call_target="tpu_custom_call" | custom-call | tf_op jit(solution)/shard_map/swap/pallas_call | solution.py:214
  64.1 0.8 gather_fusion
  64.9 1.1 %slice.53 = bf16[16,256,128]{2,1,0:T(8,128)(2,1)} slice(bf16[16,258,128]{2,1,0:T(8,128)(2,1)S(1)} %gather_fusion), slice={[0:16], [0:256], [0:128]} | slice | bytes 2097152 | tf_op jit(solution)/shard_map/slice | solution.py:251
  66.6 0.8 copy-done
  67.4 29.2 %step.1 = (f32[2,64,256]{2,1,0:T(8,128)}, f32[256,512]{1,0:T(8,128)}, f32[256,512]{1,0:T(8,128)}, f32[136,256]{1,0:T(8,128)}) custom-call(s32[1]{0:T(128)} %bitcast.refs_0_, bf16[192,256]{1,0:T(8,128)(2,1)} %copy-done.1, bf16[192,256]{1,0:T(8,128)(2,1)} %copy-done.6, bf16[192,256]{1,0:T(8,128)(2,1)} %copy-done.7, bf16[192,256]{1,0:T(8,128)(2,1)} %copy-done.8, ...), custom_call_target="tpu_custom_call" | custom-call | tf_op jit(solution)/shard_map/step/pallas_call | solution.py:257
  97.1 1.8 %collective-permute-done.17 = f32[136,256]{1,0:T(8,128)S(1)} collective-permute-done((f32[136,256]{1,0:T(8,128)}, f32[136,256]{1,0:T(8,128)S(1)}, u32[]{:S(2)}, u32[]{:S(2)}) %collective-permute-start.17) | collective-permute-done | bytes 139296 | tf_op jit(solution)/shard_map/ppermute | solution.py:222
  98.9 0.9 add.119
  99.8 0.7 slice.56
  101.7 1.9 %add.120 = f32[256,512]{1,0:T(8,128)} add(f32[256,512]{1,0:T(8,128)} %get-tuple-element.10, f32[256,512]{1,0:T(8,128)S(1)} %collective-permute-done.18) | non-fusion elementwise | flops 131072 | bytes 1572864 | tf_op jit(solution)/shard_map/add | solution.py:288
  (75 shorter events, 7.3 us)
Async XLA Ops:
  2.8 33.3 %collective-permute-start.14 = (bf16[258,128]{1,0:T(8,128)(2,1)S(1)}, bf16[258,128]{1,0:T(8,128)(2,1)S(1)}, u32[]{:S(2)}, u32[]{:S(2)}) collective-permute-start(bf16[258,128]{1,0:T(8,128)(2,1)S(1)} %pad_maximum_fusion.2), channel_id=1, source_target_pairs={{0,12},{1,13},{2,14},{3,15},{4,0},{5,1},{6,2},{7,3},{8,4},{9,5},{1... | collective-permute-start | bytes 198152 | tf_op jit(solution)/shard_map/ppermute | solution.py:243
  7.8 23.8 %collective-permute-start.13 = (bf16[258,128]{1,0:T(8,128)(2,1)S(1)}, bf16[258,128]{1,0:T(8,128)(2,1)S(1)}, u32[]{:S(2)}, u32[]{:S(2)}) collective-permute-start(bf16[258,128]{1,0:T(8,128)(2,1)S(1)} %pad_maximum_fusion.2), channel_id=1, source_target_pairs={{0,10},{1,11},{2,8},{3,9},{4,14},{5,15},{6,12},{7,13},{8,2},{9,3},... | collective-permute-start | bytes 198152 | tf_op jit(solution)/shard_map/ppermute | solution.py:243
  8.2 23.4 %collective-permute-start.12 = (bf16[258,128]{1,0:T(8,128)(2,1)S(1)}, bf16[258,128]{1,0:T(8,128)(2,1)S(1)}, u32[]{:S(2)}, u32[]{:S(2)}) collective-permute-start(bf16[258,128]{1,0:T(8,128)(2,1)S(1)} %pad_maximum_fusion.2), channel_id=1, source_target_pairs={{0,8},{1,9},{2,10},{3,11},{4,12},{5,13},{6,14},{7,15},{8,0},{9,1},... | collective-permute-start | bytes 198152 | tf_op jit(solution)/shard_map/ppermute | solution.py:243
  11.7 19.8 %collective-permute-start.11 = (bf16[258,128]{1,0:T(8,128)(2,1)S(1)}, bf16[258,128]{1,0:T(8,128)(2,1)S(1)}, u32[]{:S(2)}, u32[]{:S(2)}) collective-permute-start(bf16[258,128]{1,0:T(8,128)(2,1)S(1)} %pad_maximum_fusion.2), channel_id=1, source_target_pairs={{0,6},{1,7},{2,4},{3,5},{4,10},{5,11},{6,8},{7,9},{8,14},{9,15},{1... | collective-permute-start | bytes 198152 | tf_op jit(solution)/shard_map/ppermute | solution.py:243
  14.3 3.6 %collective-permute-start = (bf16[32,256]{1,0:T(8,128)(2,1)S(1)}, bf16[32,256]{1,0:T(8,128)(2,1)S(1)}, u32[]{:S(2)}, u32[]{:S(2)}) collective-permute-start(bf16[32,256]{1,0:T(8,128)(2,1)S(1)} %get-tuple-element.15), channel_id=1, source_target_pairs={{0,1},{1,0},{2,3},{3,2},{4,5},{5,4},{6,7},{7,6},{8,9},{9,8},{10,11... | collective-permute-start | bytes 49160 | tf_op jit(solution)/shard_map/ppermute | solution.py:222
  17.8 4.6 %collective-permute-start.9 = (bf16[258,128]{1,0:T(8,128)(2,1)S(1)}, bf16[258,128]{1,0:T(8,128)(2,1)S(1)}, u32[]{:S(2)}, u32[]{:S(2)}) collective-permute-start(bf16[258,128]{1,0:T(8,128)(2,1)S(1)} %pad_maximum_fusion.2), channel_id=1, source_target_pairs={{0,2},{1,3},{2,0},{3,1},{4,6},{5,7},{6,4},{7,5},{8,10},{9,11},{10,... | collective-permute-start | bytes 198152 | tf_op jit(solution)/shard_map/ppermute | solution.py:243
  19.3 29.2 %copy-start.1 = (bf16[192,256]{1,0:T(8,128)(2,1)}, bf16[192,256]{1,0:T(8,128)(2,1)S(1)}, u32[]{:S(2)}) copy-start(bf16[192,256]{1,0:T(8,128)(2,1)S(1)} %pad_maximum_fusion.1.refs_1_) | copy-start | bytes 294916
  22.4 6.1 %collective-permute-start.10 = (bf16[258,128]{1,0:T(8,128)(2,1)S(1)}, bf16[258,128]{1,0:T(8,128)(2,1)S(1)}, u32[]{:S(2)}, u32[]{:S(2)}) collective-permute-start(bf16[258,128]{1,0:T(8,128)(2,1)S(1)} %pad_maximum_fusion.2), channel_id=1, source_target_pairs={{0,4},{1,5},{2,6},{3,7},{4,8},{5,9},{6,10},{7,11},{8,12},{9,13},{1... | collective-permute-start | bytes 198152 | tf_op jit(solution)/shard_map/ppermute | solution.py:243
  28.5 7.7 %collective-permute-start.15 = (bf16[258,128]{1,0:T(8,128)(2,1)S(1)}, bf16[258,128]{1,0:T(8,128)(2,1)S(1)}, u32[]{:S(2)}, u32[]{:S(2)}) collective-permute-start(bf16[258,128]{1,0:T(8,128)(2,1)S(1)} %pad_maximum_fusion.2), channel_id=1, source_target_pairs={{0,14},{1,15},{2,12},{3,13},{4,2},{5,3},{6,0},{7,1},{8,6},{9,7},{1... | collective-permute-start | bytes 198152 | tf_op jit(solution)/shard_map/ppermute | solution.py:243
  31.5 25.8 %collective-permute-start.7 = (bf16[192,256]{1,0:T(8,128)(2,1)S(1)}, bf16[192,256]{1,0:T(8,128)(2,1)S(1)}, u32[]{:S(2)}, u32[]{:S(2)}) collective-permute-start(bf16[192,256]{1,0:T(8,128)(2,1)S(1)} %pad_maximum_fusion.1.refs_1_), channel_id=1, source_target_pairs={{0,14},{1,15},{2,12},{3,13},{4,2},{5,3},{6,0},{7,1},{8,6},{9,7},{1... | collective-permute-start | bytes 294920 | tf_op jit(solution)/shard_map/ppermute | solution.py:239
  31.6 25.1 %collective-permute-start.6 = (bf16[192,256]{1,0:T(8,128)(2,1)S(1)}, bf16[192,256]{1,0:T(8,128)(2,1)S(1)}, u32[]{:S(2)}, u32[]{:S(2)}) collective-permute-start(bf16[192,256]{1,0:T(8,128)(2,1)S(1)} %pad_maximum_fusion.1.refs_1_), channel_id=1, source_target_pairs={{0,12},{1,13},{2,14},{3,15},{4,0},{5,1},{6,2},{7,3},{8,4},{9,5},{1... | collective-permute-start | bytes 294920 | tf_op jit(solution)/shard_map/ppermute | solution.py:239
  31.7 24.3 %collective-permute-start.5 = (bf16[192,256]{1,0:T(8,128)(2,1)S(1)}, bf16[192,256]{1,0:T(8,128)(2,1)S(1)}, u32[]{:S(2)}, u32[]{:S(2)}) collective-permute-start(bf16[192,256]{1,0:T(8,128)(2,1)S(1)} %pad_maximum_fusion.1.refs_1_), channel_id=1, source_target_pairs={{0,10},{1,11},{2,8},{3,9},{4,14},{5,15},{6,12},{7,13},{8,2},{9,3},... | collective-permute-start | bytes 294920 | tf_op jit(solution)/shard_map/ppermute | solution.py:239
  36.1 19.2 %collective-permute-start.4 = (bf16[192,256]{1,0:T(8,128)(2,1)S(1)}, bf16[192,256]{1,0:T(8,128)(2,1)S(1)}, u32[]{:S(2)}, u32[]{:S(2)}) collective-permute-start(bf16[192,256]{1,0:T(8,128)(2,1)S(1)} %pad_maximum_fusion.1.refs_1_), channel_id=1, source_target_pairs={{0,8},{1,9},{2,10},{3,11},{4,12},{5,13},{6,14},{7,15},{8,0},{9,1},... | collective-permute-start | bytes 294920 | tf_op jit(solution)/shard_map/ppermute | solution.py:239
  36.2 4.7 %collective-permute-start.1 = (bf16[192,256]{1,0:T(8,128)(2,1)S(1)}, bf16[192,256]{1,0:T(8,128)(2,1)S(1)}, u32[]{:S(2)}, u32[]{:S(2)}) collective-permute-start(bf16[192,256]{1,0:T(8,128)(2,1)S(1)} %pad_maximum_fusion.1.refs_1_), channel_id=1, source_target_pairs={{0,2},{1,3},{2,0},{3,1},{4,6},{5,7},{6,4},{7,5},{8,10},{9,11},{10,... | collective-permute-start | bytes 294920 | tf_op jit(solution)/shard_map/ppermute | solution.py:239
  40.9 22.9 %copy-start.6 = (bf16[192,256]{1,0:T(8,128)(2,1)}, bf16[192,256]{1,0:T(8,128)(2,1)S(1)}, u32[]{:S(2)}) copy-start(bf16[192,256]{1,0:T(8,128)(2,1)S(1)} %collective-permute-done.1.refs_2_) | copy-start | bytes 294916
  40.9 6.4 %collective-permute-start.2 = (bf16[192,256]{1,0:T(8,128)(2,1)S(1)}, bf16[192,256]{1,0:T(8,128)(2,1)S(1)}, u32[]{:S(2)}, u32[]{:S(2)}) collective-permute-start(bf16[192,256]{1,0:T(8,128)(2,1)S(1)} %pad_maximum_fusion.1.refs_1_), channel_id=1, source_target_pairs={{0,4},{1,5},{2,6},{3,7},{4,8},{5,9},{6,10},{7,11},{8,12},{9,13},{1... | collective-permute-start | bytes 294920 | tf_op jit(solution)/shard_map/ppermute | solution.py:239
  47.3 16.4 %copy-start.7 = (bf16[192,256]{1,0:T(8,128)(2,1)}, bf16[192,256]{1,0:T(8,128)(2,1)S(1)}, u32[]{:S(2)}) copy-start(bf16[192,256]{1,0:T(8,128)(2,1)S(1)} %collective-permute-done.2.refs_3_) | copy-start | bytes 294916
  47.3 7.3 %collective-permute-start.3 = (bf16[192,256]{1,0:T(8,128)(2,1)S(1)}, bf16[192,256]{1,0:T(8,128)(2,1)S(1)}, u32[]{:S(2)}, u32[]{:S(2)}) collective-permute-start(bf16[192,256]{1,0:T(8,128)(2,1)S(1)} %pad_maximum_fusion.1.refs_1_), channel_id=1, source_target_pairs={{0,6},{1,7},{2,4},{3,5},{4,10},{5,11},{6,8},{7,9},{8,14},{9,15},{1... | collective-permute-start | bytes 294920 | tf_op jit(solution)/shard_map/ppermute | solution.py:239
  54.7 9.1 %copy-start.8 = (bf16[192,256]{1,0:T(8,128)(2,1)}, bf16[192,256]{1,0:T(8,128)(2,1)S(1)}, u32[]{:S(2)}) copy-start(bf16[192,256]{1,0:T(8,128)(2,1)S(1)} %collective-permute-done.3.refs_4_) | copy-start | bytes 294916
  54.7 9.2 %collective-permute-start.16 = (bf16[8,258,128]{2,0,1:T(8,128)(2,1)S(1)}, bf16[8,258,128]{2,0,1:T(8,128)(2,1)S(1)}, u32[]{:S(2)}, u32[]{:S(2)}) collective-permute-start(bf16[8,258,128]{2,0,1:T(8,128)(2,1)S(1)} %copy.24), channel_id=1, source_target_pairs={{0,1},{1,0},{2,3},{3,2},{4,5},{5,4},{6,7},{7,6},{8,9},{9,8},{10,11... | collective-permute-start | bytes 1585160 | tf_op jit(solution)/shard_map/ppermute | solution.py:222
  55.3 8.4 %copy-start.5 = (bf16[192,256]{1,0:T(8,128)(2,1)}, bf16[192,256]{1,0:T(8,128)(2,1)S(1)}, u32[]{:S(2)}) copy-start(bf16[192,256]{1,0:T(8,128)(2,1)S(1)} %collective-permute-done.4.refs_5_) | copy-start | bytes 294916
  56.0 7.8 %copy-start.4 = (bf16[192,256]{1,0:T(8,128)(2,1)}, bf16[192,256]{1,0:T(8,128)(2,1)S(1)}, u32[]{:S(2)}) copy-start(bf16[192,256]{1,0:T(8,128)(2,1)S(1)} %collective-permute-done.5.refs_6_) | copy-start | bytes 294916
  56.7 7.1 %copy-start.3 = (bf16[192,256]{1,0:T(8,128)(2,1)}, bf16[192,256]{1,0:T(8,128)(2,1)S(1)}, u32[]{:S(2)}) copy-start(bf16[192,256]{1,0:T(8,128)(2,1)S(1)} %collective-permute-done.6.refs_7_) | copy-start | bytes 294916
  57.3 6.5 %copy-start.2 = (bf16[192,256]{1,0:T(8,128)(2,1)}, bf16[192,256]{1,0:T(8,128)(2,1)S(1)}, u32[]{:S(2)}) copy-start(bf16[192,256]{1,0:T(8,128)(2,1)S(1)} %collective-permute-done.7.refs_8_) | copy-start | bytes 294916
  58.0 8.6 %collective-permute-start.8 = (bf16[1024,256]{1,0:T(8,128)(2,1)}, bf16[1024,256]{1,0:T(8,128)(2,1)S(1)}, u32[]{:S(2)}, u32[]{:S(2)}) collective-permute-start(bf16[1024,256]{1,0:T(8,128)(2,1)} %slice_dynamic-update-slice_fusion), channel_id=1, source_target_pairs={{0,1},{1,0},{2,3},{3,2},{4,5},{5,4},{6,7},{7,6},{8,9},{9,8},{10,11... | collective-permute-start | bytes 1572872 | tf_op jit(solution)/shard_map/ppermute | solution.py:222
  66.6 0.8 copy-start
  96.6 5.2 %collective-permute-start.18 = (f32[256,512]{1,0:T(8,128)}, f32[256,512]{1,0:T(8,128)S(1)}, u32[]{:S(2)}, u32[]{:S(2)}) collective-permute-start(f32[256,512]{1,0:T(8,128)} %get-tuple-element.11), channel_id=1, source_target_pairs={{0,1},{1,0},{2,3},{3,2},{4,5},{5,4},{6,7},{7,6},{8,9},{9,8},{10,11... | collective-permute-start | bytes 1572872 | tf_op jit(solution)/shard_map/ppermute | solution.py:222
  96.6 2.3 %collective-permute-start.17 = (f32[136,256]{1,0:T(8,128)}, f32[136,256]{1,0:T(8,128)S(1)}, u32[]{:S(2)}, u32[]{:S(2)}) collective-permute-start(f32[136,256]{1,0:T(8,128)} %get-tuple-element.9), channel_id=1, source_target_pairs={{0,1},{1,0},{2,3},{3,2},{4,5},{5,4},{6,7},{7,6},{8,9},{9,8},{10,11... | collective-permute-start | bytes 417800 | tf_op jit(solution)/shard_map/ppermute | solution.py:222

commit v2 on v0

--- a/solution.py
+++ b/solution.py
@@ -1,7 +1,297 @@
+import functools
+
 import jax
 import jax.numpy as jnp
 from jax import lax
+from jax.experimental import pallas as pl
+from jax.experimental.pallas import tpu as pltpu
 from jax.sharding import PartitionSpec as P
+
+BF16 = jnp.bfloat16
+F32 = jnp.float32
+MAIN_VMEM = 36 << 20
+WEIGHTS_VMEM = 10 << 20
+X_AFTER = 5
+
+
+def dot(a, b, dims):
+    return lax.dot_general(a, b, ((dims[:1], dims[1:]), ((), ())), preferred_element_type=F32)
+
+
+def group_kernel(dest_ref, row_ref, col_ref, feats_ref, w_first_ref, panel_ref, piece_ref, *, rs, blk_dev, orbitals):
+    pre = dot(feats_ref[...], w_first_ref[...], (1, 0))
+    hidden = (pre * (0.5 * jnp.tanh(0.5 * pre) + 0.5)).astype(BF16)
+    pairs = feats_ref.shape[0]
+    dest = dest_ref[...]
+    gid = (dest % 2) * (2 * rs) + col_ref[...] * rs + (dest // 2) * blk_dev + row_ref[...]
+    rows = lax.broadcasted_iota(jnp.int32, (4 * rs, pairs), 0)
+    pick = (rows == gid).astype(F32).astype(BF16)
+    panel_end = 4 * rs + panel_ref.shape[0]
+    piece_ref[: 4 * rs, :] = (dot(pick, hidden, (1, 0)) * (1.0 / orbitals)).astype(BF16)
+    piece_ref[4 * rs : panel_end, :] = panel_ref[...]
+    piece_ref[panel_end:, :] = jnp.broadcast_to(gid.astype(F32), (8, pairs)).astype(BF16)
+
+
+def weights_kernel(w_ref, out_ref, sems):
+    chunks = sems.shape[0]
+    width = w_ref.shape[1] // chunks
+    copies = []
+    for k in range(chunks):
+        cols = slice(k * width, (k + 1) * width)
+        copies.append(pltpu.make_async_copy(w_ref.at[:, cols], out_ref.at[0, :, cols], sems.at[k]))
+        copies[-1].start()
+    for k in range(chunks):
+        copies[k].wait()
+        for q in range(k * width // 128, (k + 1) * width // 128):
+            cols = slice(q * 128, (q + 1) * 128)
+            out_ref[1, :, cols] = pltpu.roll(out_ref[0, :, cols].astype(F32), 64, 1).astype(BF16)
+
+
+def source_chip(m, chip, chips, z_count):
+    x_count = chips // z_count
+    return ((chip // x_count - m // x_count) % z_count) * x_count + (chip % x_count - m % x_count) % x_count
+
+
+def main_kernel(*refs, chips, z_count, rows_split, half_cols, orbitals):
+    me_ref, same_refs, other_refs = refs[0], refs[1 : 1 + chips], refs[1 + chips : 1 + 2 * chips]
+    (w_ref, energies_ref, res_ref, keep_ref, send_ref, dh_ref, square_ref, h_ref, c_ref, x_ref, r_ref, g_ref, l_ref) = refs[
+        1 + 2 * chips :
+    ]
+    me = me_ref[0]
+    core = me % 2
+    chip = me // 2
+    listers = 2 * chips
+    rs = rows_split
+    half = w_ref.shape[2] // 2
+    columns = energies_ref.shape[1]
+    ah_count = half // 128
+    total_blocks = 2 * rs
+    lane = lax.broadcasted_iota(jnp.int32, (rs, 128), 1)
+    low = lane < 64
+
+    def place(lister, block):
+        at = pl.multiple_of(lister * 128, 128)
+        c_ref[0, pl.ds(at, 128), :] = block
+        c_ref[1, pl.ds(at, 64), :] = block[64:, :]
+        c_ref[1, pl.ds(at + 64, 64), :] = block[:64, :]
+
+    for m in range(chips):
+        src = source_chip(m, chip, chips, z_count)
+        for piece, lister in ((same_refs[m], 2 * src + core), (other_refs[m], 2 * src + 1 - core)):
+            place(lister, piece[4 * rs : 4 * rs + 128, :])
+            at = pl.multiple_of(lister * rs, rs)
+            for pc in range(2):
+                h_ref[pc, pl.ds(at, rs), :] = piece[pl.ds(pl.multiple_of(core * 2 * rs, rs) + pc * rs, rs), :]
+
+    h0, h1 = h_ref[0], h_ref[1]
+    step_cols = 2048
+    steps = half // step_cols
+    per = step_cols // 128
+
+    def forward(i, carry):
+        hs, nb = i // steps, i % steps
+        at = pl.multiple_of(i * step_cols, step_cols)
+        y0 = dot(h0, w_ref[0, :, pl.ds(at, step_cols)], (1, 0))
+        y1 = dot(h1, w_ref[1, :, pl.ds(at, step_cols)], (1, 0))
+        for k in range(per):
+            row = pl.multiple_of((hs * ah_count + nb * per + k) * rs, rs)
+            for j in range(listers):
+                v0 = y0[j * rs : (j + 1) * rs, k * 128 : (k + 1) * 128]
+                v1 = y1[j * rs : (j + 1) * rs, k * 128 : (k + 1) * 128]
+                cols = slice(j * 128, (j + 1) * 128)
+                x_ref[0, pl.ds(row, rs), cols] = jnp.where(low, v0, v1).astype(BF16)
+                x_ref[1, pl.ds(row, rs), cols] = jnp.where(low, v1, v0).astype(BF16)
+        return carry
+
+    lax.fori_loop(0, 2 * steps, forward, 0)
+
+    energies = energies_ref[...]
+    n_rows = ah_count * rs
+    mb = 512
+    square_ref[...] = jnp.zeros_like(square_ref)
+
+    def product(i, carry):
+        par, b = i // (n_rows // mb), i % (n_rows // mb)
+        at = pl.multiple_of(b * mb, mb)
+        r_h = dot(x_ref[par, pl.ds(at, mb), :], c_ref[par], (1, 0))
+        r_s = dot(x_ref[par, pl.ds(n_rows + at, mb), :], c_ref[par], (1, 0))
+        res = r_h - r_s * energies
+        r_ref[par, pl.ds(at, mb), :] = res
+        g_ref[0, par, pl.ds(at, mb), :] = (res / total_blocks).astype(BF16)
+        g_ref[1, par, pl.ds(at, mb), :] = (-(res * energies) / total_blocks).astype(BF16)
+        square_ref[...] += jnp.sum((res * res).reshape(mb // 8, 8, columns), axis=0)
+        return carry
+
+    lax.fori_loop(0, 2 * (n_rows // mb), product, 0)
+
+    blk_dev = res_ref.shape[0]
+    for i in range(blk_dev):
+        for par in range(2):
+            for ah in range(ah_count):
+                res_ref[i, 2 * ah + par : 2 * ah + par + 1, :] = r_ref[
+                    par, pl.ds(ah * rs + chip * blk_dev + i, 1), :
+                ]
+
+    jb_count = 8
+    jb_width = jb_count * 128
+
+    def backward(i, carry):
+        hs, jb = i // (listers // jb_count), i % (listers // jb_count)
+        at = pl.multiple_of(jb * jb_width, jb_width)
+        d_e = dot(g_ref[hs, 0], c_ref[0, pl.ds(at, jb_width), :], (1, 1))
+        d_o = dot(g_ref[hs, 1], c_ref[1, pl.ds(at, jb_width), :], (1, 1))
+        for j in range(jb_count):
+            row = pl.multiple_of((jb * jb_count + j) * rs, rs)
+            for ah in range(ah_count):
+                v0 = d_e[ah * rs : (ah + 1) * rs, j * 128 : (j + 1) * 128]
+                v1 = d_o[ah * rs : (ah + 1) * rs, j * 128 : (j + 1) * 128]
+                cols = pl.ds(pl.multiple_of(hs * half + ah * 128, 128), 128)
+                l_ref[0, pl.ds(row, rs), cols] = jnp.where(low, v0, v1).astype(BF16)
+                l_ref[1, pl.ds(row, rs), cols] = jnp.where(low, v1, v0).astype(BF16)
+        return carry
+
+    lax.fori_loop(0, 2 * (listers // jb_count), backward, 0)
+
+    for pc in range(2):
+        dh_ref[pc] = dot(l_ref[pc], w_ref[pc], (1, 1)) / orbitals
+
+    width = 2 * half_cols
+    at = pl.multiple_of(chip * width, width)
+    g0 = dot(h0, l_ref[0, :, pl.ds(at, width)], (0, 0))
+    g1 = dot(h1, l_ref[1, :, pl.ds(at, width)], (0, 0))
+    even = core == 0
+    for k in range(half_cols // 128):
+        a, b = slice(k * 128, (k + 1) * 128), slice(half_cols + k * 128, half_cols + (k + 1) * 128)
+        va = g0[:, a] + pltpu.roll(g1[:, a], 64, 1)
+        vb = g0[:, b] + pltpu.roll(g1[:, b], 64, 1)
+        keep_ref[:, a] = jnp.where(even, va, vb)
+        send_ref[:, a] = jnp.where(even, vb, va)
+
+
+def first_kernel(*refs, chips, z_count, rs, pairs):
+    me_ref, same_refs, other_refs = refs[0], refs[1 : 1 + chips], refs[1 + chips : 1 + 2 * chips]
+    feat_refs = refs[1 + 2 * chips : 5 + 2 * chips]
+    w_first_ref, dh_ref, square_ref, first_ref, f_ref, d_ref = refs[5 + 2 * chips :]
+    me = me_ref[0]
+    core, chip = me % 2, me // 2
+    f_width = w_first_ref.shape[0]
+    x_count = chips // z_count
+    group_row = (lax.broadcasted_iota(jnp.int32, (2 * rs, pairs), 0) + core * (2 * rs)).astype(F32)
+    for m in range(chips):
+        src = source_chip(m, chip, chips, z_count)
+        dz, dx = m // x_count, m % x_count
+        for which, (piece, lister) in enumerate(((same_refs[m], 2 * src + core), (other_refs[m], 2 * src + 1 - core))):
+            feats = feat_refs[2 * which + dx][dz * pairs : (dz + 1) * pairs, :]
+            label = piece[piece.shape[0] - 8 :, :].astype(F32)[:1, :]
+            pre = dot(feats, w_first_ref[...], (1, 0))
+            sig = 0.5 * jnp.tanh(0.5 * pre) + 0.5
+            at = pl.multiple_of(lister * rs, rs)
+            d_group = jnp.concatenate([dh_ref[0, pl.ds(at, rs), :], dh_ref[1, pl.ds(at, rs), :]], axis=0)
+            head = d_group.astype(BF16)
+            tail = (d_group - head.astype(F32)).astype(BF16)
+            both = jnp.concatenate([head, tail], axis=0)
+            pick = (group_row == label).astype(F32).astype(BF16)
+            d_hidden = dot(jnp.concatenate([pick, pick], axis=0), both, (0, 0))
+            to = pl.multiple_of(lister * pairs, pairs)
+            d_ref[pl.ds(to, pairs), :] = (d_hidden * sig * (1.0 + pre * (1.0 - sig))).astype(BF16)
+            f_ref[pl.ds(to, pairs), :] = feats
+    first_ref[:f_width, :] = dot(f_ref[...], d_ref[...], (0, 0))
+    first_ref[f_width:, :] = square_ref[...]
+
+
+def near(features, w_first, w_second, panel, energies, pair_dest, pair_row, pair_col, z_count):
+    n_dev = lax.axis_size("blk")
+    me = lax.axis_index("blk").reshape(1).astype(jnp.int32)
+    pairs, f_width = features.shape
+    blk_dev, orbitals, columns = panel.shape
+    hid, flat = w_second.shape
+    chips, rs = n_dev // 2, n_dev * blk_dev // 2
+    half_cols = flat // n_dev
+    smem, vmem = pl.BlockSpec(memory_space=pltpu.SMEM), pl.BlockSpec(memory_space=pltpu.VMEM)
+
+    def to_x(v):
+        return from_chip(v, 1)
+
+    piece = pl.pallas_call(
+        functools.partial(group_kernel, rs=rs, blk_dev=blk_dev, orbitals=orbitals),
+        out_shape=jax.ShapeDtypeStruct((4 * rs + blk_dev * orbitals + 8, hid), BF16),
+        cost_estimate=pl.CostEstimate(flops=1 << 28, transcendentals=0, bytes_accessed=1 << 20),
+        name="group",
+    )(
+        pair_dest.reshape(1, pairs),
+        pair_row.reshape(1, pairs),
+        pair_col.reshape(1, pairs),
+        features,
+        w_first,
+        panel.reshape(blk_dev * orbitals, columns),
+    )
+    weights = pl.pallas_call(
+        weights_kernel,
+        out_shape=jax.ShapeDtypeStruct((2, hid, flat), BF16),
+        in_specs=[pl.BlockSpec(memory_space=pl.ANY)],
+        scratch_shapes=[pltpu.SemaphoreType.DMA((8,))],
+        compiler_params=pltpu.CompilerParams(vmem_limit_bytes=WEIGHTS_VMEM),
+        cost_estimate=pl.CostEstimate(flops=0, transcendentals=0, bytes_accessed=8 * hid * flat),
+        name="weights",
+    )(w_second)
+
+    def to_core(v):
+        return lax.ppermute(v, "blk", [(i, i ^ 1) for i in range(n_dev)])
+
+    def from_chip(v, m):
+        sends = [(2 * source_chip(m, q, chips, z_count) + c, 2 * q + c) for q in range(chips) for c in range(2)]
+        return lax.ppermute(v, "blk", sends) if m else v
+
+    x_count = chips // z_count
+    parts = [from_chip(features, dz * x_count) for dz in range(z_count)]
+    piece, *parts = lax.optimization_barrier((piece, *parts))
+    same = [from_chip(piece, m) for m in range(chips)]
+    feats_mine, same[X_AFTER] = lax.optimization_barrier((jnp.concatenate(parts, axis=0), same[X_AFTER]))
+    feats = [feats_mine, to_x(feats_mine)]
+    other = [to_core(v) for v in same]
+    feats += [to_core(v) for v in feats]
+
+    listers = n_dev
+    k_width = listers * 128
+    n_rows = rs * orbitals // 2
+    res, keep, send, d_hidden, square = pl.pallas_call(
+        functools.partial(
+            main_kernel, chips=chips, z_count=z_count, rows_split=rs, half_cols=half_cols, orbitals=orbitals
+        ),
+        out_shape=(
+            jax.ShapeDtypeStruct((blk_dev, orbitals, columns), F32),
+            jax.ShapeDtypeStruct((hid, half_cols), F32),
+            jax.ShapeDtypeStruct((hid, half_cols), F32),
+            jax.ShapeDtypeStruct((2, listers * rs, hid), F32),
+            jax.ShapeDtypeStruct((8, columns), F32),
+        ),
+        in_specs=[smem] + [vmem] * (2 * chips + 2),
+        scratch_shapes=[
+            pltpu.VMEM((2, listers * rs, hid), BF16),
+            pltpu.VMEM((2, k_width, columns), BF16),
+            pltpu.VMEM((2, 2 * n_rows, k_width), BF16),
+            pltpu.VMEM((2, n_rows, columns), F32),
+            pltpu.VMEM((2, 2, n_rows, columns), BF16),
+            pltpu.VMEM((2, listers * rs, flat), BF16),
+        ],
+        compiler_params=pltpu.CompilerParams(vmem_limit_bytes=MAIN_VMEM),
+        cost_estimate=pl.CostEstimate(flops=16 * listers * rs * hid * flat, transcendentals=0, bytes_accessed=1 << 24),
+        name="step",
+    )(me, *same, *other, weights, energies.reshape(1, columns))
+    send = to_core(send)
+    first = pl.pallas_call(
+        functools.partial(first_kernel, chips=chips, z_count=z_count, rs=rs, pairs=pairs),
+        out_shape=jax.ShapeDtypeStruct((f_width + 8, hid), F32),
+        in_specs=[smem] + [vmem] * (2 * chips + 7),
+        scratch_shapes=[pltpu.VMEM((n_dev * pairs, f_width), BF16), pltpu.VMEM((n_dev * pairs, hid), BF16)],
+        compiler_params=pltpu.CompilerParams(vmem_limit_bytes=12 << 20),
+        cost_estimate=pl.CostEstimate(flops=1 << 31, transcendentals=0, bytes_accessed=1 << 22),
+        name="first",
+    )(me, *same, *other, *feats, w_first, d_hidden, square)
+    grad_second = keep + send
+    first = first + to_core(first)
+    loss = (jnp.sum(first[f_width:]) / (n_dev * blk_dev * orbitals * columns)).reshape(1)
+    return (res, loss, first[:f_width], grad_second)
 
 
 def predict(feats, w_first, w_second, orbitals):
@@ -140,4 +430,6 @@
         P(("parts", "blk")),
     )
     out_specs = (P(("parts", "blk"), None, None), P("parts"), P("parts", None), P("parts", "blk"))
-    return jax.shard_map(local, mesh=mesh, in_specs=in_specs, out_specs=out_specs, check_vma=False)
+    n_dev = mesh.shape["blk"]
+    step = functools.partial(near, z_count=4) if n_dev == 16 else local
+    return jax.shard_map(step, mesh=mesh, in_specs=in_specs, out_specs=out_specs, check_vma=False)

time: 830 us -> 63.1 us (0.08)
  waiting for transfers between devices: 377 us -> 14.4 us
  local copies, waits for them, and re-layouts: 186 us -> 2.87 us
  matrix products: 124 us -> 0 us
  blocking collectives: 56.7 us -> 0 us
  starting transfers between devices: 42.1 us -> 19.6 us
  Pallas kernels: 0 us -> 21.1 us
  other arithmetic: 21.9 us -> 2.34 us
  between operations: 15.7 us -> 2.51 us
    dot_general x64 -> x0, matrix products: 124 us -> none  [the longest x12 26.3 us: forward(): jnp.einsum('rs,sap->rap', selector, contrib, precision=lax.Precision.HIGH...]
    all_to_all x3 -> x0, waiting for transfers between devices: 123 us -> none  [the longest x1 114 us: local(): lax.all_to_all(d_blocks.reshape(n_dev, capacity, 2, orbitals, orbitals),...]
    reduce_scatter x1 -> x0, waiting for transfers between devices: 109 us -> none  [local(): lax.psum_scatter(term_second, 'blk', scatter_dimension=1, tiled=True)]
    all_gather x1 -> x0, waiting for transfers between devices: 98 us -> none  [local(): whole_panel = lax.all_gather(panel, 'blk', axis=0, tiled=True)]
    unnamed x10 -> x8, local copies, waits for them, and re-layouts: 68.4 us -> 2.2 us
    gather x29 -> x0, local copies, waits for them, and re-layouts: 62.9 us -> none  [the longest x1 17.6 us: local(): send_blocks = padded[source].reshape(n_dev, capacity, 2, orbitals, orbitals)]
    psum x1 -> x0, blocking collectives: 56.7 us -> none  [local(): lax.psum((term_first, jnp.sum(residual * residual)), 'blk')]
    psum x1 -> x0, waiting for transfers between devices: 45.8 us -> none  [local(): lax.psum((term_first, jnp.sum(residual * residual)), 'blk')]
  transfers between devices with their start and end apart: 6 -> 23, of which waited for: 5 -> 7; matrix products, arithmetic and copies ran while one was open for 10% -> 3% of each run, Pallas kernels for 0% -> 34%
where the time goes in v2:
time: 63.1 us; the launch traced here: 62.8 us
  Pallas kernels  21.1 us (33%)
  starting transfers between devices  19.6 us (31%)
  waiting for transfers between devices  14.4 us (23%)
  local copies, waits for them, and re-layouts  2.87 us (5%)
  between operations  2.51 us (4%)
  other arithmetic  2.34 us (4%)
    ppermute x11, starting transfers between devices, from_chip(): return lax.ppermute(v, 'blk', sends) if m else v  16.8 us
    pallas_call x1, Pallas kernels, near(): pl.pallas_call(functools.partial(main_kernel, chips=chips, z_count=z_coun...  14.5 us
    ppermute x11, waiting for transfers between devices, from_chip(): return lax.ppermute(v, 'blk', sends) if m else v  13.7 us
    ppermute x12, starting transfers between devices, to_core(): return lax.ppermute(v, 'blk', [(i, i ^ 1) for i in range(n_dev)])  2.84 us
    pallas_call x1, Pallas kernels, near(): pl.pallas_call(functools.partial(first_kernel, chips=chips, z_count=z_cou...  2.56 us
    unnamed x8, local copies, waits for them, and re-layouts  2.2 us
    pallas_call x1, Pallas kernels, near(): pl.pallas_call(weights_kernel, out_shape=jax.ShapeDtypeStruct((2, hid, fl...  2.19 us
    pallas_call x1, Pallas kernels, near(): pl.pallas_call(functools.partial(group_kernel, rs=rs, blk_dev=blk_dev, or...  1.93 us
  transfers between devices with their start and end apart: 23, of which 7 were waited for; matrix products, arithmetic and copies ran while one was open for 3% of the time, Pallas kernels for 34%

profile of v2, /device:TPU:0, one launch (start us, length us, event | category | flops | bytes accessed | tf_op | source)
XLA Modules:
  0.0 62.8 jit_solution(765370079590451371)
XLA Ops:
  0.6 3.1 %collective-permute-start = (bf16[256,128]{1,0:T(8,128)(2,1)}, bf16[256,128]{1,0:T(8,128)(2,1)S(1)}, u32[]{:S(2)}, u32[]{:S(2)}) collective-permute-start(bf16[256,128]{1,0:T(8,128)(2,1)} %feats_ref.1), channel_id=1, source_target_pairs={{12,0},{13,1},{14,2},{15,3},{0,4},{1,5},{2,6},{3,7},{4,8},{5,9},{6... | collective-permute-start | bytes 196616 | tf_op jit(solution)/shard_map/ppermute | solution.py:243
  3.7 2.6 %collective-permute-start.1 = (bf16[256,128]{1,0:T(8,128)(2,1)}, bf16[256,128]{1,0:T(8,128)(2,1)S(1)}, u32[]{:S(2)}, u32[]{:S(2)}) collective-permute-start(bf16[256,128]{1,0:T(8,128)(2,1)} %feats_ref.1), channel_id=1, source_target_pairs={{8,0},{9,1},{10,2},{11,3},{12,4},{13,5},{14,6},{15,7},{0,8},{1,9},... | collective-permute-start | bytes 196616 | tf_op jit(solution)/shard_map/ppermute | solution.py:243
  6.3 1.3 %collective-permute-start.2 = (bf16[256,128]{1,0:T(8,128)(2,1)}, bf16[256,128]{1,0:T(8,128)(2,1)S(1)}, u32[]{:S(2)}, u32[]{:S(2)}) collective-permute-start(bf16[256,128]{1,0:T(8,128)(2,1)} %feats_ref.1), channel_id=1, source_target_pairs={{4,0},{5,1},{6,2},{7,3},{8,4},{9,5},{10,6},{11,7},{12,8},{13,9},{1... | collective-permute-start | bytes 196616 | tf_op jit(solution)/shard_map/ppermute | solution.py:243
  7.7 1.9 %group.1.refs_1_ = bf16[200,256]{1,0:T(8,128)(2,1)} custom-call(s32[1,256]{1,0:T(1,128)} %bitcast.9, s32[1,256]{1,0:T(1,128)} %bitcast.10, s32[1,256]{1,0:T(1,128)} %bitcast.11, bf16[256,128]{1,0:T(8,128)(2,1)} %feats_ref.1, bf16[128,256]{1,0:T(8,128)(2,1)} %refs_21_.1, bf16[128,256]{1,0:T(8,128)(2,1)} %bitcast.8), custom_call_target="tpu_custom_call" | custom-call | flops 268435456 | bytes 1048576 | tf_op jit(solution)/shard_map/group/pallas_call | solution.py:215
  9.6 1.4 %collective-permute-done.1 = bf16[256,128]{1,0:T(8,128)(2,1)S(1)} collective-permute-done((bf16[256,128]{1,0:T(8,128)(2,1)}, bf16[256,128]{1,0:T(8,128)(2,1)S(1)}, u32[]{:S(2)}, u32[]{:S(2)}) %collective-permute-start.1) | collective-permute-done | bytes 65568 | tf_op jit(solution)/shard_map/ppermute | solution.py:243
  11.0 0.2 collective-permute-done.2
  11.2 1.7 %collective-permute-start.7 = (bf16[200,256]{1,0:T(8,128)(2,1)}, bf16[200,256]{1,0:T(8,128)(2,1)S(1)}, u32[]{:S(2)}, u32[]{:S(2)}) collective-permute-start(bf16[200,256]{1,0:T(8,128)(2,1)} %group.1.refs_1_), channel_id=1, source_target_pairs={{10,0},{11,1},{8,2},{9,3},{14,4},{15,5},{12,6},{13,7},{2,8},{3,9},... | collective-permute-start | bytes 307208 | tf_op jit(solution)/shard_map/ppermute | solution.py:243
  13.0 0.5 collective-permute-start.3
  13.5 2.8 %collective-permute-start.4 = (bf16[200,256]{1,0:T(8,128)(2,1)}, bf16[200,256]{1,0:T(8,128)(2,1)S(1)}, u32[]{:S(2)}, u32[]{:S(2)}) collective-permute-start(bf16[200,256]{1,0:T(8,128)(2,1)} %group.1.refs_1_), channel_id=1, source_target_pairs={{12,0},{13,1},{14,2},{15,3},{0,4},{1,5},{2,6},{3,7},{4,8},{5,9},{6... | collective-permute-start | bytes 307208 | tf_op jit(solution)/shard_map/ppermute | solution.py:243
  16.3 0.9 %collective-permute-start.5 = (bf16[200,256]{1,0:T(8,128)(2,1)}, bf16[200,256]{1,0:T(8,128)(2,1)S(1)}, u32[]{:S(2)}, u32[]{:S(2)}) collective-permute-start(bf16[200,256]{1,0:T(8,128)(2,1)} %group.1.refs_1_), channel_id=1, source_target_pairs={{14,0},{15,1},{12,2},{13,3},{2,4},{3,5},{0,6},{1,7},{6,8},{7,9},{4... | collective-permute-start | bytes 307208 | tf_op jit(solution)/shard_map/ppermute | solution.py:243
  17.2 1.6 %collective-permute-start.6 = (bf16[200,256]{1,0:T(8,128)(2,1)}, bf16[200,256]{1,0:T(8,128)(2,1)S(1)}, u32[]{:S(2)}, u32[]{:S(2)}) collective-permute-start(bf16[200,256]{1,0:T(8,128)(2,1)} %group.1.refs_1_), channel_id=1, source_target_pairs={{8,0},{9,1},{10,2},{11,3},{12,4},{13,5},{14,6},{15,7},{0,8},{1,9},... | collective-permute-start | bytes 307208 | tf_op jit(solution)/shard_map/ppermute | solution.py:243
  18.8 8.9 %collective-permute-done.7.refs_6_ = bf16[200,256]{1,0:T(8,128)(2,1)S(1)} collective-permute-done((bf16[200,256]{1,0:T(8,128)(2,1)}, bf16[200,256]{1,0:T(8,128)(2,1)S(1)}, u32[]{:S(2)}, u32[]{:S(2)}) %collective-permute-start.7) | collective-permute-done | bytes 102432 | tf_op jit(solution)/shard_map/ppermute | solution.py:243
  27.7 1.0 %collective-permute-start.9 = (bf16[200,256]{1,0:T(8,128)(2,1)}, bf16[200,256]{1,0:T(8,128)(2,1)S(1)}, u32[]{:S(2)}, u32[]{:S(2)}) collective-permute-start(bf16[200,256]{1,0:T(8,128)(2,1)} %group.1.refs_1_), channel_id=1, source_target_pairs={{6,0},{7,1},{4,2},{5,3},{10,4},{11,5},{8,6},{9,7},{14,8},{15,9},{1... | collective-permute-start | bytes 307208 | tf_op jit(solution)/shard_map/ppermute | solution.py:243
  28.7 0.9 %pad_maximum_fusion.refs_17_ = bf16[1024,128]{1,0:T(8,128)(2,1)S(1)} fusion(bf16[256,128]{1,0:T(8,128)(2,1)S(1)} %collective-permute-done.2, bf16[256,128]{1,0:T(8,128)(2,1)S(1)} %collective-permute-done.1, bf16[256,128]{1,0:T(8,128)(2,1)S(1)} %collective-permute-done, bf16[256,128]{1,0:T(8,128)(2,1)} %feats_ref.1), kind=kLoop, calls=%fused_computation | loop fusion | flops 1048576 | bytes 524288 | tf_op jit(solution)/shard_map/concatenate | solution.py:249
  29.5 1.2 %collective-permute-start.18 = (bf16[1024,128]{1,0:T(8,128)(2,1)S(1)}, bf16[1024,128]{1,0:T(8,128)(2,1)S(1)}, u32[]{:S(2)}, u32[]{:S(2)}) collective-permute-start(bf16[1024,128]{1,0:T(8,128)(2,1)S(1)} %pad_maximum_fusion.refs_17_), channel_id=1, source_target_pairs={{2,0},{3,1},{0,2},{1,3},{6,4},{7,5},{4,6},{5,7},{10,8},{11,9},{8,1... | collective-permute-start | bytes 786440 | tf_op jit(solution)/shard_map/ppermute | solution.py:243
  30.8 0.5 collective-permute-start.15
  31.3 1.3 %collective-permute-done.8.refs_7_ = bf16[200,256]{1,0:T(8,128)(2,1)S(1)} collective-permute-done((bf16[200,256]{1,0:T(8,128)(2,1)}, bf16[200,256]{1,0:T(8,128)(2,1)S(1)}, u32[]{:S(2)}, u32[]{:S(2)}) %collective-permute-start.8) | collective-permute-done | bytes 102432 | tf_op jit(solution)/shard_map/ppermute | solution.py:243
  32.6 1.9 %collective-permute-done.9.refs_8_ = bf16[200,256]{1,0:T(8,128)(2,1)S(1)} collective-permute-done((bf16[200,256]{1,0:T(8,128)(2,1)}, bf16[200,256]{1,0:T(8,128)(2,1)S(1)}, u32[]{:S(2)}, u32[]{:S(2)}) %collective-permute-start.9) | collective-permute-done | bytes 102432 | tf_op jit(solution)/shard_map/ppermute | solution.py:243
  34.5 0.5 collective-permute-start.13
  35.1 0.4 collective-permute-start.16
  35.5 0.3 collective-permute-done.12.refs_11_
  35.9 2.2 %copy-done = bf16[256,8192]{1,0:T(8,128)(2,1)S(1)} copy-done((bf16[256,8192]{1,0:T(8,128)(2,1)S(1)}, bf16[256,8192]{1,0:T(8,128)(2,1)}, u32[]{:S(2)}) %copy-start) | copy-done | bytes 4194328
  38.1 2.2 %weights.1.refs_17_ = bf16[2,256,8192]{2,1,0:T(8,128)(2,1)S(1)} custom-call(bf16[256,8192]{1,0:T(8,128)(2,1)S(1)} %copy-done), custom_call_target="tpu_custom_call" | custom-call | bytes 16777216 | tf_op jit(solution)/shard_map/weights/pallas_call | solution.py:228
  40.3 0.4 collective-permute-start.19
  41.0 14.5 %step.1 = (f32[2,64,256]{2,1,0:T(8,128)}, f32[256,512]{1,0:T(8,128)S(1)}, f32[256,512]{1,0:T(8,128)S(1)}, f32[2,256,256]{2,1,0:T(8,128)S(1)}, f32[8,256]{1,0:T(8,128)S(1)}) custom-call(s32[1]{0:T(128)} %bitcast.refs_0_, bf16[200,256]{1,0:T(8,128)(2,1)S(1)} %copy-done.1, bf16[200,256]{1,0:T(8,128)(2,1)S(1)} %collective-permute-done.3.refs_2_, ...), custom_call_target="tpu_custom_call" | custom-call | flops 8589934592 | bytes 16777216 | tf_op jit(solution)/shard_map/step/pallas_call | solution.py:257
  55.4 0.4 collective-permute-start.22
  55.8 2.6 %first.1 = f32[136,256]{1,0:T(8,128)S(1)} custom-call(s32[1]{0:T(128)} %bitcast.refs_0_, bf16[200,256]{1,0:T(8,128)(2,1)S(1)} %copy-done.1, bf16[200,256]{1,0:T(8,128)(2,1)S(1)} %collective-permute-done.3.refs_2_, bf16[200,256]{1,0:T(8,128)(2,1)S(1)} %collective-permute-done.4.refs_3_, bf16[200,256]{1,0:T(8,128)(2,1)S(1)} %collective-permute-done.5.refs_4_, ...), custom_call_target="tpu_custom_call" | custom-call | flops 2147483648 | bytes 4194304 | tf_op jit(solution)/shard_map/first/pallas_call | solution.py:282
  58.4 0.2 collective-permute-start.21
  58.6 0.9 %add.7 = f32[256,512]{1,0:T(8,128)} add(f32[256,512]{1,0:T(8,128)S(1)} %get-tuple-element.26, f32[256,512]{1,0:T(8,128)S(1)} %collective-permute-done.22) | non-fusion elementwise | flops 131072 | bytes 1572864 | tf_op jit(solution)/shard_map/add | solution.py:291
  59.4 0.3 collective-permute-done.21
  59.8 0.7 %slice.9 = f32[128,256]{1,0:T(8,128)} slice(f32[136,256]{1,0:T(8,128)S(1)} %add.6), slice={[0:128], [0:256]} | slice | bytes 262144 | tf_op jit(solution)/shard_map/slice | solution.py:294
  60.5 0.6 slice_reduce_fusion
  (31 shorter events, 0.5 us)
Async XLA Ops:
  0.6 40.3 %copy-start.3 = (f32[256]{0:T(256)S(1)}, f32[256]{0:T(256)}, u32[]{:S(2)}) copy-start(f32[256]{0:T(256)} %param.12) | copy-start | bytes 3076
  0.6 9.0 %collective-permute-start = (bf16[256,128]{1,0:T(8,128)(2,1)}, bf16[256,128]{1,0:T(8,128)(2,1)S(1)}, u32[]{:S(2)}, u32[]{:S(2)}) collective-permute-start(bf16[256,128]{1,0:T(8,128)(2,1)} %feats_ref.1), channel_id=1, source_target_pairs={{12,0},{13,1},{14,2},{15,3},{0,4},{1,5},{2,6},{3,7},{4,8},{5,9},{6... | collective-permute-start | bytes 196616 | tf_op jit(solution)/shard_map/ppermute | solution.py:243
  3.7 7.3 %collective-permute-start.1 = (bf16[256,128]{1,0:T(8,128)(2,1)}, bf16[256,128]{1,0:T(8,128)(2,1)S(1)}, u32[]{:S(2)}, u32[]{:S(2)}) collective-permute-start(bf16[256,128]{1,0:T(8,128)(2,1)} %feats_ref.1), channel_id=1, source_target_pairs={{8,0},{9,1},{10,2},{11,3},{12,4},{13,5},{14,6},{15,7},{0,8},{1,9},... | collective-permute-start | bytes 196616 | tf_op jit(solution)/shard_map/ppermute | solution.py:243
  6.3 4.9 %collective-permute-start.2 = (bf16[256,128]{1,0:T(8,128)(2,1)}, bf16[256,128]{1,0:T(8,128)(2,1)S(1)}, u32[]{:S(2)}, u32[]{:S(2)}) collective-permute-start(bf16[256,128]{1,0:T(8,128)(2,1)} %feats_ref.1), channel_id=1, source_target_pairs={{4,0},{5,1},{6,2},{7,3},{8,4},{9,5},{10,6},{11,7},{12,8},{13,9},{1... | collective-permute-start | bytes 196616 | tf_op jit(solution)/shard_map/ppermute | solution.py:243
  9.6 31.3 %copy-start.1 = (bf16[200,256]{1,0:T(8,128)(2,1)S(1)}, bf16[200,256]{1,0:T(8,128)(2,1)}, u32[]{:S(2)}) copy-start(bf16[200,256]{1,0:T(8,128)(2,1)} %group.1.refs_1_) | copy-start | bytes 307204
  11.2 16.5 %collective-permute-start.7 = (bf16[200,256]{1,0:T(8,128)(2,1)}, bf16[200,256]{1,0:T(8,128)(2,1)S(1)}, u32[]{:S(2)}, u32[]{:S(2)}) collective-permute-start(bf16[200,256]{1,0:T(8,128)(2,1)} %group.1.refs_1_), channel_id=1, source_target_pairs={{10,0},{11,1},{8,2},{9,3},{14,4},{15,5},{12,6},{13,7},{2,8},{3,9},... | collective-permute-start | bytes 307208 | tf_op jit(solution)/shard_map/ppermute | solution.py:243
  13.0 14.7 %collective-permute-start.3 = (bf16[200,256]{1,0:T(8,128)(2,1)}, bf16[200,256]{1,0:T(8,128)(2,1)S(1)}, u32[]{:S(2)}, u32[]{:S(2)}) collective-permute-start(bf16[200,256]{1,0:T(8,128)(2,1)} %group.1.refs_1_), channel_id=1, source_target_pairs={{2,0},{3,1},{0,2},{1,3},{6,4},{7,5},{4,6},{5,7},{10,8},{11,9},{8,1... | collective-permute-start | bytes 307208 | tf_op jit(solution)/shard_map/ppermute | solution.py:243
  13.5 16.0 %collective-permute-start.4 = (bf16[200,256]{1,0:T(8,128)(2,1)}, bf16[200,256]{1,0:T(8,128)(2,1)S(1)}, u32[]{:S(2)}, u32[]{:S(2)}) collective-permute-start(bf16[200,256]{1,0:T(8,128)(2,1)} %group.1.refs_1_), channel_id=1, source_target_pairs={{12,0},{13,1},{14,2},{15,3},{0,4},{1,5},{2,6},{3,7},{4,8},{5,9},{6... | collective-permute-start | bytes 307208 | tf_op jit(solution)/shard_map/ppermute | solution.py:243
  16.3 14.5 %collective-permute-start.5 = (bf16[200,256]{1,0:T(8,128)(2,1)}, bf16[200,256]{1,0:T(8,128)(2,1)S(1)}, u32[]{:S(2)}, u32[]{:S(2)}) collective-permute-start(bf16[200,256]{1,0:T(8,128)(2,1)} %group.1.refs_1_), channel_id=1, source_target_pairs={{14,0},{15,1},{12,2},{13,3},{2,4},{3,5},{0,6},{1,7},{6,8},{7,9},{4... | collective-permute-start | bytes 307208 | tf_op jit(solution)/shard_map/ppermute | solution.py:243
  17.2 13.5 %collective-permute-start.6 = (bf16[200,256]{1,0:T(8,128)(2,1)}, bf16[200,256]{1,0:T(8,128)(2,1)S(1)}, u32[]{:S(2)}, u32[]{:S(2)}) collective-permute-start(bf16[200,256]{1,0:T(8,128)(2,1)} %group.1.refs_1_), channel_id=1, source_target_pairs={{8,0},{9,1},{10,2},{11,3},{12,4},{13,5},{14,6},{15,7},{0,8},{1,9},... | collective-permute-start | bytes 307208 | tf_op jit(solution)/shard_map/ppermute | solution.py:243
  27.7 4.9 %collective-permute-start.8 = (bf16[200,256]{1,0:T(8,128)(2,1)}, bf16[200,256]{1,0:T(8,128)(2,1)S(1)}, u32[]{:S(2)}, u32[]{:S(2)}) collective-permute-start(bf16[200,256]{1,0:T(8,128)(2,1)} %group.1.refs_1_), channel_id=1, source_target_pairs={{4,0},{5,1},{6,2},{7,3},{8,4},{9,5},{10,6},{11,7},{12,8},{13,9},{1... | collective-permute-start | bytes 307208 | tf_op jit(solution)/shard_map/ppermute | solution.py:243
  27.7 6.8 %collective-permute-start.9 = (bf16[200,256]{1,0:T(8,128)(2,1)}, bf16[200,256]{1,0:T(8,128)(2,1)S(1)}, u32[]{:S(2)}, u32[]{:S(2)}) collective-permute-start(bf16[200,256]{1,0:T(8,128)(2,1)} %group.1.refs_1_), channel_id=1, source_target_pairs={{6,0},{7,1},{4,2},{5,3},{10,4},{11,5},{8,6},{9,7},{14,8},{15,9},{1... | collective-permute-start | bytes 307208 | tf_op jit(solution)/shard_map/ppermute | solution.py:243
  29.5 11.2 %collective-permute-start.18 = (bf16[1024,128]{1,0:T(8,128)(2,1)S(1)}, bf16[1024,128]{1,0:T(8,128)(2,1)S(1)}, u32[]{:S(2)}, u32[]{:S(2)}) collective-permute-start(bf16[1024,128]{1,0:T(8,128)(2,1)S(1)} %pad_maximum_fusion.refs_17_), channel_id=1, source_target_pairs={{2,0},{3,1},{0,2},{1,3},{6,4},{7,5},{4,6},{5,7},{10,8},{11,9},{8,1... | collective-permute-start | bytes 786440 | tf_op jit(solution)/shard_map/ppermute | solution.py:243
  30.8 3.7 %collective-permute-start.10 = (bf16[200,256]{1,0:T(8,128)(2,1)}, bf16[200,256]{1,0:T(8,128)(2,1)S(1)}, u32[]{:S(2)}, u32[]{:S(2)}) collective-permute-start(bf16[200,256]{1,0:T(8,128)(2,1)} %group.1.refs_1_), channel_id=1, source_target_pairs={{0,1},{1,0},{2,3},{3,2},{4,5},{5,4},{6,7},{7,6},{8,9},{9,8},{10,11... | collective-permute-start | bytes 307208 | tf_op jit(solution)/shard_map/ppermute | solution.py:239
  30.8 4.2 %collective-permute-start.15 = (bf16[200,256]{1,0:T(8,128)(2,1)S(1)}, bf16[200,256]{1,0:T(8,128)(2,1)S(1)}, u32[]{:S(2)}, u32[]{:S(2)}) collective-permute-start(bf16[200,256]{1,0:T(8,128)(2,1)S(1)} %collective-permute-done.7.refs_6_), channel_id=1, source_target_pairs={{0,1},{1,0},{2,3},{3,2},{4,5},{5,4},{6,7},{7,6},{8,9},{9,8},{10,11... | collective-permute-start | bytes 307208 | tf_op jit(solution)/shard_map/ppermute | solution.py:239
  32.6 2.5 %collective-permute-start.11 = (bf16[200,256]{1,0:T(8,128)(2,1)S(1)}, bf16[200,256]{1,0:T(8,128)(2,1)S(1)}, u32[]{:S(2)}, u32[]{:S(2)}) collective-permute-start(bf16[200,256]{1,0:T(8,128)(2,1)S(1)} %collective-permute-done.3.refs_2_), channel_id=1, source_target_pairs={{0,1},{1,0},{2,3},{3,2},{4,5},{5,4},{6,7},{7,6},{8,9},{9,8},{10,11... | collective-permute-start | bytes 307208 | tf_op jit(solution)/shard_map/ppermute | solution.py:239
  34.5 1.3 %collective-permute-start.12 = (bf16[200,256]{1,0:T(8,128)(2,1)S(1)}, bf16[200,256]{1,0:T(8,128)(2,1)S(1)}, u32[]{:S(2)}, u32[]{:S(2)}) collective-permute-start(bf16[200,256]{1,0:T(8,128)(2,1)S(1)} %collective-permute-done.4.refs_3_), channel_id=1, source_target_pairs={{0,1},{1,0},{2,3},{3,2},{4,5},{5,4},{6,7},{7,6},{8,9},{9,8},{10,11... | collective-permute-start | bytes 307208 | tf_op jit(solution)/shard_map/ppermute | solution.py:239
  34.5 5.8 %collective-permute-start.13 = (bf16[200,256]{1,0:T(8,128)(2,1)S(1)}, bf16[200,256]{1,0:T(8,128)(2,1)S(1)}, u32[]{:S(2)}, u32[]{:S(2)}) collective-permute-start(bf16[200,256]{1,0:T(8,128)(2,1)S(1)} %collective-permute-done.5.refs_4_), channel_id=1, source_target_pairs={{0,1},{1,0},{2,3},{3,2},{4,5},{5,4},{6,7},{7,6},{8,9},{9,8},{10,11... | collective-permute-start | bytes 307208 | tf_op jit(solution)/shard_map/ppermute | solution.py:239
  35.0 5.9 %collective-permute-start.14 = (bf16[200,256]{1,0:T(8,128)(2,1)S(1)}, bf16[200,256]{1,0:T(8,128)(2,1)S(1)}, u32[]{:S(2)}, u32[]{:S(2)}) collective-permute-start(bf16[200,256]{1,0:T(8,128)(2,1)S(1)} %collective-permute-done.6.refs_5_), channel_id=1, source_target_pairs={{0,1},{1,0},{2,3},{3,2},{4,5},{5,4},{6,7},{7,6},{8,9},{9,8},{10,11... | collective-permute-start | bytes 307208 | tf_op jit(solution)/shard_map/ppermute | solution.py:239
  35.1 5.8 %collective-permute-start.16 = (bf16[200,256]{1,0:T(8,128)(2,1)S(1)}, bf16[200,256]{1,0:T(8,128)(2,1)S(1)}, u32[]{:S(2)}, u32[]{:S(2)}) collective-permute-start(bf16[200,256]{1,0:T(8,128)(2,1)S(1)} %collective-permute-done.8.refs_7_), channel_id=1, source_target_pairs={{0,1},{1,0},{2,3},{3,2},{4,5},{5,4},{6,7},{7,6},{8,9},{9,8},{10,11... | collective-permute-start | bytes 307208 | tf_op jit(solution)/shard_map/ppermute | solution.py:239
  35.8 5.1 %collective-permute-start.17 = (bf16[200,256]{1,0:T(8,128)(2,1)S(1)}, bf16[200,256]{1,0:T(8,128)(2,1)S(1)}, u32[]{:S(2)}, u32[]{:S(2)}) collective-permute-start(bf16[200,256]{1,0:T(8,128)(2,1)S(1)} %collective-permute-done.9.refs_8_), channel_id=1, source_target_pairs={{0,1},{1,0},{2,3},{3,2},{4,5},{5,4},{6,7},{7,6},{8,9},{9,8},{10,11... | collective-permute-start | bytes 307208 | tf_op jit(solution)/shard_map/ppermute | solution.py:239
  35.9 2.2 %copy-start = (bf16[256,8192]{1,0:T(8,128)(2,1)S(1)}, bf16[256,8192]{1,0:T(8,128)(2,1)}, u32[]{:S(2)}) copy-start(bf16[256,8192]{1,0:T(8,128)(2,1)} %w_ref.1) | copy-start | bytes 12582916
  40.3 15.4 %collective-permute-start.19 = (bf16[1024,128]{1,0:T(8,128)(2,1)S(1)}, bf16[1024,128]{1,0:T(8,128)(2,1)S(1)}, u32[]{:S(2)}, u32[]{:S(2)}) collective-permute-start(bf16[1024,128]{1,0:T(8,128)(2,1)S(1)} %pad_maximum_fusion.refs_17_), channel_id=1, source_target_pairs={{0,1},{1,0},{2,3},{3,2},{4,5},{5,4},{6,7},{7,6},{8,9},{9,8},{10,11... | collective-permute-start | bytes 786440 | tf_op jit(solution)/shard_map/ppermute | solution.py:239
  40.8 15.0 %collective-permute-start.20 = (bf16[1024,128]{1,0:T(8,128)(2,1)S(1)}, bf16[1024,128]{1,0:T(8,128)(2,1)S(1)}, u32[]{:S(2)}, u32[]{:S(2)}) collective-permute-start(bf16[1024,128]{1,0:T(8,128)(2,1)S(1)} %collective-permute-done.18.refs_18_), channel_id=1, source_target_pairs={{0,1},{1,0},{2,3},{3,2},{4,5},{5,4},{6,7},{7,6},{8,9},{9,8},{10,11... | collective-permute-start | bytes 786440 | tf_op jit(solution)/shard_map/ppermute | solution.py:239
  40.9 14.8 %copy-start.2 = (bf16[128,256]{1,0:T(8,128)(2,1)S(1)}, bf16[128,256]{1,0:T(8,128)(2,1)}, u32[]{:S(2)}) copy-start(bf16[128,256]{1,0:T(8,128)(2,1)} %refs_21_.1) | copy-start | bytes 196612
  55.4 3.2 %collective-permute-start.22 = (f32[256,512]{1,0:T(8,128)S(1)}, f32[256,512]{1,0:T(8,128)S(1)}, u32[]{:S(2)}, u32[]{:S(2)}) collective-permute-start(f32[256,512]{1,0:T(8,128)S(1)} %get-tuple-element.27), channel_id=1, source_target_pairs={{0,1},{1,0},{2,3},{3,2},{4,5},{5,4},{6,7},{7,6},{8,9},{9,8},{10,11... | collective-permute-start | bytes 1572872 | tf_op jit(solution)/shard_map/ppermute | solution.py:239
  58.4 1.4 %collective-permute-start.21 = (f32[136,256]{1,0:T(8,128)S(1)}, f32[136,256]{1,0:T(8,128)S(1)}, u32[]{:S(2)}, u32[]{:S(2)}) collective-permute-start(f32[136,256]{1,0:T(8,128)S(1)} %first.1), channel_id=1, source_target_pairs={{0,1},{1,0},{2,3},{3,2},{4,5},{5,4},{6,7},{7,6},{8,9},{9,8},{10,11... | collective-permute-start | bytes 417800 | tf_op jit(solution)/shard_map/ppermute | solution.py:239

commit v3 on v2

--- a/solution.py
+++ b/solution.py
@@ -9,42 +9,50 @@
 
 BF16 = jnp.bfloat16
 F32 = jnp.float32
-MAIN_VMEM = 36 << 20
-WEIGHTS_VMEM = 10 << 20
-X_AFTER = 5
+MAIN_VMEM = 50 << 20
+W_STEPS = 4
 
 
 def dot(a, b, dims):
     return lax.dot_general(a, b, ((dims[:1], dims[1:]), ((), ())), preferred_element_type=F32)
 
 
-def group_kernel(dest_ref, row_ref, col_ref, feats_ref, w_first_ref, panel_ref, piece_ref, *, rs, blk_dev, orbitals):
-    pre = dot(feats_ref[...], w_first_ref[...], (1, 0))
-    hidden = (pre * (0.5 * jnp.tanh(0.5 * pre) + 0.5)).astype(BF16)
-    pairs = feats_ref.shape[0]
+def pack_kernel(dest_ref, row_ref, col_ref, feats_ref, out_ref, *, rs, blk_dev):
+    pairs, f_width = feats_ref.shape
     dest = dest_ref[...]
-    gid = (dest % 2) * (2 * rs) + col_ref[...] * rs + (dest // 2) * blk_dev + row_ref[...]
+    gid = ((dest % 2) * (2 * rs) + col_ref[...] * rs + (dest // 2) * blk_dev + row_ref[...]).astype(F32)
+    out_ref[:pairs, :] = feats_ref[...]
+    at = lax.broadcasted_iota(jnp.int32, (8, f_width), 0)
+    label = jnp.zeros((8, f_width), F32)
+    for k in range(pairs // f_width):
+        label = jnp.where(at == k, gid[:, k * f_width : (k + 1) * f_width], label)
+    out_ref[pairs:, :] = label.astype(BF16)
+
+
+def unpack(pack_ref, k, pairs):
+    at = k * (pairs + 8)
+    f_width = pack_ref.shape[1]
+    label = pack_ref[at + pairs : at + pairs + 8, :].astype(F32)
+    label = jnp.concatenate([label[q : q + 1, :] for q in range(pairs // f_width)], axis=1)
+    return pack_ref[at : at + pairs, :], label
+
+
+def group_kernel(me_ref, *refs, rs, pairs, orbitals):
+    *pack_refs, w_first_ref, mine_ref, theirs_ref = refs
+    core = me_ref[0] % 2
     rows = lax.broadcasted_iota(jnp.int32, (4 * rs, pairs), 0)
-    pick = (rows == gid).astype(F32).astype(BF16)
-    panel_end = 4 * rs + panel_ref.shape[0]
-    piece_ref[: 4 * rs, :] = (dot(pick, hidden, (1, 0)) * (1.0 / orbitals)).astype(BF16)
-    piece_ref[4 * rs : panel_end, :] = panel_ref[...]
-    piece_ref[panel_end:, :] = jnp.broadcast_to(gid.astype(F32), (8, pairs)).astype(BF16)
-
-
-def weights_kernel(w_ref, out_ref, sems):
-    chunks = sems.shape[0]
-    width = w_ref.shape[1] // chunks
-    copies = []
-    for k in range(chunks):
-        cols = slice(k * width, (k + 1) * width)
-        copies.append(pltpu.make_async_copy(w_ref.at[:, cols], out_ref.at[0, :, cols], sems.at[k]))
-        copies[-1].start()
-    for k in range(chunks):
-        copies[k].wait()
-        for q in range(k * width // 128, (k + 1) * width // 128):
-            cols = slice(q * 128, (q + 1) * 128)
-            out_ref[1, :, cols] = pltpu.roll(out_ref[0, :, cols].astype(F32), 64, 1).astype(BF16)
+    rows = ((rows + core * (2 * rs)) % (4 * rs)).astype(F32)
+    to = 0
+    for pack_ref in pack_refs:
+        for k in range(pack_ref.shape[0] // (pairs + 8)):
+            feats, label = unpack(pack_ref, k, pairs)
+            pre = dot(feats, w_first_ref[...], (1, 0))
+            hidden = (pre * (0.5 * jnp.tanh(0.5 * pre) + 0.5)).astype(BF16)
+            pick = (rows == label).astype(F32).astype(BF16)
+            sums = (dot(pick, hidden, (1, 0)) * (1.0 / orbitals)).astype(BF16)
+            mine_ref[to : to + 2 * rs, :] = sums[: 2 * rs, :]
+            theirs_ref[to : to + 2 * rs, :] = sums[2 * rs :, :]
+            to += 2 * rs
 
 
 def source_chip(m, chip, chips, z_count):
@@ -53,10 +61,16 @@
 
 
 def main_kernel(*refs, chips, z_count, rows_split, half_cols, orbitals):
-    me_ref, same_refs, other_refs = refs[0], refs[1 : 1 + chips], refs[1 + chips : 1 + 2 * chips]
-    (w_ref, energies_ref, res_ref, keep_ref, send_ref, dh_ref, square_ref, h_ref, c_ref, x_ref, r_ref, g_ref, l_ref) = refs[
-        1 + 2 * chips :
-    ]
+    me_ref, h_refs, p_refs, w_hbm = refs[0], refs[1:3], refs[3:7], refs[7]
+    energies_ref, res_ref, keep_ref, send_ref, dh_ref, square_ref = refs[8:14]
+    w_ref, w_sems, h_ref, c_ref, x_ref, r_ref, g_ref, l_ref = refs[14:]
+    w_steps = w_sems.shape[0]
+    step_cols = w_ref.shape[2] // w_steps
+    w_copies = []
+    for i in range(w_steps):
+        cols = slice(i * step_cols, (i + 1) * step_cols)
+        w_copies.append(pltpu.make_async_copy(w_hbm.at[:, cols], w_ref.at[0, :, cols], w_sems.at[i]))
+        w_copies[i].start()
     me = me_ref[0]
     core = me % 2
     chip = me // 2
@@ -75,16 +89,24 @@
         c_ref[1, pl.ds(at, 64), :] = block[64:, :]
         c_ref[1, pl.ds(at + 64, 64), :] = block[:64, :]
 
+    x_count = chips // z_count
     for m in range(chips):
         src = source_chip(m, chip, chips, z_count)
-        for piece, lister in ((same_refs[m], 2 * src + core), (other_refs[m], 2 * src + 1 - core)):
-            place(lister, piece[4 * rs : 4 * rs + 128, :])
+        dz, dx = m // x_count, m % x_count
+        for which, lister in ((0, 2 * src + core), (1, 2 * src + 1 - core)):
+            place(lister, p_refs[2 * which + dx][dz * 128 : (dz + 1) * 128, :])
             at = pl.multiple_of(lister * rs, rs)
             for pc in range(2):
-                h_ref[pc, pl.ds(at, rs), :] = piece[pl.ds(pl.multiple_of(core * 2 * rs, rs) + pc * rs, rs), :]
+                lo = (dx * z_count + dz) * 2 * rs + pc * rs
+                h_ref[pc, pl.ds(at, rs), :] = h_refs[which][lo : lo + rs, :]
+
+    for i in range(w_steps):
+        w_copies[i].wait()
+        for k in range(i * step_cols // 128, (i + 1) * step_cols // 128):
+            cols = slice(k * 128, (k + 1) * 128)
+            w_ref[1, :, cols] = pltpu.roll(w_ref[0, :, cols].astype(F32), 64, 1).astype(BF16)
 
     h0, h1 = h_ref[0], h_ref[1]
-    step_cols = 2048
     steps = half // step_cols
     per = step_cols // 128
 
@@ -169,9 +191,8 @@
 
 
 def first_kernel(*refs, chips, z_count, rs, pairs):
-    me_ref, same_refs, other_refs = refs[0], refs[1 : 1 + chips], refs[1 + chips : 1 + 2 * chips]
-    feat_refs = refs[1 + 2 * chips : 5 + 2 * chips]
-    w_first_ref, dh_ref, square_ref, first_ref, f_ref, d_ref = refs[5 + 2 * chips :]
+    me_ref, pack_refs = refs[0], refs[1:5]
+    w_first_ref, dh_ref, square_ref, first_ref, f_ref, d_ref = refs[5:]
     me = me_ref[0]
     core, chip = me % 2, me // 2
     f_width = w_first_ref.shape[0]
@@ -180,9 +201,8 @@
     for m in range(chips):
         src = source_chip(m, chip, chips, z_count)
         dz, dx = m // x_count, m % x_count
-        for which, (piece, lister) in enumerate(((same_refs[m], 2 * src + core), (other_refs[m], 2 * src + 1 - core))):
-            feats = feat_refs[2 * which + dx][dz * pairs : (dz + 1) * pairs, :]
-            label = piece[piece.shape[0] - 8 :, :].astype(F32)[:1, :]
+        for which, lister in ((0, 2 * src + core), (1, 2 * src + 1 - core)):
+            feats, label = unpack(pack_refs[2 * which + dx], dz, pairs)
             pre = dot(feats, w_first_ref[...], (1, 0))
             sig = 0.5 * jnp.tanh(0.5 * pre) + 0.5
             at = pl.multiple_of(lister * rs, rs)
@@ -199,6 +219,14 @@
     first_ref[f_width:, :] = square_ref[...]
 
 
+def combine_kernel(keep_ref, sent_ref, first_ref, got_ref, second_ref, grad_ref, loss_ref, *, count):
+    second_ref[...] = keep_ref[...] + sent_ref[...]
+    f_width = grad_ref.shape[0]
+    grad_ref[...] = first_ref[:f_width, :] + got_ref[:f_width, :]
+    square = first_ref[f_width:, :] + got_ref[f_width:, :]
+    loss_ref[...] = jnp.sum(jnp.sum(square, axis=0, keepdims=True), axis=1, keepdims=True) / count
+
+
 def near(features, w_first, w_second, panel, energies, pair_dest, pair_row, pair_col, z_count):
     n_dev = lax.axis_size("blk")
     me = lax.axis_index("blk").reshape(1).astype(jnp.int32)
@@ -208,32 +236,8 @@
     chips, rs = n_dev // 2, n_dev * blk_dev // 2
     half_cols = flat // n_dev
     smem, vmem = pl.BlockSpec(memory_space=pltpu.SMEM), pl.BlockSpec(memory_space=pltpu.VMEM)
-
-    def to_x(v):
-        return from_chip(v, 1)
-
-    piece = pl.pallas_call(
-        functools.partial(group_kernel, rs=rs, blk_dev=blk_dev, orbitals=orbitals),
-        out_shape=jax.ShapeDtypeStruct((4 * rs + blk_dev * orbitals + 8, hid), BF16),
-        cost_estimate=pl.CostEstimate(flops=1 << 28, transcendentals=0, bytes_accessed=1 << 20),
-        name="group",
-    )(
-        pair_dest.reshape(1, pairs),
-        pair_row.reshape(1, pairs),
-        pair_col.reshape(1, pairs),
-        features,
-        w_first,
-        panel.reshape(blk_dev * orbitals, columns),
-    )
-    weights = pl.pallas_call(
-        weights_kernel,
-        out_shape=jax.ShapeDtypeStruct((2, hid, flat), BF16),
-        in_specs=[pl.BlockSpec(memory_space=pl.ANY)],
-        scratch_shapes=[pltpu.SemaphoreType.DMA((8,))],
-        compiler_params=pltpu.CompilerParams(vmem_limit_bytes=WEIGHTS_VMEM),
-        cost_estimate=pl.CostEstimate(flops=0, transcendentals=0, bytes_accessed=8 * hid * flat),
-        name="weights",
-    )(w_second)
+    anywhere = pl.BlockSpec(memory_space=pl.ANY)
+    x_count = chips // z_count
 
     def to_core(v):
         return lax.ppermute(v, "blk", [(i, i ^ 1) for i in range(n_dev)])
@@ -242,14 +246,30 @@
         sends = [(2 * source_chip(m, q, chips, z_count) + c, 2 * q + c) for q in range(chips) for c in range(2)]
         return lax.ppermute(v, "blk", sends) if m else v
 
-    x_count = chips // z_count
-    parts = [from_chip(features, dz * x_count) for dz in range(z_count)]
-    piece, *parts = lax.optimization_barrier((piece, *parts))
-    same = [from_chip(piece, m) for m in range(chips)]
-    feats_mine, same[X_AFTER] = lax.optimization_barrier((jnp.concatenate(parts, axis=0), same[X_AFTER]))
-    feats = [feats_mine, to_x(feats_mine)]
-    other = [to_core(v) for v in same]
-    feats += [to_core(v) for v in feats]
+    def along_z(v):
+        return jnp.concatenate([from_chip(v, dz * x_count) for dz in range(z_count)], axis=0)
+
+    pack = pl.pallas_call(
+        functools.partial(pack_kernel, rs=rs, blk_dev=blk_dev),
+        out_shape=jax.ShapeDtypeStruct((pairs + 8, f_width), BF16),
+        cost_estimate=pl.CostEstimate(flops=0, transcendentals=0, bytes_accessed=1 << 20),
+        name="pack",
+    )(pair_dest.reshape(1, pairs), pair_row.reshape(1, pairs), pair_col.reshape(1, pairs), features)
+    packs_z = along_z(pack)
+    packs = [packs_z, from_chip(packs_z, 1)]
+    panels_z = along_z(panel.reshape(blk_dev * orbitals, columns))
+    panels = [panels_z, from_chip(panels_z, 1)]
+    h_mine, h_theirs = pl.pallas_call(
+        functools.partial(group_kernel, rs=rs, pairs=pairs, orbitals=orbitals),
+        out_shape=(jax.ShapeDtypeStruct((2 * rs * chips, hid), BF16),) * 2,
+        in_specs=[smem] + [vmem] * 3,
+        compiler_params=pltpu.CompilerParams(vmem_limit_bytes=12 << 20),
+        cost_estimate=pl.CostEstimate(flops=1 << 30, transcendentals=0, bytes_accessed=1 << 21),
+        name="group",
+    )(me, *packs, w_first)
+    h_other = to_core(h_theirs)
+    panels += [to_core(v) for v in panels]
+    packs += [to_core(v) for v in packs]
 
     listers = n_dev
     k_width = listers * 128
@@ -265,8 +285,10 @@
             jax.ShapeDtypeStruct((2, listers * rs, hid), F32),
             jax.ShapeDtypeStruct((8, columns), F32),
         ),
-        in_specs=[smem] + [vmem] * (2 * chips + 2),
+        in_specs=[smem] + [vmem] * 6 + [anywhere, vmem],
         scratch_shapes=[
+            pltpu.VMEM((2, hid, flat), BF16),
+            pltpu.SemaphoreType.DMA((W_STEPS,)),
             pltpu.VMEM((2, listers * rs, hid), BF16),
             pltpu.VMEM((2, k_width, columns), BF16),
             pltpu.VMEM((2, 2 * n_rows, k_width), BF16),
@@ -277,21 +299,29 @@
         compiler_params=pltpu.CompilerParams(vmem_limit_bytes=MAIN_VMEM),
         cost_estimate=pl.CostEstimate(flops=16 * listers * rs * hid * flat, transcendentals=0, bytes_accessed=1 << 24),
         name="step",
-    )(me, *same, *other, weights, energies.reshape(1, columns))
+    )(me, h_mine, h_other, *panels, w_second, energies.reshape(1, columns))
     send = to_core(send)
     first = pl.pallas_call(
         functools.partial(first_kernel, chips=chips, z_count=z_count, rs=rs, pairs=pairs),
         out_shape=jax.ShapeDtypeStruct((f_width + 8, hid), F32),
-        in_specs=[smem] + [vmem] * (2 * chips + 7),
+        in_specs=[smem] + [vmem] * 7,
         scratch_shapes=[pltpu.VMEM((n_dev * pairs, f_width), BF16), pltpu.VMEM((n_dev * pairs, hid), BF16)],
         compiler_params=pltpu.CompilerParams(vmem_limit_bytes=12 << 20),
         cost_estimate=pl.CostEstimate(flops=1 << 31, transcendentals=0, bytes_accessed=1 << 22),
         name="first",
-    )(me, *same, *other, *feats, w_first, d_hidden, square)
-    grad_second = keep + send
-    first = first + to_core(first)
-    loss = (jnp.sum(first[f_width:]) / (n_dev * blk_dev * orbitals * columns)).reshape(1)
-    return (res, loss, first[:f_width], grad_second)
+    )(me, *packs, w_first, d_hidden, square)
+    count = n_dev * blk_dev * orbitals * columns
+    grad_second, grad_first, loss = pl.pallas_call(
+        functools.partial(combine_kernel, count=count),
+        out_shape=(
+            jax.ShapeDtypeStruct((hid, half_cols), F32),
+            jax.ShapeDtypeStruct((f_width, hid), F32),
+            jax.ShapeDtypeStruct((1, 1), F32),
+        ),
+        compiler_params=pltpu.CompilerParams(vmem_limit_bytes=12 << 20),
+        name="combine",
+    )(keep, send, first, to_core(first))
+    return (res, loss.reshape(1), grad_first, grad_second)
 
 
 def predict(feats, w_first, w_second, orbitals):

time: 63.1 us -> 52.9 us (0.84)
  starting transfers between devices: 19.6 us -> 15.2 us
  waiting for transfers between devices: 14.4 us -> 10.2 us
  Pallas kernels: 21.1 us -> 23.8 us
  local copies, waits for them, and re-layouts: 2.87 us -> 0.85 us
  between operations: 2.51 us -> 0.7 us
    ppermute x11 -> x8, waiting for transfers between devices: 13.7 us -> 8.48 us  [from_chip(): return lax.ppermute(v, 'blk', sends) if m else v]
    ppermute x11 -> x8, starting transfers between devices: 16.8 us -> 14 us  [from_chip(): return lax.ppermute(v, 'blk', sends) if m else v]
    pallas_call x1, Pallas kernels: 14.5 us -> 17 us  [near(): pl.pallas_call(functools.partial(main_kernel, chips=chips, z_count=z_coun...]
    ppermute x12 -> x7, starting transfers between devices: 2.84 us -> 1.29 us  [to_core(): return lax.ppermute(v, 'blk', [(i, i ^ 1) for i in range(n_dev)])]
    unnamed x8 -> x6, local copies, waits for them, and re-layouts: 2.2 us -> 0.85 us
    ppermute x12 -> x7, waiting for transfers between devices: 0.63 us -> 1.77 us  [to_core(): return lax.ppermute(v, 'blk', [(i, i ^ 1) for i in range(n_dev)])]
    concatenate x1 -> x2, other arithmetic: 0.86 us -> 1.76 us  [along_z(): jnp.concatenate([from_chip(v, dz * x_count) for dz in range(z_count)], ax...]
    add x2 -> x0, other arithmetic: 0.89 us -> none  [the longest x1 0.87 us: near(): grad_second = keep + send]
  transfers between devices with their start and end apart: 23 -> 15, of which waited for: 7 -> 6; matrix products, arithmetic and copies ran while one was open for 3% -> 3% of each run, Pallas kernels for 34% -> 44%
where the time goes in v3:
time: 52.9 us; the launch traced here: 52.6 us
  Pallas kernels  23.8 us (45%)
  starting transfers between devices  15.2 us (29%)
  waiting for transfers between devices  10.2 us (19%)
  other arithmetic  1.76 us (3%)
  local copies, waits for them, and re-layouts  0.85 us (2%)
  between operations  0.7 us (1%)
    pallas_call x1, Pallas kernels, near(): pl.pallas_call(functools.partial(main_kernel, chips=chips, z_count=z_coun...  17 us
    ppermute x8, starting transfers between devices, from_chip(): return lax.ppermute(v, 'blk', sends) if m else v  14 us
    ppermute x8, waiting for transfers between devices, from_chip(): return lax.ppermute(v, 'blk', sends) if m else v  8.48 us
    pallas_call x1, Pallas kernels, near(): pl.pallas_call(functools.partial(first_kernel, chips=chips, z_count=z_cou...  2.56 us
    pallas_call x1, Pallas kernels, near(): pl.pallas_call(functools.partial(group_kernel, rs=rs, pairs=pairs, orbita...  1.81 us
    ppermute x7, waiting for transfers between devices, to_core(): return lax.ppermute(v, 'blk', [(i, i ^ 1) for i in range(n_dev)])  1.77 us
    concatenate x2, other arithmetic, along_z(): jnp.concatenate([from_chip(v, dz * x_count) for dz in range(z_count)], ax...  1.76 us
    pallas_call x1, Pallas kernels, near(): pl.pallas_call(functools.partial(pack_kernel, rs=rs, blk_dev=blk_dev), ou...  1.54 us
  transfers between devices with their start and end apart: 15, of which 6 were waited for; matrix products, arithmetic and copies ran while one was open for 3% of the time, Pallas kernels for 44%

profile of v3, /device:TPU:0, one launch (start us, length us, event | category | flops | bytes accessed | tf_op | source)
XLA Modules:
  0.0 52.6 jit_solution(6606811534816125249)
XLA Ops:
  0.6 3.1 %collective-permute-start.5 = (bf16[128,256]{1,0:T(8,128)(2,1)}, bf16[128,256]{1,0:T(8,128)(2,1)S(1)}, u32[]{:S(2)}, u32[]{:S(2)}) collective-permute-start(bf16[128,256]{1,0:T(8,128)(2,1)} %bitcast.8), channel_id=1, source_target_pairs={{12,0},{13,1},{14,2},{15,3},{0,4},{1,5},{2,6},{3,7},{4,8},{5,9},{6... | collective-permute-start | bytes 196616 | tf_op jit(solution)/shard_map/ppermute | solution.py:247
  3.7 2.6 %collective-permute-start.6 = (bf16[128,256]{1,0:T(8,128)(2,1)}, bf16[128,256]{1,0:T(8,128)(2,1)S(1)}, u32[]{:S(2)}, u32[]{:S(2)}) collective-permute-start(bf16[128,256]{1,0:T(8,128)(2,1)} %bitcast.9), channel_id=1, source_target_pairs={{8,0},{9,1},{10,2},{11,3},{12,4},{13,5},{14,6},{15,7},{0,8},{1,9},... | collective-permute-start | bytes 196616 | tf_op jit(solution)/shard_map/ppermute | solution.py:247
  6.3 1.3 %collective-permute-start.7 = (bf16[128,256]{1,0:T(8,128)(2,1)}, bf16[128,256]{1,0:T(8,128)(2,1)S(1)}, u32[]{:S(2)}, u32[]{:S(2)}) collective-permute-start(bf16[128,256]{1,0:T(8,128)(2,1)} %bitcast.10), channel_id=1, source_target_pairs={{4,0},{5,1},{6,2},{7,3},{8,4},{9,5},{10,6},{11,7},{12,8},{13,9},{1... | collective-permute-start | bytes 196616 | tf_op jit(solution)/shard_map/ppermute | solution.py:247
  7.7 1.5 %pack.1 = bf16[264,128]{1,0:T(8,128)(2,1)} custom-call(s32[1,256]{1,0:T(1,128)} %bitcast.12, s32[1,256]{1,0:T(1,128)} %bitcast.13, s32[1,256]{1,0:T(1,128)} %bitcast.14, bf16[256,128]{1,0:T(8,128)(2,1)} %feats_ref.1), custom_call_target="tpu_custom_call" | custom-call | bytes 1048576 | tf_op jit(solution)/shard_map/pack/pallas_call | solution.py:252
  9.2 0.7 %collective-permute-start = (bf16[264,128]{1,0:T(8,128)(2,1)}, bf16[264,128]{1,0:T(8,128)(2,1)S(1)}, u32[]{:S(2)}, u32[]{:S(2)}) collective-permute-start(bf16[264,128]{1,0:T(8,128)(2,1)} %pack.1), channel_id=1, source_target_pairs={{12,0},{13,1},{14,2},{15,3},{0,4},{1,5},{2,6},{3,7},{4,8},{5,9},{6... | collective-permute-start | bytes 202760 | tf_op jit(solution)/shard_map/ppermute | solution.py:247
  9.9 0.3 collective-permute-start.1
  10.2 0.0 collective-permute-done.5
  10.2 2.8 %collective-permute-start.2 = (bf16[264,128]{1,0:T(8,128)(2,1)}, bf16[264,128]{1,0:T(8,128)(2,1)S(1)}, u32[]{:S(2)}, u32[]{:S(2)}) collective-permute-start(bf16[264,128]{1,0:T(8,128)(2,1)} %pack.1), channel_id=1, source_target_pairs={{4,0},{5,1},{6,2},{7,3},{8,4},{9,5},{10,6},{11,7},{12,8},{13,9},{1... | collective-permute-start | bytes 202760 | tf_op jit(solution)/shard_map/ppermute | solution.py:247
  13.0 0.0 collective-permute-done.6
  13.0 0.0 collective-permute-done.7
  13.0 0.9 %pad_maximum_fusion.1.refs_3_ = bf16[512,256]{1,0:T(8,128)(2,1)S(1)} fusion(bf16[128,256]{1,0:T(8,128)(2,1)S(1)} %collective-permute-done.7, bf16[128,256]{1,0:T(8,128)(2,1)S(1)} %collective-permute-done.6, bf16[128,256]{1,0:T(8,128)(2,1)S(1)} %collective-permute-done.5, bf16[128,256]{1,0:T(8,128)(2,1)} %bitcast.11), kind=kLoop, calls=%fused_computation.1 | loop fusion | flops 1048576 | bytes 524288 | tf_op jit(solution)/shard_map/concatenate | solution.py:250
  13.9 1.6 %collective-permute-start.8 = (bf16[512,256]{1,0:T(8,128)(2,1)S(1)}, bf16[512,256]{1,0:T(8,128)(2,1)S(1)}, u32[]{:S(2)}, u32[]{:S(2)}) collective-permute-start(bf16[512,256]{1,0:T(8,128)(2,1)S(1)} %pad_maximum_fusion.1.refs_3_), channel_id=1, source_target_pairs={{2,0},{3,1},{0,2},{1,3},{6,4},{7,5},{4,6},{5,7},{10,8},{11,9},{8,1... | collective-permute-start | bytes 786440 | tf_op jit(solution)/shard_map/ppermute | solution.py:247
  15.5 0.4 collective-permute-done
  15.9 1.5 %collective-permute-done.1 = bf16[264,128]{1,0:T(8,128)(2,1)S(1)} collective-permute-done((bf16[264,128]{1,0:T(8,128)(2,1)}, bf16[264,128]{1,0:T(8,128)(2,1)S(1)}, u32[]{:S(2)}, u32[]{:S(2)}) %collective-permute-start.1) | collective-permute-done | bytes 67616 | tf_op jit(solution)/shard_map/ppermute | solution.py:247
  17.4 0.0 collective-permute-done.2
  17.4 0.9 %pad_maximum_fusion.refs_0_.refs_1_ = bf16[1056,128]{1,0:T(8,128)(2,1)S(1)} fusion(bf16[264,128]{1,0:T(8,128)(2,1)S(1)} %collective-permute-done.2, bf16[264,128]{1,0:T(8,128)(2,1)S(1)} %collective-permute-done.1, bf16[264,128]{1,0:T(8,128)(2,1)S(1)} %collective-permute-done, bf16[264,128]{1,0:T(8,128)(2,1)} %pack.1), kind=kLoop, calls=%fused_computation | loop fusion | flops 1081344 | bytes 540672 | tf_op jit(solution)/shard_map/concatenate | solution.py:250
  18.3 1.6 %collective-permute-start.3 = (bf16[1056,128]{1,0:T(8,128)(2,1)S(1)}, bf16[1056,128]{1,0:T(8,128)(2,1)S(1)}, u32[]{:S(2)}, u32[]{:S(2)}) collective-permute-start(bf16[1056,128]{1,0:T(8,128)(2,1)S(1)} %pad_maximum_fusion.refs_0_.refs_1_), channel_id=1, source_target_pairs={{2,0},{3,1},{0,2},{1,3},{6,4},{7,5},{4,6},{5,7},{10,8},{11,9},{8,1... | collective-permute-start | bytes 811016 | tf_op jit(solution)/shard_map/ppermute | solution.py:247
  19.8 0.0 collective-permute-start.9
  19.8 3.4 %collective-permute-done.8.refs_4_ = bf16[512,256]{1,0:T(8,128)(2,1)S(1)} collective-permute-done((bf16[512,256]{1,0:T(8,128)(2,1)S(1)}, bf16[512,256]{1,0:T(8,128)(2,1)S(1)}, u32[]{:S(2)}, u32[]{:S(2)}) %collective-permute-start.8) | collective-permute-done | bytes 262176 | tf_op jit(solution)/shard_map/ppermute | solution.py:247
  23.2 3.2 %collective-permute-done.3.refs_1_.refs_2_ = bf16[1056,128]{1,0:T(8,128)(2,1)S(1)} collective-permute-done((bf16[1056,128]{1,0:T(8,128)(2,1)S(1)}, bf16[1056,128]{1,0:T(8,128)(2,1)S(1)}, u32[]{:S(2)}, u32[]{:S(2)}) %collective-permute-start.3) | collective-permute-done | bytes 270368 | tf_op jit(solution)/shard_map/ppermute | solution.py:247
  26.4 0.8 %copy-done = bf16[128,256]{1,0:T(8,128)(2,1)S(1)} copy-done((bf16[128,256]{1,0:T(8,128)(2,1)S(1)}, bf16[128,256]{1,0:T(8,128)(2,1)}, u32[]{:S(2)}) %copy-start) | copy-done | bytes 65560
  27.2 1.8 %group.1 = (bf16[256,256]{1,0:T(8,128)(2,1)S(1)}, bf16[256,256]{1,0:T(8,128)(2,1)S(1)}) custom-call(s32[1]{0:T(128)} %bitcast.me_ref.refs_0_, bf16[1056,128]{1,0:T(8,128)(2,1)S(1)} %pad_maximum_fusion.refs_0_.refs_1_, bf16[1056,128]{1,0:T(8,128)(2,1)S(1)} %collective-permute-done.3.refs_1_.refs_2_, bf16[128,256]{1,0:T(8,128)(2,1)S(1)} %copy-done), custom_call_target="tpu_custom_call" | custom-call | flops 1073741824 | bytes 2097152 | tf_op jit(solution)/shard_map/group/pallas_call | solution.py:262
  29.1 0.1 collective-permute-start.4
  29.1 0.5 collective-permute-start.12
  29.6 0.1 collective-permute-start.13
  29.7 0.8 %collective-permute-done.4.refs_2_ = bf16[256,256]{1,0:T(8,128)(2,1)S(1)} collective-permute-done((bf16[256,256]{1,0:T(8,128)(2,1)S(1)}, bf16[256,256]{1,0:T(8,128)(2,1)S(1)}, u32[]{:S(2)}, u32[]{:S(2)}) %collective-permute-start.4) | collective-permute-done | bytes 131104 | tf_op jit(solution)/shard_map/ppermute | solution.py:243
  30.5 17.0 %step.1 = (f32[2,64,256]{2,1,0:T(8,128)}, f32[256,512]{1,0:T(8,128)S(1)}, f32[256,512]{1,0:T(8,128)S(1)}, f32[2,256,256]{2,1,0:T(8,128)S(1)}, f32[8,256]{1,0:T(8,128)S(1)}) custom-call(s32[1]{0:T(128)} %bitcast.me_ref.refs_0_, bf16[256,256]{1,0:T(8,128)(2,1)S(1)} %get-tuple-element.14.refs_1_, bf16[256,256]{1,0:T(8,128)(2,1)S(1)} %collective-permute-done.4.refs_2_, ...), custom_call_target="tpu_custom_call" | custom-call | flops 8589934592 | bytes 16777216 | tf_op jit(solution)/shard_map/step/pallas_call | solution.py:277
  47.5 0.2 collective-permute-start.11
  47.7 2.6 %first.1.first_ref = f32[136,256]{1,0:T(8,128)S(1)} custom-call(s32[1]{0:T(128)} %bitcast.me_ref.refs_0_, bf16[1056,128]{1,0:T(8,128)(2,1)S(1)} %pad_maximum_fusion.refs_0_.refs_1_, bf16[1056,128]{1,0:T(8,128)(2,1)S(1)} %collective-permute-done.3.refs_1_.refs_2_, bf16[1056,128]{1,0:T(8,128)(2,1)S(1)} %collective-permute-done.12.refs_3_, ...), custom_call_target="tpu_custom_call" | custom-call | flops 2147483648 | bytes 4194304 | tf_op jit(solution)/shard_map/first/pallas_call | solution.py:304
  50.3 0.4 collective-permute-start.14
  50.7 1.0 %collective-permute-done.14.got_ref = f32[136,256]{1,0:T(8,128)S(1)} collective-permute-done((f32[136,256]{1,0:T(8,128)S(1)}, f32[136,256]{1,0:T(8,128)S(1)}, u32[]{:S(2)}, u32[]{:S(2)}) %collective-permute-start.14) | collective-permute-done | bytes 139296 | tf_op jit(solution)/shard_map/ppermute | solution.py:243
  51.7 0.9 %combine.1 = (f32[256,512]{1,0:T(8,128)}, f32[128,256]{1,0:T(8,128)}, f32[1,1]{1,0:T(1,128)}) custom-call(f32[256,512]{1,0:T(8,128)S(1)} %get-tuple-element.17.keep_ref, f32[256,512]{1,0:T(8,128)S(1)} %collective-permute-done.11.sent_ref, f32[136,256]{1,0:T(8,128)S(1)} %first.1.first_ref, f32[136,256]{1,0:T(8,128)S(1)} %collective-permute-done.14.got_ref), custom_call_target="tpu_custom_call" | custom-call | tf_op jit(solution)/shard_map/combine/pallas_call | solution.py:314
  (11 shorter events, 0.0 us)
Async XLA Ops:
  0.6 29.8 %copy-start.2 = (f32[256]{0:T(256)S(1)}, f32[256]{0:T(256)}, u32[]{:S(2)}) copy-start(f32[256]{0:T(256)} %param.12) | copy-start | bytes 3076
  0.6 9.6 %collective-permute-start.5 = (bf16[128,256]{1,0:T(8,128)(2,1)}, bf16[128,256]{1,0:T(8,128)(2,1)S(1)}, u32[]{:S(2)}, u32[]{:S(2)}) collective-permute-start(bf16[128,256]{1,0:T(8,128)(2,1)} %bitcast.8), channel_id=1, source_target_pairs={{12,0},{13,1},{14,2},{15,3},{0,4},{1,5},{2,6},{3,7},{4,8},{5,9},{6... | collective-permute-start | bytes 196616 | tf_op jit(solution)/shard_map/ppermute | solution.py:247
  3.7 9.3 %collective-permute-start.6 = (bf16[128,256]{1,0:T(8,128)(2,1)}, bf16[128,256]{1,0:T(8,128)(2,1)S(1)}, u32[]{:S(2)}, u32[]{:S(2)}) collective-permute-start(bf16[128,256]{1,0:T(8,128)(2,1)} %bitcast.9), channel_id=1, source_target_pairs={{8,0},{9,1},{10,2},{11,3},{12,4},{13,5},{14,6},{15,7},{0,8},{1,9},... | collective-permute-start | bytes 196616 | tf_op jit(solution)/shard_map/ppermute | solution.py:247
  6.3 6.7 %collective-permute-start.7 = (bf16[128,256]{1,0:T(8,128)(2,1)}, bf16[128,256]{1,0:T(8,128)(2,1)S(1)}, u32[]{:S(2)}, u32[]{:S(2)}) collective-permute-start(bf16[128,256]{1,0:T(8,128)(2,1)} %bitcast.10), channel_id=1, source_target_pairs={{4,0},{5,1},{6,2},{7,3},{8,4},{9,5},{10,6},{11,7},{12,8},{13,9},{1... | collective-permute-start | bytes 196616 | tf_op jit(solution)/shard_map/ppermute | solution.py:247
  9.2 6.7 %collective-permute-start = (bf16[264,128]{1,0:T(8,128)(2,1)}, bf16[264,128]{1,0:T(8,128)(2,1)S(1)}, u32[]{:S(2)}, u32[]{:S(2)}) collective-permute-start(bf16[264,128]{1,0:T(8,128)(2,1)} %pack.1), channel_id=1, source_target_pairs={{12,0},{13,1},{14,2},{15,3},{0,4},{1,5},{2,6},{3,7},{4,8},{5,9},{6... | collective-permute-start | bytes 202760 | tf_op jit(solution)/shard_map/ppermute | solution.py:247
  9.9 7.5 %collective-permute-start.1 = (bf16[264,128]{1,0:T(8,128)(2,1)}, bf16[264,128]{1,0:T(8,128)(2,1)S(1)}, u32[]{:S(2)}, u32[]{:S(2)}) collective-permute-start(bf16[264,128]{1,0:T(8,128)(2,1)} %pack.1), channel_id=1, source_target_pairs={{8,0},{9,1},{10,2},{11,3},{12,4},{13,5},{14,6},{15,7},{0,8},{1,9},... | collective-permute-start | bytes 202760 | tf_op jit(solution)/shard_map/ppermute | solution.py:247
  10.2 7.2 %collective-permute-start.2 = (bf16[264,128]{1,0:T(8,128)(2,1)}, bf16[264,128]{1,0:T(8,128)(2,1)S(1)}, u32[]{:S(2)}, u32[]{:S(2)}) collective-permute-start(bf16[264,128]{1,0:T(8,128)(2,1)} %pack.1), channel_id=1, source_target_pairs={{4,0},{5,1},{6,2},{7,3},{8,4},{9,5},{10,6},{11,7},{12,8},{13,9},{1... | collective-permute-start | bytes 202760 | tf_op jit(solution)/shard_map/ppermute | solution.py:247
  13.9 9.3 %collective-permute-start.8 = (bf16[512,256]{1,0:T(8,128)(2,1)S(1)}, bf16[512,256]{1,0:T(8,128)(2,1)S(1)}, u32[]{:S(2)}, u32[]{:S(2)}) collective-permute-start(bf16[512,256]{1,0:T(8,128)(2,1)S(1)} %pad_maximum_fusion.1.refs_3_), channel_id=1, source_target_pairs={{2,0},{3,1},{0,2},{1,3},{6,4},{7,5},{4,6},{5,7},{10,8},{11,9},{8,1... | collective-permute-start | bytes 786440 | tf_op jit(solution)/shard_map/ppermute | solution.py:247
  18.3 8.1 %collective-permute-start.3 = (bf16[1056,128]{1,0:T(8,128)(2,1)S(1)}, bf16[1056,128]{1,0:T(8,128)(2,1)S(1)}, u32[]{:S(2)}, u32[]{:S(2)}) collective-permute-start(bf16[1056,128]{1,0:T(8,128)(2,1)S(1)} %pad_maximum_fusion.refs_0_.refs_1_), channel_id=1, source_target_pairs={{2,0},{3,1},{0,2},{1,3},{6,4},{7,5},{4,6},{5,7},{10,8},{11,9},{8,1... | collective-permute-start | bytes 811016 | tf_op jit(solution)/shard_map/ppermute | solution.py:247
  19.8 9.9 %collective-permute-start.9 = (bf16[512,256]{1,0:T(8,128)(2,1)S(1)}, bf16[512,256]{1,0:T(8,128)(2,1)S(1)}, u32[]{:S(2)}, u32[]{:S(2)}) collective-permute-start(bf16[512,256]{1,0:T(8,128)(2,1)S(1)} %pad_maximum_fusion.1.refs_3_), channel_id=1, source_target_pairs={{0,1},{1,0},{2,3},{3,2},{4,5},{5,4},{6,7},{7,6},{8,9},{9,8},{10,11... | collective-permute-start | bytes 786440 | tf_op jit(solution)/shard_map/ppermute | solution.py:243
  23.2 7.3 %collective-permute-start.10 = (bf16[512,256]{1,0:T(8,128)(2,1)S(1)}, bf16[512,256]{1,0:T(8,128)(2,1)S(1)}, u32[]{:S(2)}, u32[]{:S(2)}) collective-permute-start(bf16[512,256]{1,0:T(8,128)(2,1)S(1)} %collective-permute-done.8.refs_4_), channel_id=1, source_target_pairs={{0,1},{1,0},{2,3},{3,2},{4,5},{5,4},{6,7},{7,6},{8,9},{9,8},{10,11... | collective-permute-start | bytes 786440 | tf_op jit(solution)/shard_map/ppermute | solution.py:243
  26.4 0.8 %copy-start = (bf16[128,256]{1,0:T(8,128)(2,1)S(1)}, bf16[128,256]{1,0:T(8,128)(2,1)}, u32[]{:S(2)}) copy-start(bf16[128,256]{1,0:T(8,128)(2,1)} %refs_5_.1) | copy-start | bytes 196612
  29.1 1.4 %collective-permute-start.4 = (bf16[256,256]{1,0:T(8,128)(2,1)S(1)}, bf16[256,256]{1,0:T(8,128)(2,1)S(1)}, u32[]{:S(2)}, u32[]{:S(2)}) collective-permute-start(bf16[256,256]{1,0:T(8,128)(2,1)S(1)} %get-tuple-element.15), channel_id=1, source_target_pairs={{0,1},{1,0},{2,3},{3,2},{4,5},{5,4},{6,7},{7,6},{8,9},{9,8},{10,11... | collective-permute-start | bytes 393224 | tf_op jit(solution)/shard_map/ppermute | solution.py:243
  29.1 18.6 %collective-permute-start.12 = (bf16[1056,128]{1,0:T(8,128)(2,1)S(1)}, bf16[1056,128]{1,0:T(8,128)(2,1)S(1)}, u32[]{:S(2)}, u32[]{:S(2)}) collective-permute-start(bf16[1056,128]{1,0:T(8,128)(2,1)S(1)} %pad_maximum_fusion.refs_0_.refs_1_), channel_id=1, source_target_pairs={{0,1},{1,0},{2,3},{3,2},{4,5},{5,4},{6,7},{7,6},{8,9},{9,8},{10,11... | collective-permute-start | bytes 811016 | tf_op jit(solution)/shard_map/ppermute | solution.py:243
  29.6 18.1 %collective-permute-start.13 = (bf16[1056,128]{1,0:T(8,128)(2,1)S(1)}, bf16[1056,128]{1,0:T(8,128)(2,1)S(1)}, u32[]{:S(2)}, u32[]{:S(2)}) collective-permute-start(bf16[1056,128]{1,0:T(8,128)(2,1)S(1)} %collective-permute-done.3.refs_1_.refs_2_), channel_id=1, source_target_pairs={{0,1},{1,0},{2,3},{3,2},{4,5},{5,4},{6,7},{7,6},{8,9},{9,8},{10,11... | collective-permute-start | bytes 811016 | tf_op jit(solution)/shard_map/ppermute | solution.py:243
  30.5 17.2 %copy-start.1 = (bf16[128,256]{1,0:T(8,128)(2,1)S(1)}, bf16[128,256]{1,0:T(8,128)(2,1)}, u32[]{:S(2)}) copy-start(bf16[128,256]{1,0:T(8,128)(2,1)} %refs_5_.1) | copy-start | bytes 196612
  47.5 4.2 %collective-permute-start.11 = (f32[256,512]{1,0:T(8,128)S(1)}, f32[256,512]{1,0:T(8,128)S(1)}, u32[]{:S(2)}, u32[]{:S(2)}) collective-permute-start(f32[256,512]{1,0:T(8,128)S(1)} %get-tuple-element.18), channel_id=1, source_target_pairs={{0,1},{1,0},{2,3},{3,2},{4,5},{5,4},{6,7},{7,6},{8,9},{9,8},{10,11... | collective-permute-start | bytes 1572872 | tf_op jit(solution)/shard_map/ppermute | solution.py:243
  50.3 1.4 %collective-permute-start.14 = (f32[136,256]{1,0:T(8,128)S(1)}, f32[136,256]{1,0:T(8,128)S(1)}, u32[]{:S(2)}, u32[]{:S(2)}) collective-permute-start(f32[136,256]{1,0:T(8,128)S(1)} %first.1.first_ref), channel_id=1, source_target_pairs={{0,1},{1,0},{2,3},{3,2},{4,5},{5,4},{6,7},{7,6},{8,9},{9,8},{10,11... | collective-permute-start | bytes 417800 | tf_op jit(solution)/shard_map/ppermute | solution.py:243

commit v4 on v3

--- a/solution.py
+++ b/solution.py
@@ -11,6 +11,7 @@
 F32 = jnp.float32
 MAIN_VMEM = 50 << 20
 W_STEPS = 4
+LATE = 9
 
 
 def dot(a, b, dims):
@@ -38,21 +39,19 @@
 
 
 def group_kernel(me_ref, *refs, rs, pairs, orbitals):
-    *pack_refs, w_first_ref, mine_ref, theirs_ref = refs
+    *pack_refs, w_first_ref, mine_ref, theirs_ref, stack_ref = refs
     core = me_ref[0] % 2
     rows = lax.broadcasted_iota(jnp.int32, (4 * rs, pairs), 0)
     rows = ((rows + core * (2 * rs)) % (4 * rs)).astype(F32)
-    to = 0
-    for pack_ref in pack_refs:
-        for k in range(pack_ref.shape[0] // (pairs + 8)):
-            feats, label = unpack(pack_ref, k, pairs)
-            pre = dot(feats, w_first_ref[...], (1, 0))
-            hidden = (pre * (0.5 * jnp.tanh(0.5 * pre) + 0.5)).astype(BF16)
-            pick = (rows == label).astype(F32).astype(BF16)
-            sums = (dot(pick, hidden, (1, 0)) * (1.0 / orbitals)).astype(BF16)
-            mine_ref[to : to + 2 * rs, :] = sums[: 2 * rs, :]
-            theirs_ref[to : to + 2 * rs, :] = sums[2 * rs :, :]
-            to += 2 * rs
+    for k, pack_ref in enumerate(pack_refs):
+        feats, label = unpack(pack_ref, 0, pairs)
+        pre = dot(feats, w_first_ref[...], (1, 0))
+        hidden = (pre * (0.5 * jnp.tanh(0.5 * pre) + 0.5)).astype(BF16)
+        pick = (rows == label).astype(F32).astype(BF16)
+        sums = (dot(pick, hidden, (1, 0)) * (1.0 / orbitals)).astype(BF16)
+        mine_ref[k * 2 * rs : (k + 1) * 2 * rs, :] = sums[: 2 * rs, :]
+        theirs_ref[k * 2 * rs : (k + 1) * 2 * rs, :] = sums[2 * rs :, :]
+        stack_ref[k * (pairs + 8) : (k + 1) * (pairs + 8), :] = pack_ref[...]
 
 
 def source_chip(m, chip, chips, z_count):
@@ -61,9 +60,9 @@
 
 
 def main_kernel(*refs, chips, z_count, rows_split, half_cols, orbitals):
-    me_ref, h_refs, p_refs, w_hbm = refs[0], refs[1:3], refs[3:7], refs[7]
-    energies_ref, res_ref, keep_ref, send_ref, dh_ref, square_ref = refs[8:14]
-    w_ref, w_sems, h_ref, c_ref, x_ref, r_ref, g_ref, l_ref = refs[14:]
+    me_ref, h_refs, p_refs, w_hbm = refs[0], refs[1:5], refs[5:9], refs[9]
+    energies_ref, res_ref, keep_ref, send_ref, dh_ref, square_ref = refs[10:16]
+    w_ref, w_sems, h_ref, c_ref, x_ref, r_ref, g_ref, l_ref = refs[16:]
     w_steps = w_sems.shape[0]
     step_cols = w_ref.shape[2] // w_steps
     w_copies = []
@@ -97,35 +96,28 @@
             place(lister, p_refs[2 * which + dx][dz * 128 : (dz + 1) * 128, :])
             at = pl.multiple_of(lister * rs, rs)
             for pc in range(2):
-                lo = (dx * z_count + dz) * 2 * rs + pc * rs
-                h_ref[pc, pl.ds(at, rs), :] = h_refs[which][lo : lo + rs, :]
+                lo = dz * 2 * rs + pc * rs
+                h_ref[pc, pl.ds(at, rs), :] = h_refs[2 * which + dx][lo : lo + rs, :]
+
+    h0, h1 = h_ref[0], h_ref[1]
+    per = step_cols // 128
 
     for i in range(w_steps):
+        at = i * step_cols
         w_copies[i].wait()
-        for k in range(i * step_cols // 128, (i + 1) * step_cols // 128):
-            cols = slice(k * 128, (k + 1) * 128)
+        for k in range(per):
+            cols = slice(at + k * 128, at + (k + 1) * 128)
             w_ref[1, :, cols] = pltpu.roll(w_ref[0, :, cols].astype(F32), 64, 1).astype(BF16)
-
-    h0, h1 = h_ref[0], h_ref[1]
-    steps = half // step_cols
-    per = step_cols // 128
-
-    def forward(i, carry):
-        hs, nb = i // steps, i % steps
-        at = pl.multiple_of(i * step_cols, step_cols)
-        y0 = dot(h0, w_ref[0, :, pl.ds(at, step_cols)], (1, 0))
-        y1 = dot(h1, w_ref[1, :, pl.ds(at, step_cols)], (1, 0))
+        y0 = dot(h0, w_ref[0, :, at : at + step_cols], (1, 0))
+        y1 = dot(h1, w_ref[1, :, at : at + step_cols], (1, 0))
         for k in range(per):
-            row = pl.multiple_of((hs * ah_count + nb * per + k) * rs, rs)
+            row = (i * per + k) * rs
             for j in range(listers):
                 v0 = y0[j * rs : (j + 1) * rs, k * 128 : (k + 1) * 128]
                 v1 = y1[j * rs : (j + 1) * rs, k * 128 : (k + 1) * 128]
                 cols = slice(j * 128, (j + 1) * 128)
-                x_ref[0, pl.ds(row, rs), cols] = jnp.where(low, v0, v1).astype(BF16)
-                x_ref[1, pl.ds(row, rs), cols] = jnp.where(low, v1, v0).astype(BF16)
-        return carry
-
-    lax.fori_loop(0, 2 * steps, forward, 0)
+                x_ref[0, row : row + rs, cols] = jnp.where(low, v0, v1).astype(BF16)
+                x_ref[1, row : row + rs, cols] = jnp.where(low, v1, v0).astype(BF16)
 
     energies = energies_ref[...]
     n_rows = ah_count * rs
@@ -246,30 +238,38 @@
         sends = [(2 * source_chip(m, q, chips, z_count) + c, 2 * q + c) for q in range(chips) for c in range(2)]
         return lax.ppermute(v, "blk", sends) if m else v
 
-    def along_z(v):
-        return jnp.concatenate([from_chip(v, dz * x_count) for dz in range(z_count)], axis=0)
-
     pack = pl.pallas_call(
         functools.partial(pack_kernel, rs=rs, blk_dev=blk_dev),
         out_shape=jax.ShapeDtypeStruct((pairs + 8, f_width), BF16),
         cost_estimate=pl.CostEstimate(flops=0, transcendentals=0, bytes_accessed=1 << 20),
         name="pack",
     )(pair_dest.reshape(1, pairs), pair_row.reshape(1, pairs), pair_col.reshape(1, pairs), features)
-    packs_z = along_z(pack)
-    packs = [packs_z, from_chip(packs_z, 1)]
-    panels_z = along_z(panel.reshape(blk_dev * orbitals, columns))
+    def to_both(v):
+        sends = [(2 * source_chip(1, q, chips, z_count) + 1 - c, 2 * q + c) for q in range(chips) for c in range(2)]
+        return lax.ppermute(v, "blk", sends)
+
+    rows = panel.reshape(blk_dev * orbitals, columns)
+    rows_late, pack = lax.optimization_barrier((rows, pack))
+    packs = [from_chip(pack, dz * x_count) for dz in range(z_count)]
+    panels_z = [rows] + [from_chip(rows if dz < LATE else rows_late, dz * x_count) for dz in range(1, z_count)]
+    panels_z = jnp.concatenate(panels_z, axis=0)
     panels = [panels_z, from_chip(panels_z, 1)]
-    h_mine, h_theirs = pl.pallas_call(
+    h_mine, h_theirs, packs_z = pl.pallas_call(
         functools.partial(group_kernel, rs=rs, pairs=pairs, orbitals=orbitals),
-        out_shape=(jax.ShapeDtypeStruct((2 * rs * chips, hid), BF16),) * 2,
-        in_specs=[smem] + [vmem] * 3,
+        out_shape=(
+            jax.ShapeDtypeStruct((2 * rs * z_count, hid), BF16),
+            jax.ShapeDtypeStruct((2 * rs * z_count, hid), BF16),
+            jax.ShapeDtypeStruct((z_count * (pairs + 8), f_width), BF16),
+        ),
+        in_specs=[smem] + [vmem] * (z_count + 1),
         compiler_params=pltpu.CompilerParams(vmem_limit_bytes=12 << 20),
-        cost_estimate=pl.CostEstimate(flops=1 << 30, transcendentals=0, bytes_accessed=1 << 21),
+        cost_estimate=pl.CostEstimate(flops=1 << 34, transcendentals=0, bytes_accessed=1 << 21),
         name="group",
     )(me, *packs, w_first)
-    h_other = to_core(h_theirs)
+    hiddens = [h_mine, from_chip(h_mine, 1), to_core(h_theirs), to_both(h_theirs)]
+    panels[1], packs_z = lax.optimization_barrier((panels[1], packs_z))
     panels += [to_core(v) for v in panels]
-    packs += [to_core(v) for v in packs]
+    packs = [packs_z, from_chip(packs_z, 1), to_core(packs_z), to_both(packs_z)]
 
     listers = n_dev
     k_width = listers * 128
@@ -285,7 +285,7 @@
             jax.ShapeDtypeStruct((2, listers * rs, hid), F32),
             jax.ShapeDtypeStruct((8, columns), F32),
         ),
-        in_specs=[smem] + [vmem] * 6 + [anywhere, vmem],
+        in_specs=[smem] + [vmem] * 8 + [anywhere, vmem],
         scratch_shapes=[
             pltpu.VMEM((2, hid, flat), BF16),
             pltpu.SemaphoreType.DMA((W_STEPS,)),
@@ -297,9 +297,9 @@
             pltpu.VMEM((2, listers * rs, flat), BF16),
         ],
         compiler_params=pltpu.CompilerParams(vmem_limit_bytes=MAIN_VMEM),
-        cost_estimate=pl.CostEstimate(flops=16 * listers * rs * hid * flat, transcendentals=0, bytes_accessed=1 << 24),
+        cost_estimate=pl.CostEstimate(flops=1 << 29, transcendentals=0, bytes_accessed=1 << 20),
         name="step",
-    )(me, h_mine, h_other, *panels, w_second, energies.reshape(1, columns))
+    )(me, *hiddens, *panels, w_second, energies.reshape(1, columns))
     send = to_core(send)
     first = pl.pallas_call(
         functools.partial(first_kernel, chips=chips, z_count=z_count, rs=rs, pairs=pairs),

time: 52.9 us -> 48.7 us (0.921)
  waiting for transfers between devices: 10.2 us -> 5.98 us
  starting transfers between devices: 15.2 us -> 17.5 us
  Pallas kernels: 23.8 us -> 21.6 us
  other arithmetic: 1.76 us -> 0.86 us
  local copies, waits for them, and re-layouts: 0.85 us -> 1.73 us
    ppermute x8 -> x9, waiting for transfers between devices: 8.48 us -> 4.81 us  [from_chip(): return lax.ppermute(v, 'blk', sends) if m else v]
    ppermute x8 -> x9, starting transfers between devices: 14 us -> 15.8 us  [from_chip(): return lax.ppermute(v, 'blk', sends) if m else v]
    pallas_call x1, Pallas kernels: 17 us -> 15.6 us  [near(): pl.pallas_call(functools.partial(main_kernel, chips=chips, z_count=z_coun...]
    concatenate x2 -> x1, other arithmetic: 1.76 us -> 0.86 us  [near(): panels_z = jnp.concatenate(panels_z, axis=0)]
    unnamed x6 -> x8, local copies, waits for them, and re-layouts: 0.85 us -> 1.73 us
    ppermute x0 -> x2, starting transfers between devices: none -> 0.86 us  [to_both(): return lax.ppermute(v, 'blk', sends)]
    pallas_call x1, Pallas kernels: 1.81 us -> 0.97 us  [near(): pl.pallas_call(functools.partial(group_kernel, rs=rs, pairs=pairs, orbita...]
    ppermute x7 -> x6, waiting for transfers between devices: 1.77 us -> 1.17 us  [to_core(): return lax.ppermute(v, 'blk', [(i, i ^ 1) for i in range(n_dev)])]
  transfers between devices with their start and end apart: 15 -> 17, of which waited for: 6 -> 5; matrix products, arithmetic and copies ran while one was open for 3% -> 2% of each run, Pallas kernels for 44% -> 43%
where the time goes in v4:
time: 48.7 us; the launch traced here: 48.4 us
  Pallas kernels  21.6 us (44%)
  starting transfers between devices  17.5 us (36%)
  waiting for transfers between devices  5.98 us (12%)
  local copies, waits for them, and re-layouts  1.73 us (4%)
  other arithmetic  0.86 us (2%)
  between operations  0.7 us (1%)
    ppermute x9, starting transfers between devices, from_chip(): return lax.ppermute(v, 'blk', sends) if m else v  15.8 us
    pallas_call x1, Pallas kernels, near(): pl.pallas_call(functools.partial(main_kernel, chips=chips, z_count=z_coun...  15.6 us
    ppermute x9, waiting for transfers between devices, from_chip(): return lax.ppermute(v, 'blk', sends) if m else v  4.81 us
    pallas_call x1, Pallas kernels, near(): pl.pallas_call(functools.partial(first_kernel, chips=chips, z_count=z_cou...  2.55 us
    unnamed x8, local copies, waits for them, and re-layouts  1.73 us
    pallas_call x1, Pallas kernels, near(): pl.pallas_call(functools.partial(pack_kernel, rs=rs, blk_dev=blk_dev), ou...  1.54 us
    ppermute x6, waiting for transfers between devices, to_core(): return lax.ppermute(v, 'blk', [(i, i ^ 1) for i in range(n_dev)])  1.17 us
  transfers between devices with their start and end apart: 17, of which 5 were waited for; matrix products, arithmetic and copies ran while one was open for 2% of the time, Pallas kernels for 43%

profile of v4, /device:TPU:0, one launch (start us, length us, event | category | flops | bytes accessed | tf_op | source)
XLA Modules:
  0.0 48.4 jit_solution(7587647408345210945)
XLA Ops:
  0.6 3.1 %collective-permute-start.6 = (bf16[128,256]{1,0:T(8,128)(2,1)}, bf16[128,256]{1,0:T(8,128)(2,1)S(1)}, u32[]{:S(2)}, u32[]{:S(2)}) collective-permute-start(bf16[128,256]{1,0:T(8,128)(2,1)} %bitcast.8), channel_id=1, source_target_pairs={{12,0},{13,1},{14,2},{15,3},{0,4},{1,5},{2,6},{3,7},{4,8},{5,9},{6... | collective-permute-start | bytes 196616 | tf_op jit(solution)/shard_map/ppermute | solution.py:239
  3.7 2.6 %collective-permute-start.7 = (bf16[128,256]{1,0:T(8,128)(2,1)}, bf16[128,256]{1,0:T(8,128)(2,1)S(1)}, u32[]{:S(2)}, u32[]{:S(2)}) collective-permute-start(bf16[128,256]{1,0:T(8,128)(2,1)} %bitcast.9), channel_id=1, source_target_pairs={{8,0},{9,1},{10,2},{11,3},{12,4},{13,5},{14,6},{15,7},{0,8},{1,9},... | collective-permute-start | bytes 196616 | tf_op jit(solution)/shard_map/ppermute | solution.py:239
  6.3 1.3 %collective-permute-start.8 = (bf16[128,256]{1,0:T(8,128)(2,1)}, bf16[128,256]{1,0:T(8,128)(2,1)S(1)}, u32[]{:S(2)}, u32[]{:S(2)}) collective-permute-start(bf16[128,256]{1,0:T(8,128)(2,1)} %bitcast.10), channel_id=1, source_target_pairs={{4,0},{5,1},{6,2},{7,3},{8,4},{9,5},{10,6},{11,7},{12,8},{13,9},{1... | collective-permute-start | bytes 196616 | tf_op jit(solution)/shard_map/ppermute | solution.py:239
  7.6 1.5 %pack.1.refs_0_ = bf16[264,128]{1,0:T(8,128)(2,1)} custom-call(s32[1,256]{1,0:T(1,128)} %bitcast.12, s32[1,256]{1,0:T(1,128)} %bitcast.13, s32[1,256]{1,0:T(1,128)} %bitcast.14, bf16[256,128]{1,0:T(8,128)(2,1)} %feats_ref.1), custom_call_target="tpu_custom_call" | custom-call | bytes 1048576 | tf_op jit(solution)/shard_map/pack/pallas_call | solution.py:241
  9.2 0.7 %collective-permute-start = (bf16[264,128]{1,0:T(8,128)(2,1)}, bf16[264,128]{1,0:T(8,128)(2,1)S(1)}, u32[]{:S(2)}, u32[]{:S(2)}) collective-permute-start(bf16[264,128]{1,0:T(8,128)(2,1)} %pack.1.refs_0_), channel_id=1, source_target_pairs={{12,0},{13,1},{14,2},{15,3},{0,4},{1,5},{2,6},{3,7},{4,8},{5,9},{6... | collective-permute-start | bytes 202760 | tf_op jit(solution)/shard_map/ppermute | solution.py:239
  9.9 0.3 collective-permute-start.1
  10.2 0.0 collective-permute-done.6
  10.2 2.8 %collective-permute-start.2 = (bf16[264,128]{1,0:T(8,128)(2,1)}, bf16[264,128]{1,0:T(8,128)(2,1)S(1)}, u32[]{:S(2)}, u32[]{:S(2)}) collective-permute-start(bf16[264,128]{1,0:T(8,128)(2,1)} %pack.1.refs_0_), channel_id=1, source_target_pairs={{4,0},{5,1},{6,2},{7,3},{8,4},{9,5},{10,6},{11,7},{12,8},{13,9},{1... | collective-permute-start | bytes 202760 | tf_op jit(solution)/shard_map/ppermute | solution.py:239
  13.0 0.0 collective-permute-done.7
  13.0 0.9 %pad_maximum_fusion.refs_5_ = bf16[512,256]{1,0:T(8,128)(2,1)S(1)} fusion(bf16[128,256]{1,0:T(8,128)(2,1)S(1)} %collective-permute-done.8, bf16[128,256]{1,0:T(8,128)(2,1)S(1)} %collective-permute-done.7, bf16[128,256]{1,0:T(8,128)(2,1)S(1)} %collective-permute-done.6, bf16[128,256]{1,0:T(8,128)(2,1)} %bitcast.11), kind=kLoop, calls=%fused_computation | loop fusion | flops 1048576 | bytes 524288 | tf_op jit(solution)/shard_map/concatenate | solution.py:255
  13.9 1.6 %collective-permute-start.9 = (bf16[512,256]{1,0:T(8,128)(2,1)S(1)}, bf16[512,256]{1,0:T(8,128)(2,1)S(1)}, u32[]{:S(2)}, u32[]{:S(2)}) collective-permute-start(bf16[512,256]{1,0:T(8,128)(2,1)S(1)} %pad_maximum_fusion.refs_5_), channel_id=1, source_target_pairs={{2,0},{3,1},{0,2},{1,3},{6,4},{7,5},{4,6},{5,7},{10,8},{11,9},{8,1... | collective-permute-start | bytes 786440 | tf_op jit(solution)/shard_map/ppermute | solution.py:239
  15.4 0.4 collective-permute-done.refs_1_
  15.9 1.5 %collective-permute-done.1.refs_2_ = bf16[264,128]{1,0:T(8,128)(2,1)S(1)} collective-permute-done((bf16[264,128]{1,0:T(8,128)(2,1)}, bf16[264,128]{1,0:T(8,128)(2,1)S(1)}, u32[]{:S(2)}, u32[]{:S(2)}) %collective-permute-start.1) | collective-permute-done | bytes 67616 | tf_op jit(solution)/shard_map/ppermute | solution.py:239
  17.4 0.9 %copy-done = bf16[264,128]{1,0:T(8,128)(2,1)S(1)} copy-done((bf16[264,128]{1,0:T(8,128)(2,1)S(1)}, bf16[264,128]{1,0:T(8,128)(2,1)}, u32[]{:S(2)}) %copy-start) | copy-done | bytes 67608
  18.2 0.8 %copy-done.2 = bf16[128,256]{1,0:T(8,128)(2,1)S(1)} copy-done((bf16[128,256]{1,0:T(8,128)(2,1)S(1)}, bf16[128,256]{1,0:T(8,128)(2,1)}, u32[]{:S(2)}) %copy-start.2) | copy-done | bytes 65560
  19.1 1.0 %group.1 = (bf16[128,256]{1,0:T(8,128)(2,1)S(1)}, bf16[128,256]{1,0:T(8,128)(2,1)S(1)}, bf16[1056,128]{1,0:T(8,128)(2,1)S(1)}) custom-call(s32[1]{0:T(128)} %bitcast.me_ref.refs_0_, bf16[264,128]{1,0:T(8,128)(2,1)S(1)} %copy-done, bf16[264,128]{1,0:T(8,128)(2,1)S(1)} %collective-permute-done.refs_1_, bf16[264,128]{1,0:T(8,128)(2,1)S(1)} %collective-permute-done.1.refs_2_, ...), custom_call_target="tpu_custom_call" | custom-call | flops 17179869184 | bytes 2097152 | tf_op jit(solution)/shard_map/group/pallas_call | solution.py:257
  20.1 0.0 copy-start.3
  20.1 0.5 %collective-permute-done.9.refs_6_ = bf16[512,256]{1,0:T(8,128)(2,1)S(1)} collective-permute-done((bf16[512,256]{1,0:T(8,128)(2,1)S(1)}, bf16[512,256]{1,0:T(8,128)(2,1)S(1)}, u32[]{:S(2)}, u32[]{:S(2)}) %collective-permute-start.9) | collective-permute-done | bytes 262176 | tf_op jit(solution)/shard_map/ppermute | solution.py:239
  20.6 1.5 %collective-permute-start.3 = (bf16[128,256]{1,0:T(8,128)(2,1)S(1)}, bf16[128,256]{1,0:T(8,128)(2,1)S(1)}, u32[]{:S(2)}, u32[]{:S(2)}) collective-permute-start(bf16[128,256]{1,0:T(8,128)(2,1)S(1)} %get-tuple-element.19.refs_1_), channel_id=1, source_target_pairs={{2,0},{3,1},{0,2},{1,3},{6,4},{7,5},{4,6},{5,7},{10,8},{11,9},{8,1... | collective-permute-start | bytes 196616 | tf_op jit(solution)/shard_map/ppermute | solution.py:239
  22.1 0.2 collective-permute-start.4
  22.3 0.4 collective-permute-start.5
  22.7 2.4 %collective-permute-done.3.refs_2_ = bf16[128,256]{1,0:T(8,128)(2,1)S(1)} collective-permute-done((bf16[128,256]{1,0:T(8,128)(2,1)S(1)}, bf16[128,256]{1,0:T(8,128)(2,1)S(1)}, u32[]{:S(2)}, u32[]{:S(2)}) %collective-permute-start.3) | collective-permute-done | bytes 65568 | tf_op jit(solution)/shard_map/ppermute | solution.py:239
  25.1 1.9 %collective-permute-start.13 = (bf16[1056,128]{1,0:T(8,128)(2,1)S(1)}, bf16[1056,128]{1,0:T(8,128)(2,1)S(1)}, u32[]{:S(2)}, u32[]{:S(2)}) collective-permute-start(bf16[1056,128]{1,0:T(8,128)(2,1)S(1)} %get-tuple-element.26.refs_1_), channel_id=1, source_target_pairs={{2,0},{3,1},{0,2},{1,3},{6,4},{7,5},{4,6},{5,7},{10,8},{11,9},{8,1... | collective-permute-start | bytes 811016 | tf_op jit(solution)/shard_map/ppermute | solution.py:239
  27.0 0.0 collective-permute-done.4.refs_3_
  27.0 0.0 collective-permute-start.14
  27.0 0.4 collective-permute-start.15
  27.4 15.6 %step.1 = (f32[2,64,256]{2,1,0:T(8,128)}, f32[256,512]{1,0:T(8,128)S(1)}, f32[256,512]{1,0:T(8,128)S(1)}, f32[2,256,256]{2,1,0:T(8,128)S(1)}, f32[8,256]{1,0:T(8,128)S(1)}) custom-call(s32[1]{0:T(128)} %bitcast.me_ref.refs_0_, bf16[128,256]{1,0:T(8,128)(2,1)S(1)} %get-tuple-element.19.refs_1_, bf16[128,256]{1,0:T(8,128)(2,1)S(1)} %collective-permute-done.3.refs_2_, ...), custom_call_target="tpu_custom_call" | custom-call | flops 536870912 | bytes 1048576 | tf_op jit(solution)/shard_map/step/pallas_call | solution.py:277
  43.1 0.4 collective-permute-start.12
  43.5 2.5 %first.1.first_ref = f32[136,256]{1,0:T(8,128)S(1)} custom-call(s32[1]{0:T(128)} %bitcast.me_ref.refs_0_, bf16[1056,128]{1,0:T(8,128)(2,1)S(1)} %get-tuple-element.26.refs_1_, bf16[1056,128]{1,0:T(8,128)(2,1)S(1)} %collective-permute-done.13.refs_2_, bf16[1056,128]{1,0:T(8,128)(2,1)S(1)} %collective-permute-done.14.refs_3_, ...), custom_call_target="tpu_custom_call" | custom-call | flops 2147483648 | bytes 4194304 | tf_op jit(solution)/shard_map/first/pallas_call | solution.py:304
  46.0 0.3 collective-permute-start.16
  46.3 1.2 %collective-permute-done.16.got_ref = f32[136,256]{1,0:T(8,128)S(1)} collective-permute-done((f32[136,256]{1,0:T(8,128)S(1)}, f32[136,256]{1,0:T(8,128)S(1)}, u32[]{:S(2)}, u32[]{:S(2)}) %collective-permute-start.16) | collective-permute-done | bytes 139296 | tf_op jit(solution)/shard_map/ppermute | solution.py:235
  47.5 0.9 %combine.1 = (f32[256,512]{1,0:T(8,128)}, f32[128,256]{1,0:T(8,128)}, f32[1,1]{1,0:T(1,128)}) custom-call(f32[256,512]{1,0:T(8,128)S(1)} %get-tuple-element.24.keep_ref, f32[256,512]{1,0:T(8,128)S(1)} %collective-permute-done.12.sent_ref, f32[136,256]{1,0:T(8,128)S(1)} %first.1.first_ref, f32[136,256]{1,0:T(8,128)S(1)} %collective-permute-done.16.got_ref), custom_call_target="tpu_custom_call" | custom-call | tf_op jit(solution)/shard_map/combine/pallas_call | solution.py:314
  (16 shorter events, 0.0 us)
Async XLA Ops:
  0.6 9.6 %collective-permute-start.6 = (bf16[128,256]{1,0:T(8,128)(2,1)}, bf16[128,256]{1,0:T(8,128)(2,1)S(1)}, u32[]{:S(2)}, u32[]{:S(2)}) collective-permute-start(bf16[128,256]{1,0:T(8,128)(2,1)} %bitcast.8), channel_id=1, source_target_pairs={{12,0},{13,1},{14,2},{15,3},{0,4},{1,5},{2,6},{3,7},{4,8},{5,9},{6... | collective-permute-start | bytes 196616 | tf_op jit(solution)/shard_map/ppermute | solution.py:239
  3.7 9.3 %collective-permute-start.7 = (bf16[128,256]{1,0:T(8,128)(2,1)}, bf16[128,256]{1,0:T(8,128)(2,1)S(1)}, u32[]{:S(2)}, u32[]{:S(2)}) collective-permute-start(bf16[128,256]{1,0:T(8,128)(2,1)} %bitcast.9), channel_id=1, source_target_pairs={{8,0},{9,1},{10,2},{11,3},{12,4},{13,5},{14,6},{15,7},{0,8},{1,9},... | collective-permute-start | bytes 196616 | tf_op jit(solution)/shard_map/ppermute | solution.py:239
  6.3 6.7 %collective-permute-start.8 = (bf16[128,256]{1,0:T(8,128)(2,1)}, bf16[128,256]{1,0:T(8,128)(2,1)S(1)}, u32[]{:S(2)}, u32[]{:S(2)}) collective-permute-start(bf16[128,256]{1,0:T(8,128)(2,1)} %bitcast.10), channel_id=1, source_target_pairs={{4,0},{5,1},{6,2},{7,3},{8,4},{9,5},{10,6},{11,7},{12,8},{13,9},{1... | collective-permute-start | bytes 196616 | tf_op jit(solution)/shard_map/ppermute | solution.py:239
  9.2 6.7 %collective-permute-start = (bf16[264,128]{1,0:T(8,128)(2,1)}, bf16[264,128]{1,0:T(8,128)(2,1)S(1)}, u32[]{:S(2)}, u32[]{:S(2)}) collective-permute-start(bf16[264,128]{1,0:T(8,128)(2,1)} %pack.1.refs_0_), channel_id=1, source_target_pairs={{12,0},{13,1},{14,2},{15,3},{0,4},{1,5},{2,6},{3,7},{4,8},{5,9},{6... | collective-permute-start | bytes 202760 | tf_op jit(solution)/shard_map/ppermute | solution.py:239
  9.9 7.5 %collective-permute-start.1 = (bf16[264,128]{1,0:T(8,128)(2,1)}, bf16[264,128]{1,0:T(8,128)(2,1)S(1)}, u32[]{:S(2)}, u32[]{:S(2)}) collective-permute-start(bf16[264,128]{1,0:T(8,128)(2,1)} %pack.1.refs_0_), channel_id=1, source_target_pairs={{8,0},{9,1},{10,2},{11,3},{12,4},{13,5},{14,6},{15,7},{0,8},{1,9},... | collective-permute-start | bytes 202760 | tf_op jit(solution)/shard_map/ppermute | solution.py:239
  10.2 7.2 %collective-permute-start.2 = (bf16[264,128]{1,0:T(8,128)(2,1)}, bf16[264,128]{1,0:T(8,128)(2,1)S(1)}, u32[]{:S(2)}, u32[]{:S(2)}) collective-permute-start(bf16[264,128]{1,0:T(8,128)(2,1)} %pack.1.refs_0_), channel_id=1, source_target_pairs={{4,0},{5,1},{6,2},{7,3},{8,4},{9,5},{10,6},{11,7},{12,8},{13,9},{1... | collective-permute-start | bytes 202760 | tf_op jit(solution)/shard_map/ppermute | solution.py:239
  13.9 6.7 %collective-permute-start.9 = (bf16[512,256]{1,0:T(8,128)(2,1)S(1)}, bf16[512,256]{1,0:T(8,128)(2,1)S(1)}, u32[]{:S(2)}, u32[]{:S(2)}) collective-permute-start(bf16[512,256]{1,0:T(8,128)(2,1)S(1)} %pad_maximum_fusion.refs_5_), channel_id=1, source_target_pairs={{2,0},{3,1},{0,2},{1,3},{6,4},{7,5},{4,6},{5,7},{10,8},{11,9},{8,1... | collective-permute-start | bytes 786440 | tf_op jit(solution)/shard_map/ppermute | solution.py:239
  15.4 12.0 %collective-permute-start.10 = (bf16[512,256]{1,0:T(8,128)(2,1)S(1)}, bf16[512,256]{1,0:T(8,128)(2,1)S(1)}, u32[]{:S(2)}, u32[]{:S(2)}) collective-permute-start(bf16[512,256]{1,0:T(8,128)(2,1)S(1)} %pad_maximum_fusion.refs_5_), channel_id=1, source_target_pairs={{0,1},{1,0},{2,3},{3,2},{4,5},{5,4},{6,7},{7,6},{8,9},{9,8},{10,11... | collective-permute-start | bytes 786440 | tf_op jit(solution)/shard_map/ppermute | solution.py:235
  17.4 0.9 %copy-start = (bf16[264,128]{1,0:T(8,128)(2,1)S(1)}, bf16[264,128]{1,0:T(8,128)(2,1)}, u32[]{:S(2)}) copy-start(bf16[264,128]{1,0:T(8,128)(2,1)} %pack.1.refs_0_) | copy-start | bytes 202756
  18.2 0.8 %copy-start.2 = (bf16[128,256]{1,0:T(8,128)(2,1)S(1)}, bf16[128,256]{1,0:T(8,128)(2,1)}, u32[]{:S(2)}) copy-start(bf16[128,256]{1,0:T(8,128)(2,1)} %refs_5_.1) | copy-start | bytes 196612
  19.1 8.4 %copy-start.1 = (f32[256]{0:T(256)S(1)}, f32[256]{0:T(256)}, u32[]{:S(2)}) copy-start(f32[256]{0:T(256)} %param.12) | copy-start | bytes 3076
  20.1 23.4 %copy-start.3 = (bf16[128,256]{1,0:T(8,128)(2,1)S(1)}, bf16[128,256]{1,0:T(8,128)(2,1)}, u32[]{:S(2)}) copy-start(bf16[128,256]{1,0:T(8,128)(2,1)} %refs_5_.1) | copy-start | bytes 196612
  20.6 6.8 %collective-permute-start.11 = (bf16[512,256]{1,0:T(8,128)(2,1)S(1)}, bf16[512,256]{1,0:T(8,128)(2,1)S(1)}, u32[]{:S(2)}, u32[]{:S(2)}) collective-permute-start(bf16[512,256]{1,0:T(8,128)(2,1)S(1)} %collective-permute-done.9.refs_6_), channel_id=1, source_target_pairs={{0,1},{1,0},{2,3},{3,2},{4,5},{5,4},{6,7},{7,6},{8,9},{9,8},{10,11... | collective-permute-start | bytes 786440 | tf_op jit(solution)/shard_map/ppermute | solution.py:235
  20.6 4.5 %collective-permute-start.3 = (bf16[128,256]{1,0:T(8,128)(2,1)S(1)}, bf16[128,256]{1,0:T(8,128)(2,1)S(1)}, u32[]{:S(2)}, u32[]{:S(2)}) collective-permute-start(bf16[128,256]{1,0:T(8,128)(2,1)S(1)} %get-tuple-element.19.refs_1_), channel_id=1, source_target_pairs={{2,0},{3,1},{0,2},{1,3},{6,4},{7,5},{4,6},{5,7},{10,8},{11,9},{8,1... | collective-permute-start | bytes 196616 | tf_op jit(solution)/shard_map/ppermute | solution.py:239
  22.1 4.9 %collective-permute-start.4 = (bf16[128,256]{1,0:T(8,128)(2,1)S(1)}, bf16[128,256]{1,0:T(8,128)(2,1)S(1)}, u32[]{:S(2)}, u32[]{:S(2)}) collective-permute-start(bf16[128,256]{1,0:T(8,128)(2,1)S(1)} %get-tuple-element.20), channel_id=1, source_target_pairs={{0,1},{1,0},{2,3},{3,2},{4,5},{5,4},{6,7},{7,6},{8,9},{9,8},{10,11... | collective-permute-start | bytes 196616 | tf_op jit(solution)/shard_map/ppermute | solution.py:235
  22.3 4.7 %collective-permute-start.5 = (bf16[128,256]{1,0:T(8,128)(2,1)S(1)}, bf16[128,256]{1,0:T(8,128)(2,1)S(1)}, u32[]{:S(2)}, u32[]{:S(2)}) collective-permute-start(bf16[128,256]{1,0:T(8,128)(2,1)S(1)} %get-tuple-element.20), channel_id=1, source_target_pairs={{3,0},{2,1},{1,2},{0,3},{7,4},{6,5},{5,6},{4,7},{11,8},{10,9},{9,1... | collective-permute-start | bytes 196616 | tf_op jit(solution)/shard_map/ppermute | solution.py:249
  25.1 18.4 %collective-permute-start.13 = (bf16[1056,128]{1,0:T(8,128)(2,1)S(1)}, bf16[1056,128]{1,0:T(8,128)(2,1)S(1)}, u32[]{:S(2)}, u32[]{:S(2)}) collective-permute-start(bf16[1056,128]{1,0:T(8,128)(2,1)S(1)} %get-tuple-element.26.refs_1_), channel_id=1, source_target_pairs={{2,0},{3,1},{0,2},{1,3},{6,4},{7,5},{4,6},{5,7},{10,8},{11,9},{8,1... | collective-permute-start | bytes 811016 | tf_op jit(solution)/shard_map/ppermute | solution.py:239
  27.0 16.5 %collective-permute-start.14 = (bf16[1056,128]{1,0:T(8,128)(2,1)S(1)}, bf16[1056,128]{1,0:T(8,128)(2,1)S(1)}, u32[]{:S(2)}, u32[]{:S(2)}) collective-permute-start(bf16[1056,128]{1,0:T(8,128)(2,1)S(1)} %get-tuple-element.26.refs_1_), channel_id=1, source_target_pairs={{0,1},{1,0},{2,3},{3,2},{4,5},{5,4},{6,7},{7,6},{8,9},{9,8},{10,11... | collective-permute-start | bytes 811016 | tf_op jit(solution)/shard_map/ppermute | solution.py:235
  27.0 16.5 %collective-permute-start.15 = (bf16[1056,128]{1,0:T(8,128)(2,1)S(1)}, bf16[1056,128]{1,0:T(8,128)(2,1)S(1)}, u32[]{:S(2)}, u32[]{:S(2)}) collective-permute-start(bf16[1056,128]{1,0:T(8,128)(2,1)S(1)} %get-tuple-element.26.refs_1_), channel_id=1, source_target_pairs={{3,0},{2,1},{1,2},{0,3},{7,4},{6,5},{5,6},{4,7},{11,8},{10,9},{9,1... | collective-permute-start | bytes 811016 | tf_op jit(solution)/shard_map/ppermute | solution.py:249
  43.1 4.4 %collective-permute-start.12 = (f32[256,512]{1,0:T(8,128)S(1)}, f32[256,512]{1,0:T(8,128)S(1)}, u32[]{:S(2)}, u32[]{:S(2)}) collective-permute-start(f32[256,512]{1,0:T(8,128)S(1)} %get-tuple-element.25), channel_id=1, source_target_pairs={{0,1},{1,0},{2,3},{3,2},{4,5},{5,4},{6,7},{7,6},{8,9},{9,8},{10,11... | collective-permute-start | bytes 1572872 | tf_op jit(solution)/shard_map/ppermute | solution.py:235
  46.0 1.4 %collective-permute-start.16 = (f32[136,256]{1,0:T(8,128)S(1)}, f32[136,256]{1,0:T(8,128)S(1)}, u32[]{:S(2)}, u32[]{:S(2)}) collective-permute-start(f32[136,256]{1,0:T(8,128)S(1)} %first.1.first_ref), channel_id=1, source_target_pairs={{0,1},{1,0},{2,3},{3,2},{4,5},{5,4},{6,7},{7,6},{8,9},{9,8},{10,11... | collective-permute-start | bytes 417800 | tf_op jit(solution)/shard_map/ppermute | solution.py:235

commit v5 on v4

--- a/solution.py
+++ b/solution.py
@@ -149,22 +149,19 @@
     jb_count = 8
     jb_width = jb_count * 128
 
-    def backward(i, carry):
+    for i in range(2 * (listers // jb_count)):
         hs, jb = i // (listers // jb_count), i % (listers // jb_count)
-        at = pl.multiple_of(jb * jb_width, jb_width)
+        at = jb * jb_width
         d_e = dot(g_ref[hs, 0], c_ref[0, pl.ds(at, jb_width), :], (1, 1))
         d_o = dot(g_ref[hs, 1], c_ref[1, pl.ds(at, jb_width), :], (1, 1))
         for j in range(jb_count):
-            row = pl.multiple_of((jb * jb_count + j) * rs, rs)
+            row = (jb * jb_count + j) * rs
             for ah in range(ah_count):
                 v0 = d_e[ah * rs : (ah + 1) * rs, j * 128 : (j + 1) * 128]
                 v1 = d_o[ah * rs : (ah + 1) * rs, j * 128 : (j + 1) * 128]
-                cols = pl.ds(pl.multiple_of(hs * half + ah * 128, 128), 128)
+                cols = slice(hs * half + ah * 128, hs * half + (ah + 1) * 128)
                 l_ref[0, pl.ds(row, rs), cols] = jnp.where(low, v0, v1).astype(BF16)
                 l_ref[1, pl.ds(row, rs), cols] = jnp.where(low, v1, v0).astype(BF16)
-        return carry
-
-    lax.fori_loop(0, 2 * (listers // jb_count), backward, 0)
 
     for pc in range(2):
         dh_ref[pc] = dot(l_ref[pc], w_ref[pc], (1, 1)) / orbitals

time: 48.7 us -> 47.6 us (0.977)
  Pallas kernels: 21.6 us -> 20.5 us
    pallas_call x1, Pallas kernels: 15.6 us -> 14.5 us  [near(): pl.pallas_call(functools.partial(main_kernel, chips=chips, z_count=z_coun...]
  transfers between devices with their start and end apart: 17 -> 17, of which waited for: 5 -> 5; matrix products, arithmetic and copies ran while one was open for 2% -> 2% of each run, Pallas kernels for 43% -> 41%
where the time goes in v5:
time: 47.6 us; the launch traced here: 47.3 us
  Pallas kernels  20.5 us (43%)
  starting transfers between devices  17.5 us (37%)
  waiting for transfers between devices  5.98 us (13%)
  local copies, waits for them, and re-layouts  1.73 us (4%)
  other arithmetic  0.86 us (2%)
  between operations  0.7 us (1%)
    ppermute x9, starting transfers between devices, from_chip(): return lax.ppermute(v, 'blk', sends) if m else v  15.8 us
    pallas_call x1, Pallas kernels, near(): pl.pallas_call(functools.partial(main_kernel, chips=chips, z_count=z_coun...  14.5 us
    ppermute x9, waiting for transfers between devices, from_chip(): return lax.ppermute(v, 'blk', sends) if m else v  4.81 us
    pallas_call x1, Pallas kernels, near(): pl.pallas_call(functools.partial(first_kernel, chips=chips, z_count=z_cou...  2.55 us
    unnamed x8, local copies, waits for them, and re-layouts  1.73 us
    pallas_call x1, Pallas kernels, near(): pl.pallas_call(functools.partial(pack_kernel, rs=rs, blk_dev=blk_dev), ou...  1.54 us
    ppermute x6, waiting for transfers between devices, to_core(): return lax.ppermute(v, 'blk', [(i, i ^ 1) for i in range(n_dev)])  1.16 us
    pallas_call x1, Pallas kernels, near(): pl.pallas_call(functools.partial(group_kernel, rs=rs, pairs=pairs, orbita...  0.97 us
  transfers between devices with their start and end apart: 17, of which 5 were waited for; matrix products, arithmetic and copies ran while one was open for 2% of the time, Pallas kernels for 41%

profile of v5, /device:TPU:0, one launch (start us, length us, event | category | flops | bytes accessed | tf_op | source)
XLA Modules:
  0.0 47.3 jit_solution(1252126817970013562)
XLA Ops:
  0.6 3.1 %collective-permute-start.6 = (bf16[128,256]{1,0:T(8,128)(2,1)}, bf16[128,256]{1,0:T(8,128)(2,1)S(1)}, u32[]{:S(2)}, u32[]{:S(2)}) collective-permute-start(bf16[128,256]{1,0:T(8,128)(2,1)} %bitcast.8), channel_id=1, source_target_pairs={{12,0},{13,1},{14,2},{15,3},{0,4},{1,5},{2,6},{3,7},{4,8},{5,9},{6... | collective-permute-start | bytes 196616 | tf_op jit(solution)/shard_map/ppermute | solution.py:236
  3.7 2.6 %collective-permute-start.7 = (bf16[128,256]{1,0:T(8,128)(2,1)}, bf16[128,256]{1,0:T(8,128)(2,1)S(1)}, u32[]{:S(2)}, u32[]{:S(2)}) collective-permute-start(bf16[128,256]{1,0:T(8,128)(2,1)} %bitcast.9), channel_id=1, source_target_pairs={{8,0},{9,1},{10,2},{11,3},{12,4},{13,5},{14,6},{15,7},{0,8},{1,9},... | collective-permute-start | bytes 196616 | tf_op jit(solution)/shard_map/ppermute | solution.py:236
  6.3 1.3 %collective-permute-start.8 = (bf16[128,256]{1,0:T(8,128)(2,1)}, bf16[128,256]{1,0:T(8,128)(2,1)S(1)}, u32[]{:S(2)}, u32[]{:S(2)}) collective-permute-start(bf16[128,256]{1,0:T(8,128)(2,1)} %bitcast.10), channel_id=1, source_target_pairs={{4,0},{5,1},{6,2},{7,3},{8,4},{9,5},{10,6},{11,7},{12,8},{13,9},{1... | collective-permute-start | bytes 196616 | tf_op jit(solution)/shard_map/ppermute | solution.py:236
  7.6 1.5 %pack.1.refs_0_ = bf16[264,128]{1,0:T(8,128)(2,1)} custom-call(s32[1,256]{1,0:T(1,128)} %bitcast.12, s32[1,256]{1,0:T(1,128)} %bitcast.13, s32[1,256]{1,0:T(1,128)} %bitcast.14, bf16[256,128]{1,0:T(8,128)(2,1)} %feats_ref.1), custom_call_target="tpu_custom_call" | custom-call | bytes 1048576 | tf_op jit(solution)/shard_map/pack/pallas_call | solution.py:238
  9.2 0.7 %collective-permute-start = (bf16[264,128]{1,0:T(8,128)(2,1)}, bf16[264,128]{1,0:T(8,128)(2,1)S(1)}, u32[]{:S(2)}, u32[]{:S(2)}) collective-permute-start(bf16[264,128]{1,0:T(8,128)(2,1)} %pack.1.refs_0_), channel_id=1, source_target_pairs={{12,0},{13,1},{14,2},{15,3},{0,4},{1,5},{2,6},{3,7},{4,8},{5,9},{6... | collective-permute-start | bytes 202760 | tf_op jit(solution)/shard_map/ppermute | solution.py:236
  9.9 0.3 collective-permute-start.1
  10.2 0.0 collective-permute-done.6
  10.2 2.8 %collective-permute-start.2 = (bf16[264,128]{1,0:T(8,128)(2,1)}, bf16[264,128]{1,0:T(8,128)(2,1)S(1)}, u32[]{:S(2)}, u32[]{:S(2)}) collective-permute-start(bf16[264,128]{1,0:T(8,128)(2,1)} %pack.1.refs_0_), channel_id=1, source_target_pairs={{4,0},{5,1},{6,2},{7,3},{8,4},{9,5},{10,6},{11,7},{12,8},{13,9},{1... | collective-permute-start | bytes 202760 | tf_op jit(solution)/shard_map/ppermute | solution.py:236
  13.0 0.9 %pad_maximum_fusion.refs_5_ = bf16[512,256]{1,0:T(8,128)(2,1)S(1)} fusion(bf16[128,256]{1,0:T(8,128)(2,1)S(1)} %collective-permute-done.8, bf16[128,256]{1,0:T(8,128)(2,1)S(1)} %collective-permute-done.7, bf16[128,256]{1,0:T(8,128)(2,1)S(1)} %collective-permute-done.6, bf16[128,256]{1,0:T(8,128)(2,1)} %bitcast.11), kind=kLoop, calls=%fused_computation | loop fusion | flops 1048576 | bytes 524288 | tf_op jit(solution)/shard_map/concatenate | solution.py:252
  13.9 1.6 %collective-permute-start.9 = (bf16[512,256]{1,0:T(8,128)(2,1)S(1)}, bf16[512,256]{1,0:T(8,128)(2,1)S(1)}, u32[]{:S(2)}, u32[]{:S(2)}) collective-permute-start(bf16[512,256]{1,0:T(8,128)(2,1)S(1)} %pad_maximum_fusion.refs_5_), channel_id=1, source_target_pairs={{2,0},{3,1},{0,2},{1,3},{6,4},{7,5},{4,6},{5,7},{10,8},{11,9},{8,1... | collective-permute-start | bytes 786440 | tf_op jit(solution)/shard_map/ppermute | solution.py:236
  15.4 0.4 collective-permute-done.refs_1_
  15.9 1.5 %collective-permute-done.1.refs_2_ = bf16[264,128]{1,0:T(8,128)(2,1)S(1)} collective-permute-done((bf16[264,128]{1,0:T(8,128)(2,1)}, bf16[264,128]{1,0:T(8,128)(2,1)S(1)}, u32[]{:S(2)}, u32[]{:S(2)}) %collective-permute-start.1) | collective-permute-done | bytes 67616 | tf_op jit(solution)/shard_map/ppermute | solution.py:236
  17.4 0.9 %copy-done = bf16[264,128]{1,0:T(8,128)(2,1)S(1)} copy-done((bf16[264,128]{1,0:T(8,128)(2,1)S(1)}, bf16[264,128]{1,0:T(8,128)(2,1)}, u32[]{:S(2)}) %copy-start) | copy-done | bytes 67608
  18.2 0.8 %copy-done.2 = bf16[128,256]{1,0:T(8,128)(2,1)S(1)} copy-done((bf16[128,256]{1,0:T(8,128)(2,1)S(1)}, bf16[128,256]{1,0:T(8,128)(2,1)}, u32[]{:S(2)}) %copy-start.2) | copy-done | bytes 65560
  19.1 1.0 %group.1 = (bf16[128,256]{1,0:T(8,128)(2,1)S(1)}, bf16[128,256]{1,0:T(8,128)(2,1)S(1)}, bf16[1056,128]{1,0:T(8,128)(2,1)S(1)}) custom-call(s32[1]{0:T(128)} %bitcast.me_ref.refs_0_, bf16[264,128]{1,0:T(8,128)(2,1)S(1)} %copy-done, bf16[264,128]{1,0:T(8,128)(2,1)S(1)} %collective-permute-done.refs_1_, bf16[264,128]{1,0:T(8,128)(2,1)S(1)} %collective-permute-done.1.refs_2_, ...), custom_call_target="tpu_custom_call" | custom-call | flops 17179869184 | bytes 2097152 | tf_op jit(solution)/shard_map/group/pallas_call | solution.py:254
  20.1 0.0 copy-start.3
  20.1 0.5 %collective-permute-done.9.refs_6_ = bf16[512,256]{1,0:T(8,128)(2,1)S(1)} collective-permute-done((bf16[512,256]{1,0:T(8,128)(2,1)S(1)}, bf16[512,256]{1,0:T(8,128)(2,1)S(1)}, u32[]{:S(2)}, u32[]{:S(2)}) %collective-permute-start.9) | collective-permute-done | bytes 262176 | tf_op jit(solution)/shard_map/ppermute | solution.py:236
  20.6 1.5 %collective-permute-start.3 = (bf16[128,256]{1,0:T(8,128)(2,1)S(1)}, bf16[128,256]{1,0:T(8,128)(2,1)S(1)}, u32[]{:S(2)}, u32[]{:S(2)}) collective-permute-start(bf16[128,256]{1,0:T(8,128)(2,1)S(1)} %get-tuple-element.19.refs_1_), channel_id=1, source_target_pairs={{2,0},{3,1},{0,2},{1,3},{6,4},{7,5},{4,6},{5,7},{10,8},{11,9},{8,1... | collective-permute-start | bytes 196616 | tf_op jit(solution)/shard_map/ppermute | solution.py:236
  22.1 0.2 collective-permute-start.4
  22.3 0.4 collective-permute-start.5
  22.7 2.4 %collective-permute-done.3.refs_2_ = bf16[128,256]{1,0:T(8,128)(2,1)S(1)} collective-permute-done((bf16[128,256]{1,0:T(8,128)(2,1)S(1)}, bf16[128,256]{1,0:T(8,128)(2,1)S(1)}, u32[]{:S(2)}, u32[]{:S(2)}) %collective-permute-start.3) | collective-permute-done | bytes 65568 | tf_op jit(solution)/shard_map/ppermute | solution.py:236
  25.1 1.9 %collective-permute-start.13 = (bf16[1056,128]{1,0:T(8,128)(2,1)S(1)}, bf16[1056,128]{1,0:T(8,128)(2,1)S(1)}, u32[]{:S(2)}, u32[]{:S(2)}) collective-permute-start(bf16[1056,128]{1,0:T(8,128)(2,1)S(1)} %get-tuple-element.26.refs_1_), channel_id=1, source_target_pairs={{2,0},{3,1},{0,2},{1,3},{6,4},{7,5},{4,6},{5,7},{10,8},{11,9},{8,1... | collective-permute-start | bytes 811016 | tf_op jit(solution)/shard_map/ppermute | solution.py:236
  27.0 0.0 collective-permute-done.4.refs_3_
  27.0 0.0 collective-permute-start.14
  27.0 0.0 collective-permute-done.5.refs_4_
  27.0 0.4 collective-permute-start.15
  27.4 14.5 %step.1 = (f32[2,64,256]{2,1,0:T(8,128)}, f32[256,512]{1,0:T(8,128)S(1)}, f32[256,512]{1,0:T(8,128)S(1)}, f32[2,256,256]{2,1,0:T(8,128)S(1)}, f32[8,256]{1,0:T(8,128)S(1)}) custom-call(s32[1]{0:T(128)} %bitcast.me_ref.refs_0_, bf16[128,256]{1,0:T(8,128)(2,1)S(1)} %get-tuple-element.19.refs_1_, bf16[128,256]{1,0:T(8,128)(2,1)S(1)} %collective-permute-done.3.refs_2_, ...), custom_call_target="tpu_custom_call" | custom-call | flops 536870912 | bytes 1048576 | tf_op jit(solution)/shard_map/step/pallas_call | solution.py:274
  42.0 0.4 collective-permute-start.12
  42.4 2.5 %first.1.first_ref = f32[136,256]{1,0:T(8,128)S(1)} custom-call(s32[1]{0:T(128)} %bitcast.me_ref.refs_0_, bf16[1056,128]{1,0:T(8,128)(2,1)S(1)} %get-tuple-element.26.refs_1_, bf16[1056,128]{1,0:T(8,128)(2,1)S(1)} %collective-permute-done.13.refs_2_, bf16[1056,128]{1,0:T(8,128)(2,1)S(1)} %collective-permute-done.14.refs_3_, ...), custom_call_target="tpu_custom_call" | custom-call | flops 2147483648 | bytes 4194304 | tf_op jit(solution)/shard_map/first/pallas_call | solution.py:301
  44.9 0.3 collective-permute-start.16
  45.2 1.1 %collective-permute-done.16.got_ref = f32[136,256]{1,0:T(8,128)S(1)} collective-permute-done((f32[136,256]{1,0:T(8,128)S(1)}, f32[136,256]{1,0:T(8,128)S(1)}, u32[]{:S(2)}, u32[]{:S(2)}) %collective-permute-start.16) | collective-permute-done | bytes 139296 | tf_op jit(solution)/shard_map/ppermute | solution.py:232
  46.4 0.9 %combine.1 = (f32[256,512]{1,0:T(8,128)}, f32[128,256]{1,0:T(8,128)}, f32[1,1]{1,0:T(1,128)}) custom-call(f32[256,512]{1,0:T(8,128)S(1)} %get-tuple-element.24.keep_ref, f32[256,512]{1,0:T(8,128)S(1)} %collective-permute-done.12.sent_ref, f32[136,256]{1,0:T(8,128)S(1)} %first.1.first_ref, f32[136,256]{1,0:T(8,128)S(1)} %collective-permute-done.16.got_ref), custom_call_target="tpu_custom_call" | custom-call | tf_op jit(solution)/shard_map/combine/pallas_call | solution.py:311
  (16 shorter events, 0.0 us)
Async XLA Ops:
  0.6 9.6 %collective-permute-start.6 = (bf16[128,256]{1,0:T(8,128)(2,1)}, bf16[128,256]{1,0:T(8,128)(2,1)S(1)}, u32[]{:S(2)}, u32[]{:S(2)}) collective-permute-start(bf16[128,256]{1,0:T(8,128)(2,1)} %bitcast.8), channel_id=1, source_target_pairs={{12,0},{13,1},{14,2},{15,3},{0,4},{1,5},{2,6},{3,7},{4,8},{5,9},{6... | collective-permute-start | bytes 196616 | tf_op jit(solution)/shard_map/ppermute | solution.py:236
  3.7 9.3 %collective-permute-start.7 = (bf16[128,256]{1,0:T(8,128)(2,1)}, bf16[128,256]{1,0:T(8,128)(2,1)S(1)}, u32[]{:S(2)}, u32[]{:S(2)}) collective-permute-start(bf16[128,256]{1,0:T(8,128)(2,1)} %bitcast.9), channel_id=1, source_target_pairs={{8,0},{9,1},{10,2},{11,3},{12,4},{13,5},{14,6},{15,7},{0,8},{1,9},... | collective-permute-start | bytes 196616 | tf_op jit(solution)/shard_map/ppermute | solution.py:236
  6.3 6.7 %collective-permute-start.8 = (bf16[128,256]{1,0:T(8,128)(2,1)}, bf16[128,256]{1,0:T(8,128)(2,1)S(1)}, u32[]{:S(2)}, u32[]{:S(2)}) collective-permute-start(bf16[128,256]{1,0:T(8,128)(2,1)} %bitcast.10), channel_id=1, source_target_pairs={{4,0},{5,1},{6,2},{7,3},{8,4},{9,5},{10,6},{11,7},{12,8},{13,9},{1... | collective-permute-start | bytes 196616 | tf_op jit(solution)/shard_map/ppermute | solution.py:236
  9.2 6.7 %collective-permute-start = (bf16[264,128]{1,0:T(8,128)(2,1)}, bf16[264,128]{1,0:T(8,128)(2,1)S(1)}, u32[]{:S(2)}, u32[]{:S(2)}) collective-permute-start(bf16[264,128]{1,0:T(8,128)(2,1)} %pack.1.refs_0_), channel_id=1, source_target_pairs={{12,0},{13,1},{14,2},{15,3},{0,4},{1,5},{2,6},{3,7},{4,8},{5,9},{6... | collective-permute-start | bytes 202760 | tf_op jit(solution)/shard_map/ppermute | solution.py:236
  9.9 7.5 %collective-permute-start.1 = (bf16[264,128]{1,0:T(8,128)(2,1)}, bf16[264,128]{1,0:T(8,128)(2,1)S(1)}, u32[]{:S(2)}, u32[]{:S(2)}) collective-permute-start(bf16[264,128]{1,0:T(8,128)(2,1)} %pack.1.refs_0_), channel_id=1, source_target_pairs={{8,0},{9,1},{10,2},{11,3},{12,4},{13,5},{14,6},{15,7},{0,8},{1,9},... | collective-permute-start | bytes 202760 | tf_op jit(solution)/shard_map/ppermute | solution.py:236
  10.2 7.2 %collective-permute-start.2 = (bf16[264,128]{1,0:T(8,128)(2,1)}, bf16[264,128]{1,0:T(8,128)(2,1)S(1)}, u32[]{:S(2)}, u32[]{:S(2)}) collective-permute-start(bf16[264,128]{1,0:T(8,128)(2,1)} %pack.1.refs_0_), channel_id=1, source_target_pairs={{4,0},{5,1},{6,2},{7,3},{8,4},{9,5},{10,6},{11,7},{12,8},{13,9},{1... | collective-permute-start | bytes 202760 | tf_op jit(solution)/shard_map/ppermute | solution.py:236
  13.9 6.7 %collective-permute-start.9 = (bf16[512,256]{1,0:T(8,128)(2,1)S(1)}, bf16[512,256]{1,0:T(8,128)(2,1)S(1)}, u32[]{:S(2)}, u32[]{:S(2)}) collective-permute-start(bf16[512,256]{1,0:T(8,128)(2,1)S(1)} %pad_maximum_fusion.refs_5_), channel_id=1, source_target_pairs={{2,0},{3,1},{0,2},{1,3},{6,4},{7,5},{4,6},{5,7},{10,8},{11,9},{8,1... | collective-permute-start | bytes 786440 | tf_op jit(solution)/shard_map/ppermute | solution.py:236
  15.4 12.0 %collective-permute-start.10 = (bf16[512,256]{1,0:T(8,128)(2,1)S(1)}, bf16[512,256]{1,0:T(8,128)(2,1)S(1)}, u32[]{:S(2)}, u32[]{:S(2)}) collective-permute-start(bf16[512,256]{1,0:T(8,128)(2,1)S(1)} %pad_maximum_fusion.refs_5_), channel_id=1, source_target_pairs={{0,1},{1,0},{2,3},{3,2},{4,5},{5,4},{6,7},{7,6},{8,9},{9,8},{10,11... | collective-permute-start | bytes 786440 | tf_op jit(solution)/shard_map/ppermute | solution.py:232
  17.4 0.9 %copy-start = (bf16[264,128]{1,0:T(8,128)(2,1)S(1)}, bf16[264,128]{1,0:T(8,128)(2,1)}, u32[]{:S(2)}) copy-start(bf16[264,128]{1,0:T(8,128)(2,1)} %pack.1.refs_0_) | copy-start | bytes 202756
  18.2 0.8 %copy-start.2 = (bf16[128,256]{1,0:T(8,128)(2,1)S(1)}, bf16[128,256]{1,0:T(8,128)(2,1)}, u32[]{:S(2)}) copy-start(bf16[128,256]{1,0:T(8,128)(2,1)} %refs_5_.1) | copy-start | bytes 196612
  19.1 8.4 %copy-start.1 = (f32[256]{0:T(256)S(1)}, f32[256]{0:T(256)}, u32[]{:S(2)}) copy-start(f32[256]{0:T(256)} %param.12) | copy-start | bytes 3076
  20.1 22.3 %copy-start.3 = (bf16[128,256]{1,0:T(8,128)(2,1)S(1)}, bf16[128,256]{1,0:T(8,128)(2,1)}, u32[]{:S(2)}) copy-start(bf16[128,256]{1,0:T(8,128)(2,1)} %refs_5_.1) | copy-start | bytes 196612
  20.6 6.8 %collective-permute-start.11 = (bf16[512,256]{1,0:T(8,128)(2,1)S(1)}, bf16[512,256]{1,0:T(8,128)(2,1)S(1)}, u32[]{:S(2)}, u32[]{:S(2)}) collective-permute-start(bf16[512,256]{1,0:T(8,128)(2,1)S(1)} %collective-permute-done.9.refs_6_), channel_id=1, source_target_pairs={{0,1},{1,0},{2,3},{3,2},{4,5},{5,4},{6,7},{7,6},{8,9},{9,8},{10,11... | collective-permute-start | bytes 786440 | tf_op jit(solution)/shard_map/ppermute | solution.py:232
  20.6 4.5 %collective-permute-start.3 = (bf16[128,256]{1,0:T(8,128)(2,1)S(1)}, bf16[128,256]{1,0:T(8,128)(2,1)S(1)}, u32[]{:S(2)}, u32[]{:S(2)}) collective-permute-start(bf16[128,256]{1,0:T(8,128)(2,1)S(1)} %get-tuple-element.19.refs_1_), channel_id=1, source_target_pairs={{2,0},{3,1},{0,2},{1,3},{6,4},{7,5},{4,6},{5,7},{10,8},{11,9},{8,1... | collective-permute-start | bytes 196616 | tf_op jit(solution)/shard_map/ppermute | solution.py:236
  22.1 4.9 %collective-permute-start.4 = (bf16[128,256]{1,0:T(8,128)(2,1)S(1)}, bf16[128,256]{1,0:T(8,128)(2,1)S(1)}, u32[]{:S(2)}, u32[]{:S(2)}) collective-permute-start(bf16[128,256]{1,0:T(8,128)(2,1)S(1)} %get-tuple-element.20), channel_id=1, source_target_pairs={{0,1},{1,0},{2,3},{3,2},{4,5},{5,4},{6,7},{7,6},{8,9},{9,8},{10,11... | collective-permute-start | bytes 196616 | tf_op jit(solution)/shard_map/ppermute | solution.py:232
  22.3 4.7 %collective-permute-start.5 = (bf16[128,256]{1,0:T(8,128)(2,1)S(1)}, bf16[128,256]{1,0:T(8,128)(2,1)S(1)}, u32[]{:S(2)}, u32[]{:S(2)}) collective-permute-start(bf16[128,256]{1,0:T(8,128)(2,1)S(1)} %get-tuple-element.20), channel_id=1, source_target_pairs={{3,0},{2,1},{1,2},{0,3},{7,4},{6,5},{5,6},{4,7},{11,8},{10,9},{9,1... | collective-permute-start | bytes 196616 | tf_op jit(solution)/shard_map/ppermute | solution.py:246
  25.1 17.3 %collective-permute-start.13 = (bf16[1056,128]{1,0:T(8,128)(2,1)S(1)}, bf16[1056,128]{1,0:T(8,128)(2,1)S(1)}, u32[]{:S(2)}, u32[]{:S(2)}) collective-permute-start(bf16[1056,128]{1,0:T(8,128)(2,1)S(1)} %get-tuple-element.26.refs_1_), channel_id=1, source_target_pairs={{2,0},{3,1},{0,2},{1,3},{6,4},{7,5},{4,6},{5,7},{10,8},{11,9},{8,1... | collective-permute-start | bytes 811016 | tf_op jit(solution)/shard_map/ppermute | solution.py:236
  27.0 15.4 %collective-permute-start.14 = (bf16[1056,128]{1,0:T(8,128)(2,1)S(1)}, bf16[1056,128]{1,0:T(8,128)(2,1)S(1)}, u32[]{:S(2)}, u32[]{:S(2)}) collective-permute-start(bf16[1056,128]{1,0:T(8,128)(2,1)S(1)} %get-tuple-element.26.refs_1_), channel_id=1, source_target_pairs={{0,1},{1,0},{2,3},{3,2},{4,5},{5,4},{6,7},{7,6},{8,9},{9,8},{10,11... | collective-permute-start | bytes 811016 | tf_op jit(solution)/shard_map/ppermute | solution.py:232
  27.0 15.4 %collective-permute-start.15 = (bf16[1056,128]{1,0:T(8,128)(2,1)S(1)}, bf16[1056,128]{1,0:T(8,128)(2,1)S(1)}, u32[]{:S(2)}, u32[]{:S(2)}) collective-permute-start(bf16[1056,128]{1,0:T(8,128)(2,1)S(1)} %get-tuple-element.26.refs_1_), channel_id=1, source_target_pairs={{3,0},{2,1},{1,2},{0,3},{7,4},{6,5},{5,6},{4,7},{11,8},{10,9},{9,1... | collective-permute-start | bytes 811016 | tf_op jit(solution)/shard_map/ppermute | solution.py:246
  42.0 4.4 %collective-permute-start.12 = (f32[256,512]{1,0:T(8,128)S(1)}, f32[256,512]{1,0:T(8,128)S(1)}, u32[]{:S(2)}, u32[]{:S(2)}) collective-permute-start(f32[256,512]{1,0:T(8,128)S(1)} %get-tuple-element.25), channel_id=1, source_target_pairs={{0,1},{1,0},{2,3},{3,2},{4,5},{5,4},{6,7},{7,6},{8,9},{9,8},{10,11... | collective-permute-start | bytes 1572872 | tf_op jit(solution)/shard_map/ppermute | solution.py:232
  44.9 1.4 %collective-permute-start.16 = (f32[136,256]{1,0:T(8,128)S(1)}, f32[136,256]{1,0:T(8,128)S(1)}, u32[]{:S(2)}, u32[]{:S(2)}) collective-permute-start(f32[136,256]{1,0:T(8,128)S(1)} %first.1.first_ref), channel_id=1, source_target_pairs={{0,1},{1,0},{2,3},{3,2},{4,5},{5,4},{6,7},{7,6},{8,9},{9,8},{10,11... | collective-permute-start | bytes 417800 | tf_op jit(solution)/shard_map/ppermute | solution.py:232

commit v6 on v5

--- a/solution.py
+++ b/solution.py
@@ -124,9 +124,9 @@
     mb = 512
     square_ref[...] = jnp.zeros_like(square_ref)
 
-    def product(i, carry):
+    for i in range(2 * (n_rows // mb)):
         par, b = i // (n_rows // mb), i % (n_rows // mb)
-        at = pl.multiple_of(b * mb, mb)
+        at = b * mb
         r_h = dot(x_ref[par, pl.ds(at, mb), :], c_ref[par], (1, 0))
         r_s = dot(x_ref[par, pl.ds(n_rows + at, mb), :], c_ref[par], (1, 0))
         res = r_h - r_s * energies
@@ -134,9 +134,6 @@
         g_ref[0, par, pl.ds(at, mb), :] = (res / total_blocks).astype(BF16)
         g_ref[1, par, pl.ds(at, mb), :] = (-(res * energies) / total_blocks).astype(BF16)
         square_ref[...] += jnp.sum((res * res).reshape(mb // 8, 8, columns), axis=0)
-        return carry
-
-    lax.fori_loop(0, 2 * (n_rows // mb), product, 0)
 
     blk_dev = res_ref.shape[0]
     for i in range(blk_dev):

time: 47.6 us -> 45.9 us (0.964)
  Pallas kernels: 20.5 us -> 18.8 us
    pallas_call x1, Pallas kernels: 14.5 us -> 12.9 us  [near(): pl.pallas_call(functools.partial(main_kernel, chips=chips, z_count=z_coun...]
  transfers between devices with their start and end apart: 17 -> 17, of which waited for: 5 -> 5; matrix products, arithmetic and copies ran while one was open for 2% -> 2% of each run, Pallas kernels for 41% -> 39%
where the time goes in v6:
time: 45.9 us; the launch traced here: 45.6 us
  Pallas kernels  18.8 us (41%)
  starting transfers between devices  17.5 us (38%)
  waiting for transfers between devices  5.97 us (13%)
  local copies, waits for them, and re-layouts  1.73 us (4%)
  other arithmetic  0.86 us (2%)
  between operations  0.7 us (2%)
    ppermute x9, starting transfers between devices, from_chip(): return lax.ppermute(v, 'blk', sends) if m else v  15.8 us
    pallas_call x1, Pallas kernels, near(): pl.pallas_call(functools.partial(main_kernel, chips=chips, z_count=z_coun...  12.9 us
    ppermute x9, waiting for transfers between devices, from_chip(): return lax.ppermute(v, 'blk', sends) if m else v  4.81 us
    pallas_call x1, Pallas kernels, near(): pl.pallas_call(functools.partial(first_kernel, chips=chips, z_count=z_cou...  2.55 us
    unnamed x8, local copies, waits for them, and re-layouts  1.73 us
    pallas_call x1, Pallas kernels, near(): pl.pallas_call(functools.partial(pack_kernel, rs=rs, blk_dev=blk_dev), ou...  1.54 us
    ppermute x6, waiting for transfers between devices, to_core(): return lax.ppermute(v, 'blk', [(i, i ^ 1) for i in range(n_dev)])  1.16 us
    pallas_call x1, Pallas kernels, near(): pl.pallas_call(functools.partial(group_kernel, rs=rs, pairs=pairs, orbita...  0.97 us
  transfers between devices with their start and end apart: 17, of which 5 were waited for; matrix products, arithmetic and copies ran while one was open for 2% of the time, Pallas kernels for 39%

profile of v6, /device:TPU:0, one launch (start us, length us, event | category | flops | bytes accessed | tf_op | source)
XLA Modules:
  0.0 45.6 jit_solution(1265887368088436511)
XLA Ops:
  0.6 3.1 %collective-permute-start.6 = (bf16[128,256]{1,0:T(8,128)(2,1)}, bf16[128,256]{1,0:T(8,128)(2,1)S(1)}, u32[]{:S(2)}, u32[]{:S(2)}) collective-permute-start(bf16[128,256]{1,0:T(8,128)(2,1)} %bitcast.8), channel_id=1, source_target_pairs={{12,0},{13,1},{14,2},{15,3},{0,4},{1,5},{2,6},{3,7},{4,8},{5,9},{6... | collective-permute-start | bytes 196616 | tf_op jit(solution)/shard_map/ppermute | solution.py:233
  3.7 2.6 %collective-permute-start.7 = (bf16[128,256]{1,0:T(8,128)(2,1)}, bf16[128,256]{1,0:T(8,128)(2,1)S(1)}, u32[]{:S(2)}, u32[]{:S(2)}) collective-permute-start(bf16[128,256]{1,0:T(8,128)(2,1)} %bitcast.9), channel_id=1, source_target_pairs={{8,0},{9,1},{10,2},{11,3},{12,4},{13,5},{14,6},{15,7},{0,8},{1,9},... | collective-permute-start | bytes 196616 | tf_op jit(solution)/shard_map/ppermute | solution.py:233
  6.3 1.3 %collective-permute-start.8 = (bf16[128,256]{1,0:T(8,128)(2,1)}, bf16[128,256]{1,0:T(8,128)(2,1)S(1)}, u32[]{:S(2)}, u32[]{:S(2)}) collective-permute-start(bf16[128,256]{1,0:T(8,128)(2,1)} %bitcast.10), channel_id=1, source_target_pairs={{4,0},{5,1},{6,2},{7,3},{8,4},{9,5},{10,6},{11,7},{12,8},{13,9},{1... | collective-permute-start | bytes 196616 | tf_op jit(solution)/shard_map/ppermute | solution.py:233
  7.6 1.5 %pack.1.refs_0_ = bf16[264,128]{1,0:T(8,128)(2,1)} custom-call(s32[1,256]{1,0:T(1,128)} %bitcast.12, s32[1,256]{1,0:T(1,128)} %bitcast.13, s32[1,256]{1,0:T(1,128)} %bitcast.14, bf16[256,128]{1,0:T(8,128)(2,1)} %feats_ref.1), custom_call_target="tpu_custom_call" | custom-call | bytes 1048576 | tf_op jit(solution)/shard_map/pack/pallas_call | solution.py:235
  9.2 0.7 %collective-permute-start = (bf16[264,128]{1,0:T(8,128)(2,1)}, bf16[264,128]{1,0:T(8,128)(2,1)S(1)}, u32[]{:S(2)}, u32[]{:S(2)}) collective-permute-start(bf16[264,128]{1,0:T(8,128)(2,1)} %pack.1.refs_0_), channel_id=1, source_target_pairs={{12,0},{13,1},{14,2},{15,3},{0,4},{1,5},{2,6},{3,7},{4,8},{5,9},{6... | collective-permute-start | bytes 202760 | tf_op jit(solution)/shard_map/ppermute | solution.py:233
  9.9 0.3 collective-permute-start.1
  10.2 0.0 collective-permute-done.6
  10.2 2.8 %collective-permute-start.2 = (bf16[264,128]{1,0:T(8,128)(2,1)}, bf16[264,128]{1,0:T(8,128)(2,1)S(1)}, u32[]{:S(2)}, u32[]{:S(2)}) collective-permute-start(bf16[264,128]{1,0:T(8,128)(2,1)} %pack.1.refs_0_), channel_id=1, source_target_pairs={{4,0},{5,1},{6,2},{7,3},{8,4},{9,5},{10,6},{11,7},{12,8},{13,9},{1... | collective-permute-start | bytes 202760 | tf_op jit(solution)/shard_map/ppermute | solution.py:233
  13.0 0.0 collective-permute-done.7
  13.0 0.9 %pad_maximum_fusion.refs_5_ = bf16[512,256]{1,0:T(8,128)(2,1)S(1)} fusion(bf16[128,256]{1,0:T(8,128)(2,1)S(1)} %collective-permute-done.8, bf16[128,256]{1,0:T(8,128)(2,1)S(1)} %collective-permute-done.7, bf16[128,256]{1,0:T(8,128)(2,1)S(1)} %collective-permute-done.6, bf16[128,256]{1,0:T(8,128)(2,1)} %bitcast.11), kind=kLoop, calls=%fused_computation | loop fusion | flops 1048576 | bytes 524288 | tf_op jit(solution)/shard_map/concatenate | solution.py:249
  13.9 1.6 %collective-permute-start.9 = (bf16[512,256]{1,0:T(8,128)(2,1)S(1)}, bf16[512,256]{1,0:T(8,128)(2,1)S(1)}, u32[]{:S(2)}, u32[]{:S(2)}) collective-permute-start(bf16[512,256]{1,0:T(8,128)(2,1)S(1)} %pad_maximum_fusion.refs_5_), channel_id=1, source_target_pairs={{2,0},{3,1},{0,2},{1,3},{6,4},{7,5},{4,6},{5,7},{10,8},{11,9},{8,1... | collective-permute-start | bytes 786440 | tf_op jit(solution)/shard_map/ppermute | solution.py:233
  15.4 0.4 collective-permute-done.refs_1_
  15.9 1.5 %collective-permute-done.1.refs_2_ = bf16[264,128]{1,0:T(8,128)(2,1)S(1)} collective-permute-done((bf16[264,128]{1,0:T(8,128)(2,1)}, bf16[264,128]{1,0:T(8,128)(2,1)S(1)}, u32[]{:S(2)}, u32[]{:S(2)}) %collective-permute-start.1) | collective-permute-done | bytes 67616 | tf_op jit(solution)/shard_map/ppermute | solution.py:233
  17.4 0.9 %copy-done = bf16[264,128]{1,0:T(8,128)(2,1)S(1)} copy-done((bf16[264,128]{1,0:T(8,128)(2,1)S(1)}, bf16[264,128]{1,0:T(8,128)(2,1)}, u32[]{:S(2)}) %copy-start) | copy-done | bytes 67608
  18.2 0.8 %copy-done.2 = bf16[128,256]{1,0:T(8,128)(2,1)S(1)} copy-done((bf16[128,256]{1,0:T(8,128)(2,1)S(1)}, bf16[128,256]{1,0:T(8,128)(2,1)}, u32[]{:S(2)}) %copy-start.2) | copy-done | bytes 65560
  19.1 1.0 %group.1 = (bf16[128,256]{1,0:T(8,128)(2,1)S(1)}, bf16[128,256]{1,0:T(8,128)(2,1)S(1)}, bf16[1056,128]{1,0:T(8,128)(2,1)S(1)}) custom-call(s32[1]{0:T(128)} %bitcast.me_ref.refs_0_, bf16[264,128]{1,0:T(8,128)(2,1)S(1)} %copy-done, bf16[264,128]{1,0:T(8,128)(2,1)S(1)} %collective-permute-done.refs_1_, bf16[264,128]{1,0:T(8,128)(2,1)S(1)} %collective-permute-done.1.refs_2_, ...), custom_call_target="tpu_custom_call" | custom-call | flops 17179869184 | bytes 2097152 | tf_op jit(solution)/shard_map/group/pallas_call | solution.py:251
  20.1 0.0 copy-start.3
  20.1 0.5 %collective-permute-done.9.refs_6_ = bf16[512,256]{1,0:T(8,128)(2,1)S(1)} collective-permute-done((bf16[512,256]{1,0:T(8,128)(2,1)S(1)}, bf16[512,256]{1,0:T(8,128)(2,1)S(1)}, u32[]{:S(2)}, u32[]{:S(2)}) %collective-permute-start.9) | collective-permute-done | bytes 262176 | tf_op jit(solution)/shard_map/ppermute | solution.py:233
  20.6 1.5 %collective-permute-start.3 = (bf16[128,256]{1,0:T(8,128)(2,1)S(1)}, bf16[128,256]{1,0:T(8,128)(2,1)S(1)}, u32[]{:S(2)}, u32[]{:S(2)}) collective-permute-start(bf16[128,256]{1,0:T(8,128)(2,1)S(1)} %get-tuple-element.19.refs_1_), channel_id=1, source_target_pairs={{2,0},{3,1},{0,2},{1,3},{6,4},{7,5},{4,6},{5,7},{10,8},{11,9},{8,1... | collective-permute-start | bytes 196616 | tf_op jit(solution)/shard_map/ppermute | solution.py:233
  22.1 0.2 collective-permute-start.4
  22.3 0.4 collective-permute-start.5
  22.7 2.4 %collective-permute-done.3.refs_2_ = bf16[128,256]{1,0:T(8,128)(2,1)S(1)} collective-permute-done((bf16[128,256]{1,0:T(8,128)(2,1)S(1)}, bf16[128,256]{1,0:T(8,128)(2,1)S(1)}, u32[]{:S(2)}, u32[]{:S(2)}) %collective-permute-start.3) | collective-permute-done | bytes 65568 | tf_op jit(solution)/shard_map/ppermute | solution.py:233
  25.1 1.9 %collective-permute-start.13 = (bf16[1056,128]{1,0:T(8,128)(2,1)S(1)}, bf16[1056,128]{1,0:T(8,128)(2,1)S(1)}, u32[]{:S(2)}, u32[]{:S(2)}) collective-permute-start(bf16[1056,128]{1,0:T(8,128)(2,1)S(1)} %get-tuple-element.26.refs_1_), channel_id=1, source_target_pairs={{2,0},{3,1},{0,2},{1,3},{6,4},{7,5},{4,6},{5,7},{10,8},{11,9},{8,1... | collective-permute-start | bytes 811016 | tf_op jit(solution)/shard_map/ppermute | solution.py:233
  27.0 0.0 collective-permute-start.14
  27.0 0.0 collective-permute-done.5.refs_4_
  27.0 0.4 collective-permute-start.15
  27.4 12.9 %step.1 = (f32[2,64,256]{2,1,0:T(8,128)}, f32[256,512]{1,0:T(8,128)S(1)}, f32[256,512]{1,0:T(8,128)S(1)}, f32[2,256,256]{2,1,0:T(8,128)S(1)}, f32[8,256]{1,0:T(8,128)S(1)}) custom-call(s32[1]{0:T(128)} %bitcast.me_ref.refs_0_, bf16[128,256]{1,0:T(8,128)(2,1)S(1)} %get-tuple-element.19.refs_1_, bf16[128,256]{1,0:T(8,128)(2,1)S(1)} %collective-permute-done.3.refs_2_, ...), custom_call_target="tpu_custom_call" | custom-call | flops 536870912 | bytes 1048576 | tf_op jit(solution)/shard_map/step/pallas_call | solution.py:271
  40.3 0.4 collective-permute-start.12
  40.7 2.5 %first.1.first_ref = f32[136,256]{1,0:T(8,128)S(1)} custom-call(s32[1]{0:T(128)} %bitcast.me_ref.refs_0_, bf16[1056,128]{1,0:T(8,128)(2,1)S(1)} %get-tuple-element.26.refs_1_, bf16[1056,128]{1,0:T(8,128)(2,1)S(1)} %collective-permute-done.13.refs_2_, bf16[1056,128]{1,0:T(8,128)(2,1)S(1)} %collective-permute-done.14.refs_3_, ...), custom_call_target="tpu_custom_call" | custom-call | flops 2147483648 | bytes 4194304 | tf_op jit(solution)/shard_map/first/pallas_call | solution.py:298
  43.3 0.3 collective-permute-start.16
  43.5 1.1 %collective-permute-done.16.got_ref = f32[136,256]{1,0:T(8,128)S(1)} collective-permute-done((f32[136,256]{1,0:T(8,128)S(1)}, f32[136,256]{1,0:T(8,128)S(1)}, u32[]{:S(2)}, u32[]{:S(2)}) %collective-permute-start.16) | collective-permute-done | bytes 139296 | tf_op jit(solution)/shard_map/ppermute | solution.py:229
  44.7 0.9 %combine.1 = (f32[256,512]{1,0:T(8,128)}, f32[128,256]{1,0:T(8,128)}, f32[1,1]{1,0:T(1,128)}) custom-call(f32[256,512]{1,0:T(8,128)S(1)} %get-tuple-element.24.keep_ref, f32[256,512]{1,0:T(8,128)S(1)} %collective-permute-done.12.sent_ref, f32[136,256]{1,0:T(8,128)S(1)} %first.1.first_ref, f32[136,256]{1,0:T(8,128)S(1)} %collective-permute-done.16.got_ref), custom_call_target="tpu_custom_call" | custom-call | tf_op jit(solution)/shard_map/combine/pallas_call | solution.py:308
  (16 shorter events, 0.0 us)
Async XLA Ops:
  0.6 9.6 %collective-permute-start.6 = (bf16[128,256]{1,0:T(8,128)(2,1)}, bf16[128,256]{1,0:T(8,128)(2,1)S(1)}, u32[]{:S(2)}, u32[]{:S(2)}) collective-permute-start(bf16[128,256]{1,0:T(8,128)(2,1)} %bitcast.8), channel_id=1, source_target_pairs={{12,0},{13,1},{14,2},{15,3},{0,4},{1,5},{2,6},{3,7},{4,8},{5,9},{6... | collective-permute-start | bytes 196616 | tf_op jit(solution)/shard_map/ppermute | solution.py:233
  3.7 9.3 %collective-permute-start.7 = (bf16[128,256]{1,0:T(8,128)(2,1)}, bf16[128,256]{1,0:T(8,128)(2,1)S(1)}, u32[]{:S(2)}, u32[]{:S(2)}) collective-permute-start(bf16[128,256]{1,0:T(8,128)(2,1)} %bitcast.9), channel_id=1, source_target_pairs={{8,0},{9,1},{10,2},{11,3},{12,4},{13,5},{14,6},{15,7},{0,8},{1,9},... | collective-permute-start | bytes 196616 | tf_op jit(solution)/shard_map/ppermute | solution.py:233
  6.3 6.7 %collective-permute-start.8 = (bf16[128,256]{1,0:T(8,128)(2,1)}, bf16[128,256]{1,0:T(8,128)(2,1)S(1)}, u32[]{:S(2)}, u32[]{:S(2)}) collective-permute-start(bf16[128,256]{1,0:T(8,128)(2,1)} %bitcast.10), channel_id=1, source_target_pairs={{4,0},{5,1},{6,2},{7,3},{8,4},{9,5},{10,6},{11,7},{12,8},{13,9},{1... | collective-permute-start | bytes 196616 | tf_op jit(solution)/shard_map/ppermute | solution.py:233
  9.2 6.7 %collective-permute-start = (bf16[264,128]{1,0:T(8,128)(2,1)}, bf16[264,128]{1,0:T(8,128)(2,1)S(1)}, u32[]{:S(2)}, u32[]{:S(2)}) collective-permute-start(bf16[264,128]{1,0:T(8,128)(2,1)} %pack.1.refs_0_), channel_id=1, source_target_pairs={{12,0},{13,1},{14,2},{15,3},{0,4},{1,5},{2,6},{3,7},{4,8},{5,9},{6... | collective-permute-start | bytes 202760 | tf_op jit(solution)/shard_map/ppermute | solution.py:233
  9.9 7.5 %collective-permute-start.1 = (bf16[264,128]{1,0:T(8,128)(2,1)}, bf16[264,128]{1,0:T(8,128)(2,1)S(1)}, u32[]{:S(2)}, u32[]{:S(2)}) collective-permute-start(bf16[264,128]{1,0:T(8,128)(2,1)} %pack.1.refs_0_), channel_id=1, source_target_pairs={{8,0},{9,1},{10,2},{11,3},{12,4},{13,5},{14,6},{15,7},{0,8},{1,9},... | collective-permute-start | bytes 202760 | tf_op jit(solution)/shard_map/ppermute | solution.py:233
  10.2 7.2 %collective-permute-start.2 = (bf16[264,128]{1,0:T(8,128)(2,1)}, bf16[264,128]{1,0:T(8,128)(2,1)S(1)}, u32[]{:S(2)}, u32[]{:S(2)}) collective-permute-start(bf16[264,128]{1,0:T(8,128)(2,1)} %pack.1.refs_0_), channel_id=1, source_target_pairs={{4,0},{5,1},{6,2},{7,3},{8,4},{9,5},{10,6},{11,7},{12,8},{13,9},{1... | collective-permute-start | bytes 202760 | tf_op jit(solution)/shard_map/ppermute | solution.py:233
  13.9 6.7 %collective-permute-start.9 = (bf16[512,256]{1,0:T(8,128)(2,1)S(1)}, bf16[512,256]{1,0:T(8,128)(2,1)S(1)}, u32[]{:S(2)}, u32[]{:S(2)}) collective-permute-start(bf16[512,256]{1,0:T(8,128)(2,1)S(1)} %pad_maximum_fusion.refs_5_), channel_id=1, source_target_pairs={{2,0},{3,1},{0,2},{1,3},{6,4},{7,5},{4,6},{5,7},{10,8},{11,9},{8,1... | collective-permute-start | bytes 786440 | tf_op jit(solution)/shard_map/ppermute | solution.py:233
  15.4 12.0 %collective-permute-start.10 = (bf16[512,256]{1,0:T(8,128)(2,1)S(1)}, bf16[512,256]{1,0:T(8,128)(2,1)S(1)}, u32[]{:S(2)}, u32[]{:S(2)}) collective-permute-start(bf16[512,256]{1,0:T(8,128)(2,1)S(1)} %pad_maximum_fusion.refs_5_), channel_id=1, source_target_pairs={{0,1},{1,0},{2,3},{3,2},{4,5},{5,4},{6,7},{7,6},{8,9},{9,8},{10,11... | collective-permute-start | bytes 786440 | tf_op jit(solution)/shard_map/ppermute | solution.py:229
  17.4 0.9 %copy-start = (bf16[264,128]{1,0:T(8,128)(2,1)S(1)}, bf16[264,128]{1,0:T(8,128)(2,1)}, u32[]{:S(2)}) copy-start(bf16[264,128]{1,0:T(8,128)(2,1)} %pack.1.refs_0_) | copy-start | bytes 202756
  18.2 0.8 %copy-start.2 = (bf16[128,256]{1,0:T(8,128)(2,1)S(1)}, bf16[128,256]{1,0:T(8,128)(2,1)}, u32[]{:S(2)}) copy-start(bf16[128,256]{1,0:T(8,128)(2,1)} %refs_5_.1) | copy-start | bytes 196612
  19.1 8.4 %copy-start.1 = (f32[256]{0:T(256)S(1)}, f32[256]{0:T(256)}, u32[]{:S(2)}) copy-start(f32[256]{0:T(256)} %param.12) | copy-start | bytes 3076
  20.1 20.6 %copy-start.3 = (bf16[128,256]{1,0:T(8,128)(2,1)S(1)}, bf16[128,256]{1,0:T(8,128)(2,1)}, u32[]{:S(2)}) copy-start(bf16[128,256]{1,0:T(8,128)(2,1)} %refs_5_.1) | copy-start | bytes 196612
  20.6 6.8 %collective-permute-start.11 = (bf16[512,256]{1,0:T(8,128)(2,1)S(1)}, bf16[512,256]{1,0:T(8,128)(2,1)S(1)}, u32[]{:S(2)}, u32[]{:S(2)}) collective-permute-start(bf16[512,256]{1,0:T(8,128)(2,1)S(1)} %collective-permute-done.9.refs_6_), channel_id=1, source_target_pairs={{0,1},{1,0},{2,3},{3,2},{4,5},{5,4},{6,7},{7,6},{8,9},{9,8},{10,11... | collective-permute-start | bytes 786440 | tf_op jit(solution)/shard_map/ppermute | solution.py:229
  20.6 4.5 %collective-permute-start.3 = (bf16[128,256]{1,0:T(8,128)(2,1)S(1)}, bf16[128,256]{1,0:T(8,128)(2,1)S(1)}, u32[]{:S(2)}, u32[]{:S(2)}) collective-permute-start(bf16[128,256]{1,0:T(8,128)(2,1)S(1)} %get-tuple-element.19.refs_1_), channel_id=1, source_target_pairs={{2,0},{3,1},{0,2},{1,3},{6,4},{7,5},{4,6},{5,7},{10,8},{11,9},{8,1... | collective-permute-start | bytes 196616 | tf_op jit(solution)/shard_map/ppermute | solution.py:233
  22.1 4.9 %collective-permute-start.4 = (bf16[128,256]{1,0:T(8,128)(2,1)S(1)}, bf16[128,256]{1,0:T(8,128)(2,1)S(1)}, u32[]{:S(2)}, u32[]{:S(2)}) collective-permute-start(bf16[128,256]{1,0:T(8,128)(2,1)S(1)} %get-tuple-element.20), channel_id=1, source_target_pairs={{0,1},{1,0},{2,3},{3,2},{4,5},{5,4},{6,7},{7,6},{8,9},{9,8},{10,11... | collective-permute-start | bytes 196616 | tf_op jit(solution)/shard_map/ppermute | solution.py:229
  22.3 4.7 %collective-permute-start.5 = (bf16[128,256]{1,0:T(8,128)(2,1)S(1)}, bf16[128,256]{1,0:T(8,128)(2,1)S(1)}, u32[]{:S(2)}, u32[]{:S(2)}) collective-permute-start(bf16[128,256]{1,0:T(8,128)(2,1)S(1)} %get-tuple-element.20), channel_id=1, source_target_pairs={{3,0},{2,1},{1,2},{0,3},{7,4},{6,5},{5,6},{4,7},{11,8},{10,9},{9,1... | collective-permute-start | bytes 196616 | tf_op jit(solution)/shard_map/ppermute | solution.py:243
  25.1 15.6 %collective-permute-start.13 = (bf16[1056,128]{1,0:T(8,128)(2,1)S(1)}, bf16[1056,128]{1,0:T(8,128)(2,1)S(1)}, u32[]{:S(2)}, u32[]{:S(2)}) collective-permute-start(bf16[1056,128]{1,0:T(8,128)(2,1)S(1)} %get-tuple-element.26.refs_1_), channel_id=1, source_target_pairs={{2,0},{3,1},{0,2},{1,3},{6,4},{7,5},{4,6},{5,7},{10,8},{11,9},{8,1... | collective-permute-start | bytes 811016 | tf_op jit(solution)/shard_map/ppermute | solution.py:233
  27.0 13.7 %collective-permute-start.14 = (bf16[1056,128]{1,0:T(8,128)(2,1)S(1)}, bf16[1056,128]{1,0:T(8,128)(2,1)S(1)}, u32[]{:S(2)}, u32[]{:S(2)}) collective-permute-start(bf16[1056,128]{1,0:T(8,128)(2,1)S(1)} %get-tuple-element.26.refs_1_), channel_id=1, source_target_pairs={{0,1},{1,0},{2,3},{3,2},{4,5},{5,4},{6,7},{7,6},{8,9},{9,8},{10,11... | collective-permute-start | bytes 811016 | tf_op jit(solution)/shard_map/ppermute | solution.py:229
  27.0 13.7 %collective-permute-start.15 = (bf16[1056,128]{1,0:T(8,128)(2,1)S(1)}, bf16[1056,128]{1,0:T(8,128)(2,1)S(1)}, u32[]{:S(2)}, u32[]{:S(2)}) collective-permute-start(bf16[1056,128]{1,0:T(8,128)(2,1)S(1)} %get-tuple-element.26.refs_1_), channel_id=1, source_target_pairs={{3,0},{2,1},{1,2},{0,3},{7,4},{6,5},{5,6},{4,7},{11,8},{10,9},{9,1... | collective-permute-start | bytes 811016 | tf_op jit(solution)/shard_map/ppermute | solution.py:243
  40.3 4.4 %collective-permute-start.12 = (f32[256,512]{1,0:T(8,128)S(1)}, f32[256,512]{1,0:T(8,128)S(1)}, u32[]{:S(2)}, u32[]{:S(2)}) collective-permute-start(f32[256,512]{1,0:T(8,128)S(1)} %get-tuple-element.25), channel_id=1, source_target_pairs={{0,1},{1,0},{2,3},{3,2},{4,5},{5,4},{6,7},{7,6},{8,9},{9,8},{10,11... | collective-permute-start | bytes 1572872 | tf_op jit(solution)/shard_map/ppermute | solution.py:229
  43.3 1.4 %collective-permute-start.16 = (f32[136,256]{1,0:T(8,128)S(1)}, f32[136,256]{1,0:T(8,128)S(1)}, u32[]{:S(2)}, u32[]{:S(2)}) collective-permute-start(f32[136,256]{1,0:T(8,128)S(1)} %first.1.first_ref), channel_id=1, source_target_pairs={{0,1},{1,0},{2,3},{3,2},{4,5},{5,4},{6,7},{7,6},{8,9},{9,8},{10,11... | collective-permute-start | bytes 417800 | tf_op jit(solution)/shard_map/ppermute | solution.py:229

commit v7 on v6

--- a/solution.py
+++ b/solution.py
@@ -121,7 +121,7 @@
 
     energies = energies_ref[...]
     n_rows = ah_count * rs
-    mb = 512
+    mb = 256
     square_ref[...] = jnp.zeros_like(square_ref)
 
     for i in range(2 * (n_rows // mb)):

time: 45.9 us -> 45.9 us (level)
  no operation moved by 1% of the time
where the time goes in v7:
time: 45.9 us; the launch traced here: 45.6 us
  Pallas kernels  18.8 us (41%)
  starting transfers between devices  17.5 us (38%)
  waiting for transfers between devices  5.97 us (13%)
  local copies, waits for them, and re-layouts  1.73 us (4%)
  other arithmetic  0.86 us (2%)
  between operations  0.7 us (2%)
    ppermute x9, starting transfers between devices, from_chip(): return lax.ppermute(v, 'blk', sends) if m else v  15.8 us
    pallas_call x1, Pallas kernels, near(): pl.pallas_call(functools.partial(main_kernel, chips=chips, z_count=z_coun...  12.9 us
    ppermute x9, waiting for transfers between devices, from_chip(): return lax.ppermute(v, 'blk', sends) if m else v  4.81 us
    pallas_call x1, Pallas kernels, near(): pl.pallas_call(functools.partial(first_kernel, chips=chips, z_count=z_cou...  2.55 us
    unnamed x8, local copies, waits for them, and re-layouts  1.73 us
    pallas_call x1, Pallas kernels, near(): pl.pallas_call(functools.partial(pack_kernel, rs=rs, blk_dev=blk_dev), ou...  1.54 us
    ppermute x6, waiting for transfers between devices, to_core(): return lax.ppermute(v, 'blk', [(i, i ^ 1) for i in range(n_dev)])  1.16 us
    pallas_call x1, Pallas kernels, near(): pl.pallas_call(functools.partial(group_kernel, rs=rs, pairs=pairs, orbita...  0.97 us
  transfers between devices with their start and end apart: 17, of which 5 were waited for; matrix products, arithmetic and copies ran while one was open for 2% of the time, Pallas kernels for 39%

profile of v7, /device:TPU:0, one launch (start us, length us, event | category | flops | bytes accessed | tf_op | source)
XLA Modules:
  0.0 45.6 jit_solution(18282839481341161155)
XLA Ops:
  0.6 3.1 %collective-permute-start.6 = (bf16[128,256]{1,0:T(8,128)(2,1)}, bf16[128,256]{1,0:T(8,128)(2,1)S(1)}, u32[]{:S(2)}, u32[]{:S(2)}) collective-permute-start(bf16[128,256]{1,0:T(8,128)(2,1)} %bitcast.8), channel_id=1, source_target_pairs={{12,0},{13,1},{14,2},{15,3},{0,4},{1,5},{2,6},{3,7},{4,8},{5,9},{6... | collective-permute-start | bytes 196616 | tf_op jit(solution)/shard_map/ppermute | solution.py:233
  3.7 2.6 %collective-permute-start.7 = (bf16[128,256]{1,0:T(8,128)(2,1)}, bf16[128,256]{1,0:T(8,128)(2,1)S(1)}, u32[]{:S(2)}, u32[]{:S(2)}) collective-permute-start(bf16[128,256]{1,0:T(8,128)(2,1)} %bitcast.9), channel_id=1, source_target_pairs={{8,0},{9,1},{10,2},{11,3},{12,4},{13,5},{14,6},{15,7},{0,8},{1,9},... | collective-permute-start | bytes 196616 | tf_op jit(solution)/shard_map/ppermute | solution.py:233
  6.3 1.3 %collective-permute-start.8 = (bf16[128,256]{1,0:T(8,128)(2,1)}, bf16[128,256]{1,0:T(8,128)(2,1)S(1)}, u32[]{:S(2)}, u32[]{:S(2)}) collective-permute-start(bf16[128,256]{1,0:T(8,128)(2,1)} %bitcast.10), channel_id=1, source_target_pairs={{4,0},{5,1},{6,2},{7,3},{8,4},{9,5},{10,6},{11,7},{12,8},{13,9},{1... | collective-permute-start | bytes 196616 | tf_op jit(solution)/shard_map/ppermute | solution.py:233
  7.6 1.5 %pack.1.refs_0_ = bf16[264,128]{1,0:T(8,128)(2,1)} custom-call(s32[1,256]{1,0:T(1,128)} %bitcast.12, s32[1,256]{1,0:T(1,128)} %bitcast.13, s32[1,256]{1,0:T(1,128)} %bitcast.14, bf16[256,128]{1,0:T(8,128)(2,1)} %feats_ref.1), custom_call_target="tpu_custom_call" | custom-call | bytes 1048576 | tf_op jit(solution)/shard_map/pack/pallas_call | solution.py:235
  9.2 0.7 %collective-permute-start = (bf16[264,128]{1,0:T(8,128)(2,1)}, bf16[264,128]{1,0:T(8,128)(2,1)S(1)}, u32[]{:S(2)}, u32[]{:S(2)}) collective-permute-start(bf16[264,128]{1,0:T(8,128)(2,1)} %pack.1.refs_0_), channel_id=1, source_target_pairs={{12,0},{13,1},{14,2},{15,3},{0,4},{1,5},{2,6},{3,7},{4,8},{5,9},{6... | collective-permute-start | bytes 202760 | tf_op jit(solution)/shard_map/ppermute | solution.py:233
  9.9 0.3 collective-permute-start.1
  10.2 0.0 collective-permute-done.6
  10.2 2.8 %collective-permute-start.2 = (bf16[264,128]{1,0:T(8,128)(2,1)}, bf16[264,128]{1,0:T(8,128)(2,1)S(1)}, u32[]{:S(2)}, u32[]{:S(2)}) collective-permute-start(bf16[264,128]{1,0:T(8,128)(2,1)} %pack.1.refs_0_), channel_id=1, source_target_pairs={{4,0},{5,1},{6,2},{7,3},{8,4},{9,5},{10,6},{11,7},{12,8},{13,9},{1... | collective-permute-start | bytes 202760 | tf_op jit(solution)/shard_map/ppermute | solution.py:233
  13.0 0.0 collective-permute-done.7
  13.0 0.0 collective-permute-done.8
  13.0 0.9 %pad_maximum_fusion.refs_5_ = bf16[512,256]{1,0:T(8,128)(2,1)S(1)} fusion(bf16[128,256]{1,0:T(8,128)(2,1)S(1)} %collective-permute-done.8, bf16[128,256]{1,0:T(8,128)(2,1)S(1)} %collective-permute-done.7, bf16[128,256]{1,0:T(8,128)(2,1)S(1)} %collective-permute-done.6, bf16[128,256]{1,0:T(8,128)(2,1)} %bitcast.11), kind=kLoop, calls=%fused_computation | loop fusion | flops 1048576 | bytes 524288 | tf_op jit(solution)/shard_map/concatenate | solution.py:249
  13.9 1.6 %collective-permute-start.9 = (bf16[512,256]{1,0:T(8,128)(2,1)S(1)}, bf16[512,256]{1,0:T(8,128)(2,1)S(1)}, u32[]{:S(2)}, u32[]{:S(2)}) collective-permute-start(bf16[512,256]{1,0:T(8,128)(2,1)S(1)} %pad_maximum_fusion.refs_5_), channel_id=1, source_target_pairs={{2,0},{3,1},{0,2},{1,3},{6,4},{7,5},{4,6},{5,7},{10,8},{11,9},{8,1... | collective-permute-start | bytes 786440 | tf_op jit(solution)/shard_map/ppermute | solution.py:233
  15.4 0.0 collective-permute-start.10
  15.4 0.4 collective-permute-done.refs_1_
  15.9 1.5 %collective-permute-done.1.refs_2_ = bf16[264,128]{1,0:T(8,128)(2,1)S(1)} collective-permute-done((bf16[264,128]{1,0:T(8,128)(2,1)}, bf16[264,128]{1,0:T(8,128)(2,1)S(1)}, u32[]{:S(2)}, u32[]{:S(2)}) %collective-permute-start.1) | collective-permute-done | bytes 67616 | tf_op jit(solution)/shard_map/ppermute | solution.py:233
  17.4 0.9 %copy-done = bf16[264,128]{1,0:T(8,128)(2,1)S(1)} copy-done((bf16[264,128]{1,0:T(8,128)(2,1)S(1)}, bf16[264,128]{1,0:T(8,128)(2,1)}, u32[]{:S(2)}) %copy-start) | copy-done | bytes 67608
  18.2 0.8 %copy-done.2 = bf16[128,256]{1,0:T(8,128)(2,1)S(1)} copy-done((bf16[128,256]{1,0:T(8,128)(2,1)S(1)}, bf16[128,256]{1,0:T(8,128)(2,1)}, u32[]{:S(2)}) %copy-start.2) | copy-done | bytes 65560
  19.1 1.0 %group.1 = (bf16[128,256]{1,0:T(8,128)(2,1)S(1)}, bf16[128,256]{1,0:T(8,128)(2,1)S(1)}, bf16[1056,128]{1,0:T(8,128)(2,1)S(1)}) custom-call(s32[1]{0:T(128)} %bitcast.me_ref.refs_0_, bf16[264,128]{1,0:T(8,128)(2,1)S(1)} %copy-done, bf16[264,128]{1,0:T(8,128)(2,1)S(1)} %collective-permute-done.refs_1_, bf16[264,128]{1,0:T(8,128)(2,1)S(1)} %collective-permute-done.1.refs_2_, ...), custom_call_target="tpu_custom_call" | custom-call | flops 17179869184 | bytes 2097152 | tf_op jit(solution)/shard_map/group/pallas_call | solution.py:251
  20.1 0.0 copy-start.3
  20.1 0.5 %collective-permute-done.9.refs_6_ = bf16[512,256]{1,0:T(8,128)(2,1)S(1)} collective-permute-done((bf16[512,256]{1,0:T(8,128)(2,1)S(1)}, bf16[512,256]{1,0:T(8,128)(2,1)S(1)}, u32[]{:S(2)}, u32[]{:S(2)}) %collective-permute-start.9) | collective-permute-done | bytes 262176 | tf_op jit(solution)/shard_map/ppermute | solution.py:233
  20.6 1.5 %collective-permute-start.3 = (bf16[128,256]{1,0:T(8,128)(2,1)S(1)}, bf16[128,256]{1,0:T(8,128)(2,1)S(1)}, u32[]{:S(2)}, u32[]{:S(2)}) collective-permute-start(bf16[128,256]{1,0:T(8,128)(2,1)S(1)} %get-tuple-element.19.refs_1_), channel_id=1, source_target_pairs={{2,0},{3,1},{0,2},{1,3},{6,4},{7,5},{4,6},{5,7},{10,8},{11,9},{8,1... | collective-permute-start | bytes 196616 | tf_op jit(solution)/shard_map/ppermute | solution.py:233
  22.1 0.2 collective-permute-start.4
  22.3 0.4 collective-permute-start.5
  22.7 2.4 %collective-permute-done.3.refs_2_ = bf16[128,256]{1,0:T(8,128)(2,1)S(1)} collective-permute-done((bf16[128,256]{1,0:T(8,128)(2,1)S(1)}, bf16[128,256]{1,0:T(8,128)(2,1)S(1)}, u32[]{:S(2)}, u32[]{:S(2)}) %collective-permute-start.3) | collective-permute-done | bytes 65568 | tf_op jit(solution)/shard_map/ppermute | solution.py:233
  25.1 1.9 %collective-permute-start.13 = (bf16[1056,128]{1,0:T(8,128)(2,1)S(1)}, bf16[1056,128]{1,0:T(8,128)(2,1)S(1)}, u32[]{:S(2)}, u32[]{:S(2)}) collective-permute-start(bf16[1056,128]{1,0:T(8,128)(2,1)S(1)} %get-tuple-element.26.refs_1_), channel_id=1, source_target_pairs={{2,0},{3,1},{0,2},{1,3},{6,4},{7,5},{4,6},{5,7},{10,8},{11,9},{8,1... | collective-permute-start | bytes 811016 | tf_op jit(solution)/shard_map/ppermute | solution.py:233
  27.0 0.4 collective-permute-start.15
  27.4 12.9 %step.1 = (f32[2,64,256]{2,1,0:T(8,128)}, f32[256,512]{1,0:T(8,128)S(1)}, f32[256,512]{1,0:T(8,128)S(1)}, f32[2,256,256]{2,1,0:T(8,128)S(1)}, f32[8,256]{1,0:T(8,128)S(1)}) custom-call(s32[1]{0:T(128)} %bitcast.me_ref.refs_0_, bf16[128,256]{1,0:T(8,128)(2,1)S(1)} %get-tuple-element.19.refs_1_, bf16[128,256]{1,0:T(8,128)(2,1)S(1)} %collective-permute-done.3.refs_2_, ...), custom_call_target="tpu_custom_call" | custom-call | flops 536870912 | bytes 1048576 | tf_op jit(solution)/shard_map/step/pallas_call | solution.py:271
  40.3 0.4 collective-permute-start.12
  40.7 2.5 %first.1.first_ref = f32[136,256]{1,0:T(8,128)S(1)} custom-call(s32[1]{0:T(128)} %bitcast.me_ref.refs_0_, bf16[1056,128]{1,0:T(8,128)(2,1)S(1)} %get-tuple-element.26.refs_1_, bf16[1056,128]{1,0:T(8,128)(2,1)S(1)} %collective-permute-done.13.refs_2_, bf16[1056,128]{1,0:T(8,128)(2,1)S(1)} %collective-permute-done.14.refs_3_, ...), custom_call_target="tpu_custom_call" | custom-call | flops 2147483648 | bytes 4194304 | tf_op jit(solution)/shard_map/first/pallas_call | solution.py:298
  43.3 0.3 collective-permute-start.16
  43.6 1.1 %collective-permute-done.16.got_ref = f32[136,256]{1,0:T(8,128)S(1)} collective-permute-done((f32[136,256]{1,0:T(8,128)S(1)}, f32[136,256]{1,0:T(8,128)S(1)}, u32[]{:S(2)}, u32[]{:S(2)}) %collective-permute-start.16) | collective-permute-done | bytes 139296 | tf_op jit(solution)/shard_map/ppermute | solution.py:229
  44.7 0.9 %combine.1 = (f32[256,512]{1,0:T(8,128)}, f32[128,256]{1,0:T(8,128)}, f32[1,1]{1,0:T(1,128)}) custom-call(f32[256,512]{1,0:T(8,128)S(1)} %get-tuple-element.24.keep_ref, f32[256,512]{1,0:T(8,128)S(1)} %collective-permute-done.12.sent_ref, f32[136,256]{1,0:T(8,128)S(1)} %first.1.first_ref, f32[136,256]{1,0:T(8,128)S(1)} %collective-permute-done.16.got_ref), custom_call_target="tpu_custom_call" | custom-call | tf_op jit(solution)/shard_map/combine/pallas_call | solution.py:308
  (16 shorter events, 0.0 us)
Async XLA Ops:
  0.6 9.6 %collective-permute-start.6 = (bf16[128,256]{1,0:T(8,128)(2,1)}, bf16[128,256]{1,0:T(8,128)(2,1)S(1)}, u32[]{:S(2)}, u32[]{:S(2)}) collective-permute-start(bf16[128,256]{1,0:T(8,128)(2,1)} %bitcast.8), channel_id=1, source_target_pairs={{12,0},{13,1},{14,2},{15,3},{0,4},{1,5},{2,6},{3,7},{4,8},{5,9},{6... | collective-permute-start | bytes 196616 | tf_op jit(solution)/shard_map/ppermute | solution.py:233
  3.7 9.3 %collective-permute-start.7 = (bf16[128,256]{1,0:T(8,128)(2,1)}, bf16[128,256]{1,0:T(8,128)(2,1)S(1)}, u32[]{:S(2)}, u32[]{:S(2)}) collective-permute-start(bf16[128,256]{1,0:T(8,128)(2,1)} %bitcast.9), channel_id=1, source_target_pairs={{8,0},{9,1},{10,2},{11,3},{12,4},{13,5},{14,6},{15,7},{0,8},{1,9},... | collective-permute-start | bytes 196616 | tf_op jit(solution)/shard_map/ppermute | solution.py:233
  6.3 6.7 %collective-permute-start.8 = (bf16[128,256]{1,0:T(8,128)(2,1)}, bf16[128,256]{1,0:T(8,128)(2,1)S(1)}, u32[]{:S(2)}, u32[]{:S(2)}) collective-permute-start(bf16[128,256]{1,0:T(8,128)(2,1)} %bitcast.10), channel_id=1, source_target_pairs={{4,0},{5,1},{6,2},{7,3},{8,4},{9,5},{10,6},{11,7},{12,8},{13,9},{1... | collective-permute-start | bytes 196616 | tf_op jit(solution)/shard_map/ppermute | solution.py:233
  9.2 6.7 %collective-permute-start = (bf16[264,128]{1,0:T(8,128)(2,1)}, bf16[264,128]{1,0:T(8,128)(2,1)S(1)}, u32[]{:S(2)}, u32[]{:S(2)}) collective-permute-start(bf16[264,128]{1,0:T(8,128)(2,1)} %pack.1.refs_0_), channel_id=1, source_target_pairs={{12,0},{13,1},{14,2},{15,3},{0,4},{1,5},{2,6},{3,7},{4,8},{5,9},{6... | collective-permute-start | bytes 202760 | tf_op jit(solution)/shard_map/ppermute | solution.py:233
  9.9 7.5 %collective-permute-start.1 = (bf16[264,128]{1,0:T(8,128)(2,1)}, bf16[264,128]{1,0:T(8,128)(2,1)S(1)}, u32[]{:S(2)}, u32[]{:S(2)}) collective-permute-start(bf16[264,128]{1,0:T(8,128)(2,1)} %pack.1.refs_0_), channel_id=1, source_target_pairs={{8,0},{9,1},{10,2},{11,3},{12,4},{13,5},{14,6},{15,7},{0,8},{1,9},... | collective-permute-start | bytes 202760 | tf_op jit(solution)/shard_map/ppermute | solution.py:233
  10.2 7.2 %collective-permute-start.2 = (bf16[264,128]{1,0:T(8,128)(2,1)}, bf16[264,128]{1,0:T(8,128)(2,1)S(1)}, u32[]{:S(2)}, u32[]{:S(2)}) collective-permute-start(bf16[264,128]{1,0:T(8,128)(2,1)} %pack.1.refs_0_), channel_id=1, source_target_pairs={{4,0},{5,1},{6,2},{7,3},{8,4},{9,5},{10,6},{11,7},{12,8},{13,9},{1... | collective-permute-start | bytes 202760 | tf_op jit(solution)/shard_map/ppermute | solution.py:233
  13.9 6.7 %collective-permute-start.9 = (bf16[512,256]{1,0:T(8,128)(2,1)S(1)}, bf16[512,256]{1,0:T(8,128)(2,1)S(1)}, u32[]{:S(2)}, u32[]{:S(2)}) collective-permute-start(bf16[512,256]{1,0:T(8,128)(2,1)S(1)} %pad_maximum_fusion.refs_5_), channel_id=1, source_target_pairs={{2,0},{3,1},{0,2},{1,3},{6,4},{7,5},{4,6},{5,7},{10,8},{11,9},{8,1... | collective-permute-start | bytes 786440 | tf_op jit(solution)/shard_map/ppermute | solution.py:233
  15.4 12.0 %collective-permute-start.10 = (bf16[512,256]{1,0:T(8,128)(2,1)S(1)}, bf16[512,256]{1,0:T(8,128)(2,1)S(1)}, u32[]{:S(2)}, u32[]{:S(2)}) collective-permute-start(bf16[512,256]{1,0:T(8,128)(2,1)S(1)} %pad_maximum_fusion.refs_5_), channel_id=1, source_target_pairs={{0,1},{1,0},{2,3},{3,2},{4,5},{5,4},{6,7},{7,6},{8,9},{9,8},{10,11... | collective-permute-start | bytes 786440 | tf_op jit(solution)/shard_map/ppermute | solution.py:229
  17.4 0.9 %copy-start = (bf16[264,128]{1,0:T(8,128)(2,1)S(1)}, bf16[264,128]{1,0:T(8,128)(2,1)}, u32[]{:S(2)}) copy-start(bf16[264,128]{1,0:T(8,128)(2,1)} %pack.1.refs_0_) | copy-start | bytes 202756
  18.2 0.8 %copy-start.2 = (bf16[128,256]{1,0:T(8,128)(2,1)S(1)}, bf16[128,256]{1,0:T(8,128)(2,1)}, u32[]{:S(2)}) copy-start(bf16[128,256]{1,0:T(8,128)(2,1)} %refs_5_.1) | copy-start | bytes 196612
  19.1 8.4 %copy-start.1 = (f32[256]{0:T(256)S(1)}, f32[256]{0:T(256)}, u32[]{:S(2)}) copy-start(f32[256]{0:T(256)} %param.12) | copy-start | bytes 3076
  20.1 20.7 %copy-start.3 = (bf16[128,256]{1,0:T(8,128)(2,1)S(1)}, bf16[128,256]{1,0:T(8,128)(2,1)}, u32[]{:S(2)}) copy-start(bf16[128,256]{1,0:T(8,128)(2,1)} %refs_5_.1) | copy-start | bytes 196612
  20.6 6.8 %collective-permute-start.11 = (bf16[512,256]{1,0:T(8,128)(2,1)S(1)}, bf16[512,256]{1,0:T(8,128)(2,1)S(1)}, u32[]{:S(2)}, u32[]{:S(2)}) collective-permute-start(bf16[512,256]{1,0:T(8,128)(2,1)S(1)} %collective-permute-done.9.refs_6_), channel_id=1, source_target_pairs={{0,1},{1,0},{2,3},{3,2},{4,5},{5,4},{6,7},{7,6},{8,9},{9,8},{10,11... | collective-permute-start | bytes 786440 | tf_op jit(solution)/shard_map/ppermute | solution.py:229
  20.6 4.5 %collective-permute-start.3 = (bf16[128,256]{1,0:T(8,128)(2,1)S(1)}, bf16[128,256]{1,0:T(8,128)(2,1)S(1)}, u32[]{:S(2)}, u32[]{:S(2)}) collective-permute-start(bf16[128,256]{1,0:T(8,128)(2,1)S(1)} %get-tuple-element.19.refs_1_), channel_id=1, source_target_pairs={{2,0},{3,1},{0,2},{1,3},{6,4},{7,5},{4,6},{5,7},{10,8},{11,9},{8,1... | collective-permute-start | bytes 196616 | tf_op jit(solution)/shard_map/ppermute | solution.py:233
  22.1 4.9 %collective-permute-start.4 = (bf16[128,256]{1,0:T(8,128)(2,1)S(1)}, bf16[128,256]{1,0:T(8,128)(2,1)S(1)}, u32[]{:S(2)}, u32[]{:S(2)}) collective-permute-start(bf16[128,256]{1,0:T(8,128)(2,1)S(1)} %get-tuple-element.20), channel_id=1, source_target_pairs={{0,1},{1,0},{2,3},{3,2},{4,5},{5,4},{6,7},{7,6},{8,9},{9,8},{10,11... | collective-permute-start | bytes 196616 | tf_op jit(solution)/shard_map/ppermute | solution.py:229
  22.3 4.7 %collective-permute-start.5 = (bf16[128,256]{1,0:T(8,128)(2,1)S(1)}, bf16[128,256]{1,0:T(8,128)(2,1)S(1)}, u32[]{:S(2)}, u32[]{:S(2)}) collective-permute-start(bf16[128,256]{1,0:T(8,128)(2,1)S(1)} %get-tuple-element.20), channel_id=1, source_target_pairs={{3,0},{2,1},{1,2},{0,3},{7,4},{6,5},{5,6},{4,7},{11,8},{10,9},{9,1... | collective-permute-start | bytes 196616 | tf_op jit(solution)/shard_map/ppermute | solution.py:243
  25.1 15.6 %collective-permute-start.13 = (bf16[1056,128]{1,0:T(8,128)(2,1)S(1)}, bf16[1056,128]{1,0:T(8,128)(2,1)S(1)}, u32[]{:S(2)}, u32[]{:S(2)}) collective-permute-start(bf16[1056,128]{1,0:T(8,128)(2,1)S(1)} %get-tuple-element.26.refs_1_), channel_id=1, source_target_pairs={{2,0},{3,1},{0,2},{1,3},{6,4},{7,5},{4,6},{5,7},{10,8},{11,9},{8,1... | collective-permute-start | bytes 811016 | tf_op jit(solution)/shard_map/ppermute | solution.py:233
  27.0 13.7 %collective-permute-start.14 = (bf16[1056,128]{1,0:T(8,128)(2,1)S(1)}, bf16[1056,128]{1,0:T(8,128)(2,1)S(1)}, u32[]{:S(2)}, u32[]{:S(2)}) collective-permute-start(bf16[1056,128]{1,0:T(8,128)(2,1)S(1)} %get-tuple-element.26.refs_1_), channel_id=1, source_target_pairs={{0,1},{1,0},{2,3},{3,2},{4,5},{5,4},{6,7},{7,6},{8,9},{9,8},{10,11... | collective-permute-start | bytes 811016 | tf_op jit(solution)/shard_map/ppermute | solution.py:229
  27.0 13.7 %collective-permute-start.15 = (bf16[1056,128]{1,0:T(8,128)(2,1)S(1)}, bf16[1056,128]{1,0:T(8,128)(2,1)S(1)}, u32[]{:S(2)}, u32[]{:S(2)}) collective-permute-start(bf16[1056,128]{1,0:T(8,128)(2,1)S(1)} %get-tuple-element.26.refs_1_), channel_id=1, source_target_pairs={{3,0},{2,1},{1,2},{0,3},{7,4},{6,5},{5,6},{4,7},{11,8},{10,9},{9,1... | collective-permute-start | bytes 811016 | tf_op jit(solution)/shard_map/ppermute | solution.py:243
  40.3 4.4 %collective-permute-start.12 = (f32[256,512]{1,0:T(8,128)S(1)}, f32[256,512]{1,0:T(8,128)S(1)}, u32[]{:S(2)}, u32[]{:S(2)}) collective-permute-start(f32[256,512]{1,0:T(8,128)S(1)} %get-tuple-element.25), channel_id=1, source_target_pairs={{0,1},{1,0},{2,3},{3,2},{4,5},{5,4},{6,7},{7,6},{8,9},{9,8},{10,11... | collective-permute-start | bytes 1572872 | tf_op jit(solution)/shard_map/ppermute | solution.py:229
  43.3 1.4 %collective-permute-start.16 = (f32[136,256]{1,0:T(8,128)S(1)}, f32[136,256]{1,0:T(8,128)S(1)}, u32[]{:S(2)}, u32[]{:S(2)}) collective-permute-start(f32[136,256]{1,0:T(8,128)S(1)} %first.1.first_ref), channel_id=1, source_target_pairs={{0,1},{1,0},{2,3},{3,2},{4,5},{5,4},{6,7},{7,6},{8,9},{9,8},{10,11... | collective-permute-start | bytes 417800 | tf_op jit(solution)/shard_map/ppermute | solution.py:229
